TPU v7x, 32 devices: a whole 2x2x4 slice. The times are simulated.
32 devices in a mesh: groups: 2 (over y), freq: 16 (over z, x, core).
Axes of the slice: x: 2, y: 2, z: 4, core: 2. Of those that a mesh axis runs over, the one named last changes fastest.
Arguments:
- refl: bfloat16 [128, 2, 512, 512], P(('groups', 'freq')), parts along dimension 0, may hold values from -0.1875 to 0.1875
- refl_scale: float32 [128, 4], P(('groups', 'freq')), parts along dimension 0, may hold values from 0.5 to 4
- freq_index: int32 [128], P(('groups', 'freq')), parts along dimension 0, may hold values from 1 to 1023, as said below
- fd_plus: bfloat16 [4096, 32, 512], P(('groups', 'freq')), parts along dimension 0, may hold values from -6 to 6
- onset: int32 [32768], P(('groups', 'freq')), parts along dimension 0, may hold values from 128 to 767
Outputs:
- f_minus: bfloat16 [4096, 32, 512], P(('groups', 'freq')), parts along dimension 0
- f_plus: float32 [4096, 32, 512], P(('groups', 'freq')), parts along dimension 0
There are 2 independent parts, one for each index of `groups`. A program takes and returns all parts, laid end to end along the dimension named above; each array names one. Nothing has to cross between parts.
Inputs may be any that keep to these rules, and one draw needn't show every extreme that they name: `freq_index`: the bins are distinct and ascending; the first is 1 and the last is 1023.
All inputs are finite; a program needn't handle non-finite values.
Results may differ from a plain program's by a relative error of at most 0.01.
Values may be sent and summed in bfloat16 or wider, within the bound.
No kernel may reach another device: no remote copies, remote signals or barrier semaphores. Data moves between devices by JAX's collectives and lax.ppermute only.
A program may use at most 128 MiB of HBM per device.

v0:
```python
import math

import jax
import jax.numpy as jnp
from jax import lax
from jax.sharding import PartitionSpec as P


def to_columns(field):
    return lax.all_to_all(field, "freq", split_axis=1, concat_axis=0, tiled=True)


def to_time(field):
    return lax.all_to_all(field, "freq", split_axis=0, concat_axis=1, tiled=True)


def local(refl, refl_scale, freq_index, fd_plus, onset):
    nfreq_dev = refl.shape[0]
    nrec = refl.shape[2]
    t_dev, points, _ = fd_plus.shape
    columns = points * nrec
    nshard = lax.axis_size("freq")
    ntime = t_dev * nshard
    width = columns // nshard
    first_col = lax.axis_index("freq") * width
    bins, scales = (
        lax.all_gather(freq_index, "freq", axis=0, tiled=True),
        lax.all_gather(refl_scale, "freq", axis=0, tiled=True),
    )
    nblocks = scales.shape[1]
    times = jnp.arange(ntime, dtype=jnp.int32)
    phase = bins[:, None] * times[None, :] % ntime
    angle = phase.astype(jnp.float32) * jnp.float32(2.0 * math.pi / ntime)
    cosine = jnp.cos(angle).astype(jnp.bfloat16)
    sine = jnp.sin(angle).astype(jnp.bfloat16)
    col_ids = first_col + jnp.arange(width, dtype=jnp.int32)
    block_ids = col_ids % nrec // (nrec // nblocks)
    onehot = (block_ids[None, :] == jnp.arange(nblocks, dtype=jnp.int32)[:, None]).astype(
        jnp.float32
    )
    col_scale = jnp.dot(
        scales, onehot, precision=lax.Precision.HIGHEST, preferred_element_type=jnp.float32
    )
    signed = jnp.where(times < ntime // 2, times, times - ntime)
    keep = (jnp.abs(signed)[:, None] < onset[None, :]).astype(jnp.float32)
    contract_time = (((0,), (0,)), ((), ()))

    def forward(colfield, table_c, table_s):
        real = jnp.dot(table_c, colfield, preferred_element_type=jnp.float32)
        imag = -jnp.dot(table_s, colfield, preferred_element_type=jnp.float32)
        spectrum = jnp.stack(
            [(real * col_scale).astype(jnp.bfloat16), (imag * col_scale).astype(jnp.bfloat16)],
            axis=1,
        )
        return lax.all_to_all(spectrum, "freq", split_axis=0, concat_axis=2, tiled=True)

    def convolve(spectrum, sign):
        spectrum = spectrum.reshape(nfreq_dev, 2, points, nrec)
        spec_r = spectrum[:, 0]
        spec_i = spectrum[:, 1]
        resp_r = refl[:, 0]
        resp_i = refl[:, 1]

        def apply(resp, spec):
            return jnp.einsum("frs,fvs->fvr", resp, spec, preferred_element_type=jnp.float32)

        out_r = apply(resp_r, spec_r) - sign * apply(resp_i, spec_i)
        out_i = apply(resp_r, spec_i) + sign * apply(resp_i, spec_r)
        stacked = jnp.stack([out_r.astype(jnp.bfloat16), out_i.astype(jnp.bfloat16)], axis=1)
        return lax.all_to_all(
            stacked.reshape(nfreq_dev, 2, columns), "freq", split_axis=2, concat_axis=0, tiled=True
        )

    def inverse(spectrum):
        trace = lax.dot_general(
            cosine, spectrum[:, 0], contract_time, preferred_element_type=jnp.float32
        )
        trace = trace - lax.dot_general(
            sine, spectrum[:, 1], contract_time, preferred_element_type=jnp.float32
        )
        return (trace * jnp.float32(2.0 / ntime) * keep).astype(jnp.bfloat16)

    direct = fd_plus.reshape(t_dev, columns)
    minus_cols = inverse(convolve(forward(to_columns(direct), cosine, sine), 1.0))
    minus_time = to_time(minus_cols)
    update_cols = inverse(convolve(forward(minus_cols, cosine, sine), -1.0))
    plus_time = direct.astype(jnp.float32) + to_time(update_cols).astype(jnp.float32)
    return (minus_time.reshape(t_dev, points, nrec), plus_time.reshape(t_dev, points, nrec))


def solution(mesh):
    return jax.shard_map(
        local,
        mesh=mesh,
        in_specs=(
            P(("groups", "freq"), None, None, None),
            P(("groups", "freq"), None),
            P(("groups", "freq")),
            P(("groups", "freq"), None, None),
            P(("groups", "freq")),
        ),
        out_specs=(P(("groups", "freq"), None, None), P(("groups", "freq"), None, None)),
        check_vma=False,
    )
```

profile of v0, /device:TPU:11, one launch (start us, length us, event | category | flops | bytes accessed | tf_op | source)
XLA Modules:
  0.0 541.1 jit_solution(8030469073627968279)
XLA Ops:
  0.6 7.9 %copy.51 = bf16[128,32,512]{0,2,1:T(8,128)(2,1)} copy(bf16[128,32,512]{2,1,0:T(8,128)(2,1)} %param.8) | data formatting | bytes 8388608 | tf_op args[3]
  8.5 6.7 %all-to-all-start = ((bf16[128,16,1024]{0,2,1:T(8,128)(2,1)}), bf16[128,16,1024]{0,2,1:T(8,128)(2,1)}, u32[]{:S(2)}, u32[]{:S(2)}) async-start(bf16[128,16,1024]{0,2,1:T(8,128)(2,1)} %bitcast.126), calls=%async_computation | async-start | bytes 8388608 | tf_op jit(solution)/shard_map/all_to_all | solution.py:10
  15.2 0.6 dynamic-slice
  16.7 88.9 %all-reduce = s32[64]{0:T(128)S(1)} all-reduce(s32[64]{0:T(128)S(1)} %dynamic-update-slice), channel_id=1, replica_groups=mesh['groups'=2,'freq'=16] {'freq'}, use_global_device_ids=true, to_apply=%add | all-reduce | flops 64 | bytes 512
  105.6 18.6 %all-gather = f32[16,4,4]{2,1,0:T(4,128)S(1)} all-gather(f32[1,4,4]{2,1,0:T(4,128)S(1)} %bitcast.140), channel_id=1, replica_groups=mesh['groups'=2,'freq'=16] {'freq'}, dimensions={0}, use_global_device_ids=true | all-gather | bytes 1088 | tf_op jit(solution)/shard_map/all_gather | solution.py:28
  124.5 6.4 %copy.52 = bf16[16,128,1024]{2,1,0:T(8,128)(2,1)} copy(bf16[16,128,1024]{1,2,0:T(8,128)(2,1)} %bitcast.2) | data formatting | bytes 8388608 | tf_op jit(solution)/shard_map/all_to_all | solution.py:10
  130.9 4.5 fusion.64
  135.4 2.5 fusion.65
  138.0 0.3 copy.53
  138.2 15.2 %all_to_all.114 = bf16[64,2,1024]{2,1,0:T(2,128)(2,1)S(1)} all-to-all(bf16[64,2,1024]{2,1,0:T(2,128)(2,1)S(1)} %copy.53), channel_id=1, replica_groups=mesh['groups'=2,'freq'=16] {'freq'}, dimensions={0} | all-to-all | bytes 524288 | tf_op jit(solution)/shard_map/all_to_all | solution.py:55
  153.7 2.4 fusion.6
  156.1 2.3 fusion.8
  158.5 0.7 fusion.56
  159.3 2.3 fusion.59
  161.9 13.0 %copy.57 = bf16[4,2,16384]{0,1,2:T(2,128)(2,1)} copy(bf16[4,2,16384]{2,0,1:T(4,128)(2,1)S(1)} %pad_maximum_fusion.1) | data formatting | bytes 524288 | tf_op jit(solution)/shard_map/stack | solution.py:69
  174.8 16.8 %reshape.93 = bf16[16,2,4096]{2,1,0:T(2,128)(2,1)} reshape(bf16[16384,2,4]{2,1,0:T(2,128)(2,1)} %bitcast.122) | data formatting | bytes 524288
  191.7 5.8 %all-to-all-start.2 = ((bf16[16,2,4096]{2,1,0:T(2,128)(2,1)}), bf16[16,2,4096]{2,1,0:T(2,128)(2,1)S(1)}, u32[]{:S(2)}, u32[]{:S(2)}) async-start(bf16[16,2,4096]{2,1,0:T(2,128)(2,1)} %reshape.93), calls=%async_computation.2 | async-start | bytes 524288 | tf_op jit(solution)/shard_map/all_to_all | solution.py:70
  197.5 7.9 %all-to-all-done.2 = bf16[16,2,4096]{2,1,0:T(2,128)(2,1)S(1)} async-done(((bf16[16,2,4096]{2,1,0:T(2,128)(2,1)}), bf16[16,2,4096]{2,1,0:T(2,128)(2,1)S(1)}, u32[]{:S(2)}, u32[]{:S(2)}) %all-to-all-start.2) | async-done | bytes 262176 | tf_op jit(solution)/shard_map/all_to_all | solution.py:70
  205.4 19.0 %reshape.94 = bf16[16384,2,4]{2,1,0:T(2,128)(2,1)} reshape(bf16[16,2,4096]{2,1,0:T(2,128)(2,1)S(1)} %all-to-all-done.2) | data formatting | bytes 524288
  224.4 11.9 %copy.67 = bf16[4,2,16,1024]{3,2,1,0:T(8,128)(2,1)S(1)} copy(bf16[4,2,16,1024]{0,1,3,2:T(2,128)(2,1)} %bitcast.123) | data formatting | bytes 524288 | tf_op jit(solution)/shard_map/all_to_all | solution.py:70
  236.6 0.4 fusion.123
  237.0 3.1 fusion.73
  240.1 4.1 fusion
  244.2 2.5 fusion.62
  246.8 2.5 fusion.63
  249.6 13.1 %all_to_all.115 = bf16[64,2,1024]{2,1,0:T(2,128)(2,1)S(1)} all-to-all(bf16[64,2,1024]{2,1,0:T(2,128)(2,1)S(1)} %copy.61), channel_id=1, replica_groups=mesh['groups'=2,'freq'=16] {'freq'}, dimensions={0} | all-to-all | bytes 524288 | tf_op jit(solution)/shard_map/all_to_all | solution.py:55
  263.0 2.5 fusion.41
  265.4 2.3 fusion.38
  267.7 0.7 fusion.50
  268.6 2.3 fusion.53
  271.2 13.0 %copy.63 = bf16[4,2,16384]{0,1,2:T(2,128)(2,1)} copy(bf16[4,2,16384]{2,0,1:T(4,128)(2,1)S(1)} %pad_maximum_fusion.3) | data formatting | bytes 524288 | tf_op jit(solution)/shard_map/stack | solution.py:69
  284.1 16.2 %reshape.95 = bf16[16,2,4096]{2,1,0:T(2,128)(2,1)S(1)} reshape(bf16[16384,2,4]{2,1,0:T(2,128)(2,1)} %bitcast.124) | data formatting | bytes 524288
  300.3 12.8 %all_to_all.116 = bf16[16,2,4096]{2,1,0:T(2,128)(2,1)S(1)} all-to-all(bf16[16,2,4096]{2,1,0:T(2,128)(2,1)S(1)} %reshape.95), channel_id=1, replica_groups=mesh['groups'=2,'freq'=16] {'freq'}, dimensions={0} | all-to-all | bytes 524288 | tf_op jit(solution)/shard_map/all_to_all | solution.py:70
  313.1 6.5 %all-to-all-start.3 = ((bf16[16,128,1024]{2,1,0:T(8,128)(2,1)}), bf16[16,128,1024]{2,1,0:T(8,128)(2,1)}, u32[]{:S(2)}, u32[]{:S(2)}) async-start(bf16[16,128,1024]{2,1,0:T(8,128)(2,1)} %bitcast.127), calls=%async_computation.3 | async-start | bytes 8388608 | tf_op jit(solution)/shard_map/all_to_all | solution.py:14
  319.6 19.1 %reshape.96 = bf16[16384,2,4]{2,1,0:T(2,128)(2,1)} reshape(bf16[16,2,4096]{2,1,0:T(2,128)(2,1)S(1)} %all_to_all.116) | data formatting | bytes 524288
  338.7 11.9 %copy.68 = bf16[4,2,16,1024]{3,2,1,0:T(8,128)(2,1)S(1)} copy(bf16[4,2,16,1024]{0,1,3,2:T(2,128)(2,1)} %bitcast.125) | data formatting | bytes 524288 | tf_op jit(solution)/shard_map/all_to_all | solution.py:70
  350.9 0.4 fusion.122
  351.2 3.1 fusion.72
  354.4 4.9 fusion.1
  359.3 52.8 %all-to-all-done.3 = bf16[16,128,1024]{2,1,0:T(8,128)(2,1)} async-done(((bf16[16,128,1024]{2,1,0:T(8,128)(2,1)}), bf16[16,128,1024]{2,1,0:T(8,128)(2,1)}, u32[]{:S(2)}, u32[]{:S(2)}) %all-to-all-start.3) | async-done | bytes 4194336 | tf_op jit(solution)/shard_map/all_to_all | solution.py:14
  412.1 5.3 all-to-all-start.6
  417.4 6.5 %copy.60 = bf16[128,16,1024]{2,1,0:T(8,128)(2,1)} copy(bf16[128,16,1024]{2,0,1:T(8,128)(2,1)} %bitcast.19) | data formatting | bytes 8388608 | tf_op jit(solution)/shard_map/all_to_all | solution.py:14
  423.9 7.1 %reshape.83 = bf16[128,32,512]{2,1,0:T(8,128)(2,1)} reshape(bf16[128,16,1024]{2,1,0:T(8,128)(2,1)} %copy.60) | data formatting | bytes 8388608 | tf_op jit(solution)/shard_map/reshape | solution.py:88
  431.0 78.7 %all-to-all-done.6 = bf16[16,128,1024]{2,1,0:T(8,128)(2,1)} async-done(((bf16[16,128,1024]{2,1,0:T(8,128)(2,1)}), bf16[16,128,1024]{2,1,0:T(8,128)(2,1)}, u32[]{:S(2)}, u32[]{:S(2)}) %all-to-all-start.6) | async-done | bytes 4194336 | tf_op jit(solution)/shard_map/all_to_all | solution.py:14
  509.7 3.2 convert_bitcast_fusion
  512.9 8.3 %copy.66 = f32[128,16,1024]{2,1,0:T(8,128)} copy(f32[128,16,1024]{2,0,1:T(8,128)S(1)} %convert_bitcast_fusion) | data formatting | bytes 16777216 | tf_op jit(solution)/shard_map/convert_element_type | solution.py:87
  521.2 9.3 %reshape.85 = f32[128,32,512]{2,1,0:T(8,128)} reshape(f32[128,16,1024]{2,1,0:T(8,128)} %copy.66) | data formatting | bytes 16777216 | tf_op jit(solution)/shard_map/convert_element_type | solution.py:87
  530.5 10.2 %convert_add_fusion = f32[128,32,512]{2,1,0:T(8,128)} fusion(f32[128,32,512]{2,1,0:T(8,128)} %reshape.85, bf16[128,32,512]{2,1,0:T(8,128)(2,1)} %param.8), kind=kLoop, calls=%fused_computation.5 | loop fusion | flops 4194304 | bytes 20971520 | tf_op jit(solution)/shard_map/add | solution.py:87
  (37 shorter events, 2.6 us)
Async XLA Ops:
  8.5 6.7 %copy-start.7 = (u32[32]{0:T(128)S(1)}, u32[32]{0:T(128)}, u32[]{:S(2)}) copy-start(u32[32]{0:T(128)} %constant.68) | copy-start | bytes 388
  8.5 8.0 %copy-start.6 = (s32[4]{0:T(128)S(1)}, s32[4]{0:T(128)}, u32[]{:S(2)}) copy-start(s32[4]{0:T(128)} %param.7) | copy-start | bytes 52
  8.5 97.1 %copy-start.4 = (f32[4,4]{1,0:T(4,128)S(1)}, f32[4,4]{1,0:T(4,128)}, u32[]{:S(2)}) copy-start(f32[4,4]{1,0:T(4,128)} %param.6) | copy-start | bytes 196
  8.5 115.9 %all-to-all-start = ((bf16[128,16,1024]{0,2,1:T(8,128)(2,1)}), bf16[128,16,1024]{0,2,1:T(8,128)(2,1)}, u32[]{:S(2)}, u32[]{:S(2)}) async-start(bf16[128,16,1024]{0,2,1:T(8,128)(2,1)} %bitcast.126), calls=%async_computation | async-start | bytes 8388608 | tf_op jit(solution)/shard_map/all_to_all | solution.py:10
  130.9 4.5 copy-start.3
  153.7 4.8 copy-start
  191.7 13.7 %all-to-all-start.2 = ((bf16[16,2,4096]{2,1,0:T(2,128)(2,1)}), bf16[16,2,4096]{2,1,0:T(2,128)(2,1)S(1)}, u32[]{:S(2)}, u32[]{:S(2)}) async-start(bf16[16,2,4096]{2,1,0:T(2,128)(2,1)} %reshape.93), calls=%async_computation.2 | async-start | bytes 524288 | tf_op jit(solution)/shard_map/all_to_all | solution.py:70
  237.0 3.1 copy-start.5
  244.2 5.1 copy-start.2
  262.9 4.8 copy-start.1
  313.1 99.0 %all-to-all-start.3 = ((bf16[16,128,1024]{2,1,0:T(8,128)(2,1)}), bf16[16,128,1024]{2,1,0:T(8,128)(2,1)}, u32[]{:S(2)}, u32[]{:S(2)}) async-start(bf16[16,128,1024]{2,1,0:T(8,128)(2,1)} %bitcast.127), calls=%async_computation.3 | async-start | bytes 8388608 | tf_op jit(solution)/shard_map/all_to_all | solution.py:14
  412.1 97.6 %all-to-all-start.6 = ((bf16[16,128,1024]{2,1,0:T(8,128)(2,1)}), bf16[16,128,1024]{2,1,0:T(8,128)(2,1)}, u32[]{:S(2)}, u32[]{:S(2)}) async-start(bf16[16,128,1024]{2,1,0:T(8,128)(2,1)} %bitcast.128), calls=%async_computation.6 | async-start | bytes 8388608 | tf_op jit(solution)/shard_map/all_to_all | solution.py:14
where the time goes:
time: 550 us; the launch traced here: 541 us
  local copies, waits for them, and re-layouts  170 us (31%)
  blocking collectives  149 us (27%)
  waiting for transfers between devices  139 us (25%)
  matrix products  43.1 us (8%)
  starting transfers between devices  24.3 us (4%)
  other arithmetic  13.8 us (3%)
    all_to_all x2, waiting for transfers between devices, to_time(): lax.all_to_all(field, 'freq', split_axis=0, concat_axis=1, tiled=True)  132 us
    unnamed x1, blocking collectives  88.9 us
    unnamed x24, local copies, waits for them, and re-layouts  79.9 us
    all_to_all x2, blocking collectives, forward(): lax.all_to_all(spectrum, 'freq', split_axis=0, concat_axis=2, tiled=True)  28.3 us
    another operation x6, local copies, waits for them, and re-layouts, convolve(): jnp.stack([out_r.astype(jnp.bfloat16), out_i.astype(jnp.bfloat16)], axis=1)  26.2 us
    all_to_all x4, local copies, waits for them, and re-layouts, convolve(): lax.all_to_all(stacked.reshape(nfreq_dev, 2, columns), 'freq', split_axis...  24.3 us
    all_gather x1, blocking collectives, local(): lax.all_gather(refl_scale, 'freq', axis=0, tiled=True)  18.6 us
    convert_element_type x2, local copies, waits for them, and re-layouts, local(): to_time(update_cols).astype(jnp.float32)  17.6 us
  transfers between devices with their start and end apart: 4, of which 3 were waited for; matrix products, arithmetic and copies ran while one was open for 10% of the time, Pallas kernels for 0%

commit v1 on v0

v1 whole, which is shorter than its diff:
```python
import functools
import math

import jax
import jax.numpy as jnp
from jax import lax
from jax.experimental import pallas as pl
from jax.experimental.pallas import tpu as pltpu
from jax.sharding import PartitionSpec as P

ONSET_TOP = 767
VMEM_LIMIT = 56 << 20


def params():
    return pltpu.CompilerParams(vmem_limit_bytes=VMEM_LIMIT)


def swap(x, stride):
    n = lax.axis_size("freq")
    return lax.ppermute(x, "freq", [(i, i ^ stride) for i in range(n)])


def cos_table(bins, rows_quarter, times, ntime):
    phase = (bins * times + rows_quarter) % ntime
    angle = phase.astype(jnp.float32) * jnp.float32(2.0 * math.pi / ntime)
    return jnp.cos(angle)


def points_major(x):
    t, v, s = x.shape
    sb = 128

    def kernel(x_ref, o_ref, scr):
        scr[...] = x_ref[...].astype(jnp.float32).reshape(t * v, sb)
        for i in range(v):
            o_ref[i] = scr[pl.ds(i, t, stride=v), :].astype(jnp.bfloat16)

    return pl.pallas_call(
        kernel,
        grid=(s // sb,),
        in_specs=[pl.BlockSpec((t, v, sb), lambda i: (0, 0, i))],
        out_specs=pl.BlockSpec((v, t, sb), lambda i: (0, 0, i)),
        out_shape=jax.ShapeDtypeStruct((v, t, s), x.dtype),
        scratch_shapes=[pltpu.VMEM((t * v, sb), jnp.float32)],
        compiler_params=params(),
        name="points_major",
    )(x)


def partial_spectra(table, own, other, rb, nq):
    rows, _ = table.shape
    v, t, s = own.shape
    ndest = rows // rb
    c = s // nq
    vb = 4 if v % 4 == 0 else 1

    def kernel(tab_ref, own_ref, other_ref, *outs):
        for i in range(vb):
            x = jnp.concatenate([own_ref[i], other_ref[i]], axis=0)
            res = jnp.dot(tab_ref[...], x, preferred_element_type=jnp.float32)
            for j in range(ndest):
                part = res[j * rb : (j + 1) * rb].astype(jnp.bfloat16)
                for q in range(nq):
                    outs[j][i, q] = part[:, q * c : (q + 1) * c]

    return pl.pallas_call(
        kernel,
        grid=(v // vb,),
        in_specs=[
            pl.BlockSpec((rows, 2 * t), lambda i: (0, 0)),
            pl.BlockSpec((vb, t, s), lambda i: (i, 0, 0)),
            pl.BlockSpec((vb, t, s), lambda i: (i, 0, 0)),
        ],
        out_specs=[pl.BlockSpec((vb, nq, rb, c), lambda i: (i, 0, 0, 0))] * ndest,
        out_shape=[jax.ShapeDtypeStruct((v, nq, rb, c), jnp.bfloat16)] * ndest,
        compiler_params=params(),
        name="partial_spectra",
    )(table, own, other)


def convolve(parts, scale, refl, sign):
    v, nq, rb, c = parts[0].shape
    nf, _, r, s = refl.shape
    nparts = len(parts)

    def kernel(*refs):
        part_refs = refs[:nparts]
        scale_ref = None if scale is None else refs[nparts]
        refl_ref, out_ref, x_scr, y_scr = refs[-4:]
        k = pl.program_id(0)

        @pl.when(k == 0)
        def _():
            for i in range(v):
                for q in range(nq):
                    x = part_refs[0][i, q].astype(jnp.float32)
                    for ref in part_refs[1:]:
                        x = x + ref[i, q].astype(jnp.float32)
                    if scale_ref is not None:
                        x = x * scale_ref[:, q * c : (q + 1) * c]
                    for b in range(c // 128):
                        x_scr[q * (c // 128) + b, pl.ds(i, rb, stride=v), :] = x[
                            :, b * 128 : (b + 1) * 128
                        ]

        rows = pl.ds(pl.multiple_of(k * 2 * v, 2 * v), 2 * v)
        x = jnp.concatenate(
            [x_scr[b, rows, :].astype(jnp.bfloat16) for b in range(s // 128)], axis=1
        )
        dims = (((1,), (1,)), ((), ()))
        a = lax.dot_general(x, refl_ref[0, 0], dims, preferred_element_type=jnp.float32)
        b = lax.dot_general(x, refl_ref[0, 1], dims, preferred_element_type=jnp.float32)
        y = jnp.concatenate([a[:v] - sign * b[v:], a[v:] + sign * b[:v]], axis=0)
        for b in range(r // 128):
            y_scr[b, rows, :] = y[:, b * 128 : (b + 1) * 128]

        @pl.when(k == nf - 1)
        def _():
            for i in range(v):
                for q in range(nq):
                    for b in range(c // 128):
                        y = y_scr[q * (c // 128) + b, pl.ds(i, rb, stride=v), :]
                        out_ref[i, q, :, b * 128 : (b + 1) * 128] = y.astype(jnp.bfloat16)

    whole = pl.BlockSpec((v, nq, rb, c), lambda k: (0, 0, 0, 0))
    args = list(parts)
    specs = [whole] * nparts
    if scale is not None:
        args.append(scale)
        specs.append(pl.BlockSpec((rb, s), lambda k: (0, 0)))
    args.append(refl)
    specs.append(pl.BlockSpec((1, 2, r, s), lambda k: (k, 0, 0, 0)))
    return pl.pallas_call(
        kernel,
        grid=(nf,),
        in_specs=specs,
        out_specs=whole,
        out_shape=jax.ShapeDtypeStruct((v, nq, rb, c), jnp.bfloat16),
        scratch_shapes=[
            pltpu.VMEM((s // 128, rb * v, 128), jnp.float32),
            pltpu.VMEM((r // 128, rb * v, 128), jnp.float32),
        ],
        compiler_params=params(),
        name="convolve",
    )(*args)


def window_columns(y, inv_table, fwd_table, absq, onset, scale):
    n, h, rb, c = y.shape
    rows = n * rb
    th = inv_table.shape[0]
    tb = 256

    def kernel(y_ref, inv_ref, fwd_ref, q_ref, onset_ref, scale_ref, out_ref):
        for i in range(h):
            spec = jnp.concatenate([y_ref[j, i] for j in range(n)], axis=0)
            acc = jnp.zeros((rows, c), jnp.float32)
            for k in range(th // tb):
                at = slice(k * tb, (k + 1) * tb)
                trace = jnp.dot(inv_ref[at, :], spec, preferred_element_type=jnp.float32)
                kept = q_ref[at, :] < onset_ref[i]
                trace = jnp.where(kept, trace, 0.0).astype(jnp.bfloat16)
                acc += jnp.dot(fwd_ref[:, at], trace, preferred_element_type=jnp.float32)
            acc = (acc * scale_ref[:, i * c : (i + 1) * c]).astype(jnp.bfloat16)
            for j in range(n):
                out_ref[j, i] = acc[j * rb : (j + 1) * rb]

    return pl.pallas_call(
        kernel,
        out_shape=jax.ShapeDtypeStruct((n, h, rb, c), jnp.bfloat16),
        compiler_params=params(),
        name="window_columns",
    )(y, inv_table, fwd_table, absq, onset, scale)


def time_block(pieces, table, absq, onset, direct, t):
    v, nq, rb, c = pieces[0].shape
    npieces = len(pieces)
    s = nq * c
    sb = 128
    vb = 2 if v % 2 == 0 else 1
    tb = 8

    def kernel(*refs):
        piece_refs = refs[:npieces]
        tab_ref, q_ref, onset_ref = refs[npieces : npieces + 3]
        direct_ref = None if direct is None else refs[npieces + 3]
        out_ref, scr = refs[-2:]
        for i in range(0, v, vb):
            spec = jnp.concatenate(
                [
                    jnp.concatenate([ref[i + j, 0] for ref in piece_refs], axis=0)
                    for j in range(vb)
                ],
                axis=1,
            )
            res = jnp.dot(tab_ref[...], spec, preferred_element_type=jnp.float32)
            for j in range(vb):
                kept = q_ref[...] < onset_ref[i + j : i + j + 1, :]
                y = jnp.where(kept, res[:, j * sb : (j + 1) * sb], 0.0)
                scr[pl.ds(i + j, t, stride=v), :] = y

        @pl.loop(0, t // tb)
        def _(k):
            y = scr[pl.ds(pl.multiple_of(k * tb * v, tb * v), tb * v), :]
            y = y.astype(jnp.bfloat16).reshape(tb, v, sb)
            at = pl.ds(k * tb, tb)
            if direct_ref is None:
                out_ref[at] = y
            else:
                out_ref[at] = direct_ref[at].astype(jnp.float32) + y.astype(jnp.float32)

    per = c // sb
    piece_spec = pl.BlockSpec((v, 1, rb, sb), lambda i: (0, i // per, 0, i % per))
    field_spec = pl.BlockSpec((t, v, sb), lambda i: (0, 0, i))
    args = list(pieces) + [table, absq, onset]
    specs = [piece_spec] * npieces + [
        pl.BlockSpec(table.shape, lambda i: (0, 0)),
        pl.BlockSpec(absq.shape, lambda i: (0, 0)),
        pl.BlockSpec((v, sb), lambda i: (0, i)),
    ]
    if direct is not None:
        args.append(direct)
        specs.append(field_spec)
    dtype = jnp.bfloat16 if direct is None else jnp.float32
    return pl.pallas_call(
        kernel,
        grid=(s // sb,),
        in_specs=specs,
        out_specs=field_spec,
        out_shape=jax.ShapeDtypeStruct((t, v, s), dtype),
        scratch_shapes=[pltpu.VMEM((t * v, sb), jnp.float32)],
        compiler_params=params(),
        name="time_block",
    )(*args)


def local(refl, refl_scale, freq_index, fd_plus, onset):
    nf = refl.shape[0]
    nrec = refl.shape[2]
    t, v, _ = fd_plus.shape
    n = lax.axis_size("freq")
    me = lax.axis_index("freq")
    nz = n // 4
    ntime = t * n
    columns = v * nrec
    width = columns // n
    c = min(width, nrec)
    nq = nrec // c
    h = width // c
    rb = 2 * nf
    nblocks = refl_scale.shape[1]
    quarter = ntime // 4

    info = jnp.concatenate(
        [onset.astype(jnp.float32), freq_index.astype(jnp.float32), refl_scale.reshape(-1)]
    )
    pad = -info.shape[0] % 128
    info = jnp.pad(info, (0, pad)).reshape(-1, 128)
    pair = jnp.stack([info, swap(info, 1)])
    quad = jnp.stack([pair, swap(pair, 2)])
    infos = jnp.stack([quad] + [swap(quad, 4 * d) for d in range(1, nz)])
    infos = infos.reshape(n, -1)
    bins_rel = infos[:, width : width + nf].astype(jnp.int32)

    ids = jnp.arange(n, dtype=jnp.int32)
    chosen = (ids[:, None] ^ me) == ids[None, :]
    infos_abs = jnp.sum(jnp.where(chosen[:, :, None], infos[None], 0.0), axis=1)
    onset_all = infos_abs[:, :width].astype(jnp.int32).reshape(v, nrec)
    bins_abs = infos_abs[:, width : width + nf].astype(jnp.int32)
    scale_abs = infos_abs[:, width + nf : width + nf + nf * nblocks].reshape(n * nf, nblocks)

    ri = jnp.arange(2, dtype=jnp.int32) * quarter
    def bin_rows(b):
        return jnp.broadcast_to(b.reshape(-1, 1), (b.size, 2)).reshape(-1)
    def quarters(b):
        return jnp.broadcast_to(ri[None, :], (b.size, 2)).reshape(-1)

    own_t = me * t + jnp.arange(t, dtype=jnp.int32)
    other_t = (me ^ 1) * t + jnp.arange(t, dtype=jnp.int32)
    even = bins_rel.reshape(2 * nz, 2, nf)[:, 0]
    table_part = cos_table(
        bin_rows(even)[:, None],
        quarters(even)[:, None],
        jnp.concatenate([own_t, other_t])[None, :],
        ntime,
    ).astype(jnp.bfloat16)
    inv_scale = jnp.float32(2.0 / ntime)
    table_time = (
        cos_table(
            bin_rows(bins_rel)[None, :], quarters(bins_rel)[None, :], own_t[:, None], ntime
        ).astype(jnp.bfloat16)
        * inv_scale.astype(jnp.bfloat16)
    )
    absq_own = jnp.where(own_t < ntime // 2, own_t, ntime - own_t)
    absq_own = jnp.broadcast_to(absq_own[:, None], (t, 128))

    half = min(-(-ONSET_TOP // 256) * 256, ntime // 2)
    times = jnp.concatenate(
        [jnp.arange(half, dtype=jnp.int32), ntime - half + jnp.arange(half, dtype=jnp.int32)]
    )
    absq_cols = jnp.where(times < ntime // 2, times, ntime - times)[:, None]
    table_fwd = cos_table(
        bin_rows(bins_abs)[:, None], quarters(bins_abs)[:, None], times[None, :], ntime
    ).astype(jnp.bfloat16)
    table_inv = (
        cos_table(
            bin_rows(bins_abs)[None, :], quarters(bins_abs)[None, :], times[:, None], ntime
        ).astype(jnp.bfloat16)
        * inv_scale.astype(jnp.bfloat16)
    )

    def spread(scales, first, count):
        block = (first + jnp.arange(count, dtype=jnp.int32)) % nrec // (nrec // nblocks)
        out = jnp.zeros((scales.shape[0], count), jnp.float32)
        for b in range(nblocks):
            out = jnp.where(block[None, :] == b, scales[:, b : b + 1], out)
        return jnp.repeat(out, 2, axis=0)

    scale_own = spread(refl_scale, 0, nrec)
    scale_cols = spread(scale_abs, me * width, width)

    mine = points_major(fd_plus)
    theirs = swap(mine, 1)
    part = partial_spectra(table_part, mine, theirs, rb, nq)
    arrived = {d: swap(part[2 * d + 1], 2) for d in range(nz - 1, -1, -1)}
    summed = {
        d: (part[2 * d].astype(jnp.float32) + arrived[d].astype(jnp.float32)).astype(jnp.bfloat16)
        for d in range(1, nz)
    }
    sent = [swap(summed[d], 4 * d) for d in range(nz - 1, 0, -1)]
    y1 = convolve([part[0], arrived[0]] + sent, scale_own, refl, 1.0)

    def exchange(x, shape):
        x = x.reshape(n, h, rb, c)
        x = lax.all_to_all(x, "freq", split_axis=0, concat_axis=0, tiled=True)
        return x.reshape(shape)

    def gather(y):
        along = [y] + [swap(y, 4 * d) for d in range(1, nz)]
        across = [swap(a, 2) for a in along]
        pairs = [p for z in zip(along, across) for p in z]
        return [p for a in pairs for p in (a, swap(a, 1))]

    x2 = window_columns(
        exchange(y1, (n, h, rb, c)),
        table_inv,
        table_fwd,
        absq_cols,
        onset.reshape(h, 1, c),
        scale_cols,
    )
    y2 = convolve([exchange(x2, (v, nq, rb, c))], None, refl, -1.0)
    minus = time_block(gather(y1), table_time, absq_own, onset_all, None, t)
    plus = time_block(gather(y2), table_time, absq_own, onset_all, fd_plus, t)
    return minus, plus


def solution(mesh):
    return jax.shard_map(
        local,
        mesh=mesh,
        in_specs=(
            P(("groups", "freq"), None, None, None),
            P(("groups", "freq"), None),
            P(("groups", "freq")),
            P(("groups", "freq"), None, None),
            P(("groups", "freq")),
        ),
        out_specs=(P(("groups", "freq"), None, None), P(("groups", "freq"), None, None)),
        check_vma=False,
    )
```

time: 550 us -> 205 us (0.37)
  the two profiles are of different devices: /device:TPU:11 before, /device:TPU:0 now
where the time goes in v1:
time: 205 us; the launch traced here: 204 us
  waiting for transfers between devices  81.5 us (40%)
  Pallas kernels  53.3 us (26%)
  starting transfers between devices  41.7 us (20%)
  other arithmetic  15.7 us (8%)
  local copies, waits for them, and re-layouts  10.1 us (5%)
    ppermute x43, waiting for transfers between devices, swap(): return lax.ppermute(x, 'freq', [(i, i ^ stride) for i in range(n)])  73 us
    ppermute x43, starting transfers between devices, swap(): return lax.ppermute(x, 'freq', [(i, i ^ stride) for i in range(n)])  33.1 us
    pallas_call x2, Pallas kernels, time_block(): pl.pallas_call(kernel, grid=(s // sb,), in_specs=specs, out_specs=field_s...  20 us
    pallas_call x2, Pallas kernels, convolve(): pl.pallas_call(kernel, grid=(nf,), in_specs=specs, out_specs=whole, out_s...  11.2 us
    pallas_call x1, Pallas kernels, points_major(): pl.pallas_call(kernel, grid=(s // sb,), in_specs=[pl.BlockSpec((t, v, sb)...  9.26 us
    all_to_all x2, starting transfers between devices, exchange(): x = lax.all_to_all(x, 'freq', split_axis=0, concat_axis=0, tiled=True)  8.59 us
    all_to_all x2, waiting for transfers between devices, exchange(): x = lax.all_to_all(x, 'freq', split_axis=0, concat_axis=0, tiled=True)  8.51 us
    pallas_call x1, Pallas kernels, partial_spectra(): pl.pallas_call(kernel, grid=(v // vb,), in_specs=[pl.BlockSpec((rows, 2 *...  7.82 us
  transfers between devices with their start and end apart: 45, of which 14 were waited for; matrix products, arithmetic and copies ran while one was open for 11% of the time, Pallas kernels for 10%

profile of v1, /device:TPU:0, one launch (start us, length us, event | category | flops | bytes accessed | tf_op | source)
XLA Modules:
  0.0 203.7 jit_solution(16815963582846285583)
XLA Ops:
  0.7 9.3 %points_major.1.own_ref = bf16[32,128,512]{2,1,0:T(8,128)(2,1)} custom-call(bf16[128,32,512]{2,1,0:T(8,128)(2,1)} %refs_19_.1), custom_call_target="tpu_custom_call" | custom-call | tf_op jit(solution)/shard_map/points_major/pallas_call | solution.py:39
  11.2 5.9 %collective-permute-done = f32[9,128]{1,0:T(8,128)S(1)} collective-permute-done((f32[9,128]{1,0:T(8,128)S(1)}, f32[9,128]{1,0:T(8,128)S(1)}, u32[]{:S(2)}, u32[]{:S(2)}) %collective-permute-start) | collective-permute-done | bytes 4640 | tf_op jit(solution)/shard_map/ppermute | solution.py:21
  17.1 2.6 %collective-permute-start.1 = (f32[2,9,128]{2,1,0:T(8,128)S(1)}, f32[2,9,128]{2,1,0:T(8,128)S(1)}, u32[]{:S(2)}, u32[]{:S(2)}) collective-permute-start(f32[2,9,128]{2,1,0:T(8,128)S(1)} %get-tuple-element.31), channel_id=1, source_target_pairs={{0,2},{1,3},{2,0},{3,1},{4,6},{5,7},{6,4},{7,5},{8,10},{9,11},{10,... | collective-permute-start | bytes 27656 | tf_op jit(solution)/shard_map/ppermute | solution.py:21
  19.7 1.7 collective-permute-done.1
  21.4 3.2 %collective-permute-start.3 = (f32[2,2,9,128]{3,2,1,0:T(8,128)S(1)}, f32[2,2,9,128]{3,2,1,0:T(8,128)S(1)}, u32[]{:S(2)}, u32[]{:S(2)}) collective-permute-start(f32[2,2,9,128]{3,2,1,0:T(8,128)S(1)} %get-tuple-element.29), channel_id=1, source_target_pairs={{0,8},{1,9},{2,10},{3,11},{4,12},{5,13},{6,14},{7,15},{8,0},{9,1},... | collective-permute-start | bytes 55304 | tf_op jit(solution)/shard_map/ppermute | solution.py:21
  24.6 1.6 collective-permute-start.2
  28.1 1.0 select_n.172.q_ref
  29.1 2.8 %collective-permute-done.4 = f32[2,2,9,128]{3,2,1,0:T(8,128)S(1)} collective-permute-done((f32[2,2,9,128]{3,2,1,0:T(8,128)S(1)}, f32[2,2,9,128]{3,2,1,0:T(8,128)S(1)}, u32[]{:S(2)}, u32[]{:S(2)}) %collective-permute-start.4) | collective-permute-done | bytes 18464 | tf_op jit(solution)/shard_map/ppermute | solution.py:21
  32.2 0.9 fusion.15.tab_ref
  33.2 7.8 %partial_spectra.1 = (bf16[32,1,8,512]{3,2,1,0:T(8,128)(2,1)}, bf16[32,1,8,512]{3,2,1,0:T(8,128)(2,1)}, bf16[32,1,8,512]{3,2,1,0:T(8,128)(2,1)}, bf16[32,1,8,512...) custom-call(bf16[64,256]{1,0:T(8,128)(2,1)} %fusion.15.tab_ref, ...), custom_call_target="tpu_custom_call" | custom-call | tf_op jit(solution)/shard_map/partial_spectra/pallas_call | solution.py:67
  41.0 1.5 collective-permute-start.7
  43.8 1.6 collective-permute-start.6
  45.9 4.7 %collective-permute-done.7 = bf16[32,1,8,512]{3,2,1,0:T(8,128)(2,1)S(1)} collective-permute-done((bf16[32,1,8,512]{3,2,1,0:T(8,128)(2,1)}, bf16[32,1,8,512]{3,2,1,0:T(8,128)(2,1)S(1)}, u32[]{:S(2)}, u32[]{:S(2)}) %collective-permute-start.7) | collective-permute-done | bytes 262176 | tf_op jit(solution)/shard_map/ppermute | solution.py:21
  50.5 1.0 add_convert_fusion.2
  51.5 1.1 collective-permute-start.8
  52.6 3.5 %collective-permute-done.9 = bf16[32,1,8,512]{3,2,1,0:T(8,128)(2,1)S(1)} collective-permute-done((bf16[32,1,8,512]{3,2,1,0:T(8,128)(2,1)}, bf16[32,1,8,512]{3,2,1,0:T(8,128)(2,1)S(1)}, u32[]{:S(2)}, u32[]{:S(2)}) %collective-permute-start.9) | collective-permute-done | bytes 262176 | tf_op jit(solution)/shard_map/ppermute | solution.py:21
  56.1 1.0 add_convert_fusion.1
  57.2 6.6 %collective-permute-done.11 = bf16[32,1,8,512]{3,2,1,0:T(8,128)(2,1)S(1)} collective-permute-done((bf16[32,1,8,512]{3,2,1,0:T(8,128)(2,1)}, bf16[32,1,8,512]{3,2,1,0:T(8,128)(2,1)S(1)}, u32[]{:S(2)}, u32[]{:S(2)}) %collective-permute-start.11) | collective-permute-done | bytes 262176 | tf_op jit(solution)/shard_map/ppermute | solution.py:21
  63.8 1.0 add_convert_fusion
  64.9 3.8 %fusion.9.fwd_ref = bf16[128,1536]{1,0:T(8,128)(2,1)} fusion(s32[128]{0:T(128)S(1)} %add.217, s32[1536]{0:T(1024)S(1)} %pad_add_fusion, s32[128]{0:T(128)S(1)} %mul.133), kind=kLoop, calls=%fused_computation.16 | loop fusion | flops 3145728 | bytes 400384 | tf_op jit(solution)/shard_map/convert_element_type | solution.py:306
  68.7 1.5 collective-permute-done.10.refs_3_
  70.2 4.1 %collective-permute-done.12.refs_4_ = bf16[32,1,8,512]{3,2,1,0:T(8,128)(2,1)S(1)} collective-permute-done((bf16[32,1,8,512]{3,2,1,0:T(8,128)(2,1)S(1)}, bf16[32,1,8,512]{3,2,1,0:T(8,128)(2,1)S(1)}, u32[]{:S(2)}, u32[]{:S(2)}) %collective-permute-start.12) | collective-permute-done | bytes 262176 | tf_op jit(solution)/shard_map/ppermute | solution.py:21
  75.0 5.8 %convolve.2.refs_0_ = bf16[32,1,8,512]{3,2,1,0:T(8,128)(2,1)} custom-call(bf16[32,1,8,512]{3,2,1,0:T(8,128)(2,1)} %get-tuple-element.10.refs_0_, bf16[32,1,8,512]{3,2,1,0:T(8,128)(2,1)} %copy-done.28, bf16[32,1,8,512]{3,2,1,0:T(8,128)(2,1)} %copy-done.29, bf16[32,1,8,512]{3,2,1,0:T(8,128)(2,1)} %copy-done.30, bf16[32,1,8,512]{3,2,1,0:T(8,128)(2,1)} %copy-done.31, ...), custom_call_target="tpu_custom_call" | custom-call | tf_op jit(solution)/shard_map/convolve/pallas_call | solution.py:134
  80.8 2.3 %collective-permute-start.24 = (bf16[32,1,8,512]{3,2,1,0:T(8,128)(2,1)}, bf16[32,1,8,512]{3,2,1,0:T(8,128)(2,1)S(1)}, u32[]{:S(2)}, u32[]{:S(2)}) collective-permute-start(bf16[32,1,8,512]{3,2,1,0:T(8,128)(2,1)} %convolve.2.refs_0_), channel_id=1, source_target_pairs={{0,12},{1,13},{2,14},{3,15},{4,8},{5,9},{6,10},{7,11},{8,4},{9,5},... | collective-permute-start | bytes 786440 | tf_op jit(solution)/shard_map/ppermute | solution.py:21
  83.2 2.1 %collective-permute-start.16 = (bf16[32,1,8,512]{3,2,1,0:T(8,128)(2,1)}, bf16[32,1,8,512]{3,2,1,0:T(8,128)(2,1)S(1)}, u32[]{:S(2)}, u32[]{:S(2)}) collective-permute-start(bf16[32,1,8,512]{3,2,1,0:T(8,128)(2,1)} %convolve.2.refs_0_), channel_id=1, source_target_pairs={{0,4},{1,5},{2,6},{3,7},{4,0},{5,1},{6,2},{7,3},{8,12},{9,13},{10,... | collective-permute-start | bytes 786440 | tf_op jit(solution)/shard_map/ppermute | solution.py:21
  85.2 1.5 collective-permute-start.14
  86.7 3.8 %all-to-all-start = ((bf16[16,2,8,512]{3,2,1,0:T(8,128)(2,1)}), bf16[16,2,8,512]{3,2,1,0:T(8,128)(2,1)S(1)}, u32[]{:S(2)}, u32[]{:S(2)}) async-start(bf16[16,2,8,512]{3,2,1,0:T(8,128)(2,1)} %bitcast.22), calls=%async_computation | async-start | bytes 524288 | tf_op jit(solution)/shard_map/all_to_all | solution.py:337
  90.5 4.1 %fusion.10.inv_ref = bf16[1536,128]{1,0:T(8,128)(2,1)} fusion(s32[128]{0:T(128)S(1)} %add.217, s32[1536]{0:T(1024)S(1)} %pad_add_fusion, s32[128]{0:T(128)S(1)} %mul.133), kind=kLoop, calls=%fused_computation.20 | loop fusion | flops 3932160 | bytes 400384 | tf_op jit(solution)/shard_map/mul | solution.py:308
  95.0 2.0 collective-permute-start.26
  97.0 11.0 %collective-permute-done.20.refs_8_ = bf16[32,1,8,512]{3,2,1,0:T(8,128)(2,1)S(1)} collective-permute-done((bf16[32,1,8,512]{3,2,1,0:T(8,128)(2,1)}, bf16[32,1,8,512]{3,2,1,0:T(8,128)(2,1)S(1)}, u32[]{:S(2)}, u32[]{:S(2)}) %collective-permute-start.20) | collective-permute-done | bytes 262176 | tf_op jit(solution)/shard_map/ppermute | solution.py:21
  108.0 1.6 collective-permute-start.22
  110.8 1.2 reshape.233.scale_ref
  112.6 5.1 %window_columns.1 = bf16[16,2,8,512]{3,2,1,0:T(8,128)(2,1)} custom-call(bf16[16,2,8,512]{3,2,1,0:T(8,128)(2,1)} %copy-done, bf16[1536,128]{1,0:T(8,128)(2,1)} %fusion.10.inv_ref, bf16[128,1536]{1,0:T(8,128)(2,1)} %fusion.9.fwd_ref, s32[1536,1]{1,0:T(8,128)} %select_n.172.q_ref, s32[2,1,512]{2,1,0:T(1,128)} %bitcast.31, f32[128,1024]{1,0:T(8,128)} %reshape.233.scale_ref), custom_call_target="tpu_custom_call" | custom-call | tf_op jit(solution)/shard_map/window_columns/pallas_call | solution.py:169
  117.7 4.8 %all-to-all-start.1 = ((bf16[16,2,8,512]{3,2,1,0:T(8,128)(2,1)}), bf16[16,2,8,512]{3,2,1,0:T(8,128)(2,1)S(1)}, u32[]{:S(2)}, u32[]{:S(2)}) async-start(bf16[16,2,8,512]{3,2,1,0:T(8,128)(2,1)} %window_columns.1), calls=%async_computation.1 | async-start | bytes 524288 | tf_op jit(solution)/shard_map/all_to_all | solution.py:337
  124.0 8.5 %all-to-all-done.1 = bf16[16,2,8,512]{3,2,1,0:T(8,128)(2,1)S(1)} async-done(((bf16[16,2,8,512]{3,2,1,0:T(8,128)(2,1)}), bf16[16,2,8,512]{3,2,1,0:T(8,128)(2,1)S(1)}, u32[]{:S(2)}, u32[]{:S(2)}) %all-to-all-start.1) | async-done | bytes 262176 | tf_op jit(solution)/shard_map/all_to_all | solution.py:337
  133.2 5.4 %convolve.3.refs_0_ = bf16[32,1,8,512]{3,2,1,0:T(8,128)(2,1)} custom-call(bf16[32,1,8,512]{3,2,1,0:T(8,128)(2,1)} %bitcast.23, bf16[4,2,512,512]{3,2,1,0:T(8,128)(2,1)} %refs_1_.1), custom_call_target="tpu_custom_call" | custom-call | tf_op jit(solution)/shard_map/convolve/pallas_call | solution.py:134
  138.7 1.1 collective-permute-start.39
  140.4 2.8 %collective-permute-start.31 = (bf16[32,1,8,512]{3,2,1,0:T(8,128)(2,1)}, bf16[32,1,8,512]{3,2,1,0:T(8,128)(2,1)S(1)}, u32[]{:S(2)}, u32[]{:S(2)}) collective-permute-start(bf16[32,1,8,512]{3,2,1,0:T(8,128)(2,1)} %convolve.3.refs_0_), channel_id=1, source_target_pairs={{0,4},{1,5},{2,6},{3,7},{4,0},{5,1},{6,2},{7,3},{8,12},{9,13},{10,... | collective-permute-start | bytes 786440 | tf_op jit(solution)/shard_map/ppermute | solution.py:21
  143.4 6.7 %collective-permute-done.39.refs_12_ = bf16[32,1,8,512]{3,2,1,0:T(8,128)(2,1)S(1)} collective-permute-done((bf16[32,1,8,512]{3,2,1,0:T(8,128)(2,1)}, bf16[32,1,8,512]{3,2,1,0:T(8,128)(2,1)S(1)}, u32[]{:S(2)}, u32[]{:S(2)}) %collective-permute-start.39) | collective-permute-done | bytes 262176 | tf_op jit(solution)/shard_map/ppermute | solution.py:21
  150.0 14.1 %collective-permute-done.35.refs_8_ = bf16[32,1,8,512]{3,2,1,0:T(8,128)(2,1)S(1)} collective-permute-done((bf16[32,1,8,512]{3,2,1,0:T(8,128)(2,1)}, bf16[32,1,8,512]{3,2,1,0:T(8,128)(2,1)S(1)}, u32[]{:S(2)}, u32[]{:S(2)}) %collective-permute-start.35) | collective-permute-done | bytes 262176 | tf_op jit(solution)/shard_map/ppermute | solution.py:21
  164.2 0.8 collective-permute-start.37
  165.3 1.3 collective-permute-start.33
  167.8 5.6 %collective-permute-done.37.refs_10_ = bf16[32,1,8,512]{3,2,1,0:T(8,128)(2,1)S(1)} collective-permute-done((bf16[32,1,8,512]{3,2,1,0:T(8,128)(2,1)S(1)}, bf16[32,1,8,512]{3,2,1,0:T(8,128)(2,1)S(1)}, u32[]{:S(2)}, u32[]{:S(2)}) %collective-permute-start.37) | collective-permute-done | bytes 262176 | tf_op jit(solution)/shard_map/ppermute | solution.py:21
  173.9 4.7 %collective-permute-done.33.refs_6_ = bf16[32,1,8,512]{3,2,1,0:T(8,128)(2,1)S(1)} collective-permute-done((bf16[32,1,8,512]{3,2,1,0:T(8,128)(2,1)S(1)}, bf16[32,1,8,512]{3,2,1,0:T(8,128)(2,1)S(1)}, u32[]{:S(2)}, u32[]{:S(2)}) %collective-permute-start.33) | collective-permute-done | bytes 262176 | tf_op jit(solution)/shard_map/ppermute | solution.py:21
  179.5 1.6 fusion.21.refs_16_
  181.1 1.4 broadcast_in_dim.230.refs_17_
  182.5 9.1 %time_block.2 = bf16[128,32,512]{2,1,0:T(8,128)(2,1)} custom-call(bf16[32,1,8,512]{3,2,1,0:T(8,128)(2,1)} %convolve.2.refs_0_, bf16[32,1,8,512]{3,2,1,0:T(8,128)(2,1)} %copy-done.19, bf16[32,1,8,512]{3,2,1,0:T(8,128)(2,1)} %copy-done.18, bf16[32,1,8,512]{3,2,1,0:T(8,128)(2,1)} %copy-done.26, bf16[32,1,8,512]{3,2,1,0:T(8,128)(2,1)} %copy-done.17, ...), custom_call_target="tpu_custom_call" | custom-call | tf_op jit(solution)/shard_map/time_block/pallas_call | solution.py:227
  192.6 10.9 %time_block.3 = f32[128,32,512]{2,1,0:T(8,128)} custom-call(bf16[32,1,8,512]{3,2,1,0:T(8,128)(2,1)} %convolve.3.refs_0_, bf16[32,1,8,512]{3,2,1,0:T(8,128)(2,1)} %copy-done.6, bf16[32,1,8,512]{3,2,1,0:T(8,128)(2,1)} %copy-done.5, bf16[32,1,8,512]{3,2,1,0:T(8,128)(2,1)} %copy-done.13, bf16[32,1,8,512]{3,2,1,0:T(8,128)(2,1)} %copy-done.4, ...), custom_call_target="tpu_custom_call" | custom-call | tf_op jit(solution)/shard_map/time_block/pallas_call | solution.py:227
  (191 shorter events, 15.1 us)
Async XLA Ops:
  9.9 23.3 %collective-permute-start.5 = (bf16[32,128,512]{2,1,0:T(8,128)(2,1)}, bf16[32,128,512]{2,1,0:T(8,128)(2,1)}, u32[]{:S(2)}, u32[]{:S(2)}) collective-permute-start(bf16[32,128,512]{2,1,0:T(8,128)(2,1)} %points_major.1.own_ref), channel_id=1, source_target_pairs={{0,1},{1,0},{2,3},{3,2},{4,5},{5,4},{6,7},{7,6},{8,9},{9,8},{10,11... | collective-permute-start | bytes 12582920 | tf_op jit(solution)/shard_map/ppermute | solution.py:21
  10.6 6.5 %collective-permute-start = (f32[9,128]{1,0:T(8,128)S(1)}, f32[9,128]{1,0:T(8,128)S(1)}, u32[]{:S(2)}, u32[]{:S(2)}) collective-permute-start(f32[9,128]{1,0:T(8,128)S(1)} %get-tuple-element.33), channel_id=1, source_target_pairs={{0,1},{1,0},{2,3},{3,2},{4,5},{5,4},{6,7},{7,6},{8,9},{9,8},{10,11... | collective-permute-start | bytes 13832 | tf_op jit(solution)/shard_map/ppermute | solution.py:21
  17.1 4.3 %collective-permute-start.1 = (f32[2,9,128]{2,1,0:T(8,128)S(1)}, f32[2,9,128]{2,1,0:T(8,128)S(1)}, u32[]{:S(2)}, u32[]{:S(2)}) collective-permute-start(f32[2,9,128]{2,1,0:T(8,128)S(1)} %get-tuple-element.31), channel_id=1, source_target_pairs={{0,2},{1,3},{2,0},{3,1},{4,6},{5,7},{6,4},{7,5},{8,10},{9,11},{10,... | collective-permute-start | bytes 27656 | tf_op jit(solution)/shard_map/ppermute | solution.py:21
  21.4 7.7 %collective-permute-start.3 = (f32[2,2,9,128]{3,2,1,0:T(8,128)S(1)}, f32[2,2,9,128]{3,2,1,0:T(8,128)S(1)}, u32[]{:S(2)}, u32[]{:S(2)}) collective-permute-start(f32[2,2,9,128]{3,2,1,0:T(8,128)S(1)} %get-tuple-element.29), channel_id=1, source_target_pairs={{0,8},{1,9},{2,10},{3,11},{4,12},{5,13},{6,14},{7,15},{8,0},{9,1},... | collective-permute-start | bytes 55304 | tf_op jit(solution)/shard_map/ppermute | solution.py:21
  24.6 4.5 %collective-permute-start.2 = (f32[2,2,9,128]{3,2,1,0:T(8,128)S(1)}, f32[2,2,9,128]{3,2,1,0:T(8,128)S(1)}, u32[]{:S(2)}, u32[]{:S(2)}) collective-permute-start(f32[2,2,9,128]{3,2,1,0:T(8,128)S(1)} %get-tuple-element.29), channel_id=1, source_target_pairs={{0,4},{1,5},{2,6},{3,7},{4,0},{5,1},{6,2},{7,3},{8,12},{9,13},{10,... | collective-permute-start | bytes 55304 | tf_op jit(solution)/shard_map/ppermute | solution.py:21
  26.2 5.7 %collective-permute-start.4 = (f32[2,2,9,128]{3,2,1,0:T(8,128)S(1)}, f32[2,2,9,128]{3,2,1,0:T(8,128)S(1)}, u32[]{:S(2)}, u32[]{:S(2)}) collective-permute-start(f32[2,2,9,128]{3,2,1,0:T(8,128)S(1)} %get-tuple-element.29), channel_id=1, source_target_pairs={{0,12},{1,13},{2,14},{3,15},{4,8},{5,9},{6,10},{7,11},{8,4},{9,5},... | collective-permute-start | bytes 55304 | tf_op jit(solution)/shard_map/ppermute | solution.py:21
  27.4 67.6 %copy-start.34 = (s32[128]{0:T(128)}, s32[128]{0:T(128)S(1)}, u32[]{:S(2)}) copy-start(s32[128]{0:T(128)S(1)} %add.217) | copy-start | bytes 1540
  41.0 9.5 %collective-permute-start.7 = (bf16[32,1,8,512]{3,2,1,0:T(8,128)(2,1)}, bf16[32,1,8,512]{3,2,1,0:T(8,128)(2,1)S(1)}, u32[]{:S(2)}, u32[]{:S(2)}) collective-permute-start(bf16[32,1,8,512]{3,2,1,0:T(8,128)(2,1)} %get-tuple-element.13), channel_id=1, source_target_pairs={{0,2},{1,3},{2,0},{3,1},{4,6},{5,7},{6,4},{7,5},{8,10},{9,11},{10,... | collective-permute-start | bytes 786440 | tf_op jit(solution)/shard_map/ppermute | solution.py:21
  42.8 13.3 %collective-permute-start.9 = (bf16[32,1,8,512]{3,2,1,0:T(8,128)(2,1)}, bf16[32,1,8,512]{3,2,1,0:T(8,128)(2,1)S(1)}, u32[]{:S(2)}, u32[]{:S(2)}) collective-permute-start(bf16[32,1,8,512]{3,2,1,0:T(8,128)(2,1)} %get-tuple-element.15), channel_id=1, source_target_pairs={{0,2},{1,3},{2,0},{3,1},{4,6},{5,7},{6,4},{7,5},{8,10},{9,11},{10,... | collective-permute-start | bytes 786440 | tf_op jit(solution)/shard_map/ppermute | solution.py:21
  43.8 25.0 %collective-permute-start.6 = (bf16[32,1,8,512]{3,2,1,0:T(8,128)(2,1)}, bf16[32,1,8,512]{3,2,1,0:T(8,128)(2,1)S(1)}, u32[]{:S(2)}, u32[]{:S(2)}) collective-permute-start(bf16[32,1,8,512]{3,2,1,0:T(8,128)(2,1)} %get-tuple-element.11), channel_id=1, source_target_pairs={{0,2},{1,3},{2,0},{3,1},{4,6},{5,7},{6,4},{7,5},{8,10},{9,11},{10,... | collective-permute-start | bytes 786440 | tf_op jit(solution)/shard_map/ppermute | solution.py:21
  45.3 18.5 %collective-permute-start.11 = (bf16[32,1,8,512]{3,2,1,0:T(8,128)(2,1)}, bf16[32,1,8,512]{3,2,1,0:T(8,128)(2,1)S(1)}, u32[]{:S(2)}, u32[]{:S(2)}) collective-permute-start(bf16[32,1,8,512]{3,2,1,0:T(8,128)(2,1)} %get-tuple-element.17), channel_id=1, source_target_pairs={{0,2},{1,3},{2,0},{3,1},{4,6},{5,7},{6,4},{7,5},{8,10},{9,11},{10,... | collective-permute-start | bytes 786440 | tf_op jit(solution)/shard_map/ppermute | solution.py:21
  51.5 17.2 %collective-permute-start.8 = (bf16[32,1,8,512]{3,2,1,0:T(8,128)(2,1)S(1)}, bf16[32,1,8,512]{3,2,1,0:T(8,128)(2,1)S(1)}, u32[]{:S(2)}, u32[]{:S(2)}) collective-permute-start(bf16[32,1,8,512]{3,2,1,0:T(8,128)(2,1)S(1)} %add_convert_fusion.2), channel_id=1, source_target_pairs={{0,12},{1,13},{2,14},{3,15},{4,8},{5,9},{6,10},{7,11},{8,4},{9,5},... | collective-permute-start | bytes 786440 | tf_op jit(solution)/shard_map/ppermute | solution.py:21
  57.2 13.1 %collective-permute-start.10 = (bf16[32,1,8,512]{3,2,1,0:T(8,128)(2,1)S(1)}, bf16[32,1,8,512]{3,2,1,0:T(8,128)(2,1)S(1)}, u32[]{:S(2)}, u32[]{:S(2)}) collective-permute-start(bf16[32,1,8,512]{3,2,1,0:T(8,128)(2,1)S(1)} %add_convert_fusion.1), channel_id=1, source_target_pairs={{0,8},{1,9},{2,10},{3,11},{4,12},{5,13},{6,14},{7,15},{8,0},{9,1},... | collective-permute-start | bytes 786440 | tf_op jit(solution)/shard_map/ppermute | solution.py:21
  64.9 9.5 %collective-permute-start.12 = (bf16[32,1,8,512]{3,2,1,0:T(8,128)(2,1)S(1)}, bf16[32,1,8,512]{3,2,1,0:T(8,128)(2,1)S(1)}, u32[]{:S(2)}, u32[]{:S(2)}) collective-permute-start(bf16[32,1,8,512]{3,2,1,0:T(8,128)(2,1)S(1)} %add_convert_fusion), channel_id=1, source_target_pairs={{0,4},{1,5},{2,6},{3,7},{4,0},{5,1},{6,2},{7,3},{8,12},{9,13},{10,... | collective-permute-start | bytes 786440 | tf_op jit(solution)/shard_map/ppermute | solution.py:21
  80.8 14.2 %collective-permute-start.24 = (bf16[32,1,8,512]{3,2,1,0:T(8,128)(2,1)}, bf16[32,1,8,512]{3,2,1,0:T(8,128)(2,1)S(1)}, u32[]{:S(2)}, u32[]{:S(2)}) collective-permute-start(bf16[32,1,8,512]{3,2,1,0:T(8,128)(2,1)} %convolve.2.refs_0_), channel_id=1, source_target_pairs={{0,12},{1,13},{2,14},{3,15},{4,8},{5,9},{6,10},{7,11},{8,4},{9,5},... | collective-permute-start | bytes 786440 | tf_op jit(solution)/shard_map/ppermute | solution.py:21
  83.2 24.8 %collective-permute-start.20 = (bf16[32,1,8,512]{3,2,1,0:T(8,128)(2,1)}, bf16[32,1,8,512]{3,2,1,0:T(8,128)(2,1)S(1)}, u32[]{:S(2)}, u32[]{:S(2)}) collective-permute-start(bf16[32,1,8,512]{3,2,1,0:T(8,128)(2,1)} %convolve.2.refs_0_), channel_id=1, source_target_pairs={{0,8},{1,9},{2,10},{3,11},{4,12},{5,13},{6,14},{7,15},{8,0},{9,1},... | collective-permute-start | bytes 786440 | tf_op jit(solution)/shard_map/ppermute | solution.py:21
  83.2 24.8 %collective-permute-start.16 = (bf16[32,1,8,512]{3,2,1,0:T(8,128)(2,1)}, bf16[32,1,8,512]{3,2,1,0:T(8,128)(2,1)S(1)}, u32[]{:S(2)}, u32[]{:S(2)}) collective-permute-start(bf16[32,1,8,512]{3,2,1,0:T(8,128)(2,1)} %convolve.2.refs_0_), channel_id=1, source_target_pairs={{0,4},{1,5},{2,6},{3,7},{4,0},{5,1},{6,2},{7,3},{8,12},{9,13},{10,... | collective-permute-start | bytes 786440 | tf_op jit(solution)/shard_map/ppermute | solution.py:21
  85.2 24.4 %collective-permute-start.14 = (bf16[32,1,8,512]{3,2,1,0:T(8,128)(2,1)}, bf16[32,1,8,512]{3,2,1,0:T(8,128)(2,1)S(1)}, u32[]{:S(2)}, u32[]{:S(2)}) collective-permute-start(bf16[32,1,8,512]{3,2,1,0:T(8,128)(2,1)} %convolve.2.refs_0_), channel_id=1, source_target_pairs={{0,2},{1,3},{2,0},{3,1},{4,6},{5,7},{6,4},{7,5},{8,10},{9,11},{10,... | collective-permute-start | bytes 786440 | tf_op jit(solution)/shard_map/ppermute | solution.py:21
  86.7 23.0 %collective-permute-start.13 = (bf16[32,1,8,512]{3,2,1,0:T(8,128)(2,1)}, bf16[32,1,8,512]{3,2,1,0:T(8,128)(2,1)S(1)}, u32[]{:S(2)}, u32[]{:S(2)}) collective-permute-start(bf16[32,1,8,512]{3,2,1,0:T(8,128)(2,1)} %convolve.2.refs_0_), channel_id=1, source_target_pairs={{0,1},{1,0},{2,3},{3,2},{4,5},{5,4},{6,7},{7,6},{8,9},{9,8},{10,11... | collective-permute-start | bytes 786440 | tf_op jit(solution)/shard_map/ppermute | solution.py:21
  86.7 25.2 %all-to-all-start = ((bf16[16,2,8,512]{3,2,1,0:T(8,128)(2,1)}), bf16[16,2,8,512]{3,2,1,0:T(8,128)(2,1)S(1)}, u32[]{:S(2)}, u32[]{:S(2)}) async-start(bf16[16,2,8,512]{3,2,1,0:T(8,128)(2,1)} %bitcast.22), calls=%async_computation | async-start | bytes 524288 | tf_op jit(solution)/shard_map/all_to_all | solution.py:337
  95.0 27.4 %collective-permute-start.26 = (bf16[32,1,8,512]{3,2,1,0:T(8,128)(2,1)S(1)}, bf16[32,1,8,512]{3,2,1,0:T(8,128)(2,1)S(1)}, u32[]{:S(2)}, u32[]{:S(2)}) collective-permute-start(bf16[32,1,8,512]{3,2,1,0:T(8,128)(2,1)S(1)} %collective-permute-done.24.refs_12_), channel_id=1, source_target_pairs={{0,2},{1,3},{2,0},{3,1},{4,6},{5,7},{6,4},{7,5},{8,10},{9,11},{10,... | collective-permute-start | bytes 786440 | tf_op jit(solution)/shard_map/ppermute | solution.py:21
  108.0 15.0 %collective-permute-start.25 = (bf16[32,1,8,512]{3,2,1,0:T(8,128)(2,1)S(1)}, bf16[32,1,8,512]{3,2,1,0:T(8,128)(2,1)S(1)}, u32[]{:S(2)}, u32[]{:S(2)}) collective-permute-start(bf16[32,1,8,512]{3,2,1,0:T(8,128)(2,1)S(1)} %collective-permute-done.24.refs_12_), channel_id=1, source_target_pairs={{0,1},{1,0},{2,3},{3,2},{4,5},{5,4},{6,7},{7,6},{8,9},{9,8},{10,11... | collective-permute-start | bytes 786440 | tf_op jit(solution)/shard_map/ppermute | solution.py:21
  108.0 15.1 %collective-permute-start.22 = (bf16[32,1,8,512]{3,2,1,0:T(8,128)(2,1)S(1)}, bf16[32,1,8,512]{3,2,1,0:T(8,128)(2,1)S(1)}, u32[]{:S(2)}, u32[]{:S(2)}) collective-permute-start(bf16[32,1,8,512]{3,2,1,0:T(8,128)(2,1)S(1)} %collective-permute-done.20.refs_8_), channel_id=1, source_target_pairs={{0,2},{1,3},{2,0},{3,1},{4,6},{5,7},{6,4},{7,5},{8,10},{9,11},{10,... | collective-permute-start | bytes 786440 | tf_op jit(solution)/shard_map/ppermute | solution.py:21
  109.6 13.9 %collective-permute-start.21 = (bf16[32,1,8,512]{3,2,1,0:T(8,128)(2,1)S(1)}, bf16[32,1,8,512]{3,2,1,0:T(8,128)(2,1)S(1)}, u32[]{:S(2)}, u32[]{:S(2)}) collective-permute-start(bf16[32,1,8,512]{3,2,1,0:T(8,128)(2,1)S(1)} %collective-permute-done.20.refs_8_), channel_id=1, source_target_pairs={{0,1},{1,0},{2,3},{3,2},{4,5},{5,4},{6,7},{7,6},{8,9},{9,8},{10,11... | collective-permute-start | bytes 786440 | tf_op jit(solution)/shard_map/ppermute | solution.py:21
  109.7 13.8 %collective-permute-start.18 = (bf16[32,1,8,512]{3,2,1,0:T(8,128)(2,1)S(1)}, bf16[32,1,8,512]{3,2,1,0:T(8,128)(2,1)S(1)}, u32[]{:S(2)}, u32[]{:S(2)}) collective-permute-start(bf16[32,1,8,512]{3,2,1,0:T(8,128)(2,1)S(1)} %collective-permute-done.16.refs_4_), channel_id=1, source_target_pairs={{0,2},{1,3},{2,0},{3,1},{4,6},{5,7},{6,4},{7,5},{8,10},{9,11},{10,... | collective-permute-start | bytes 786440 | tf_op jit(solution)/shard_map/ppermute | solution.py:21
  117.7 14.8 %all-to-all-start.1 = ((bf16[16,2,8,512]{3,2,1,0:T(8,128)(2,1)}), bf16[16,2,8,512]{3,2,1,0:T(8,128)(2,1)S(1)}, u32[]{:S(2)}, u32[]{:S(2)}) async-start(bf16[16,2,8,512]{3,2,1,0:T(8,128)(2,1)} %window_columns.1), calls=%async_computation.1 | async-start | bytes 524288 | tf_op jit(solution)/shard_map/all_to_all | solution.py:337
  122.5 16.2 %collective-permute-start.17 = (bf16[32,1,8,512]{3,2,1,0:T(8,128)(2,1)S(1)}, bf16[32,1,8,512]{3,2,1,0:T(8,128)(2,1)S(1)}, u32[]{:S(2)}, u32[]{:S(2)}) collective-permute-start(bf16[32,1,8,512]{3,2,1,0:T(8,128)(2,1)S(1)} %collective-permute-done.16.refs_4_), channel_id=1, source_target_pairs={{0,1},{1,0},{2,3},{3,2},{4,5},{5,4},{6,7},{7,6},{8,9},{9,8},{10,11... | collective-permute-start | bytes 786440 | tf_op jit(solution)/shard_map/ppermute | solution.py:21
  122.9 16.8 %collective-permute-start.15 = (bf16[32,1,8,512]{3,2,1,0:T(8,128)(2,1)S(1)}, bf16[32,1,8,512]{3,2,1,0:T(8,128)(2,1)S(1)}, u32[]{:S(2)}, u32[]{:S(2)}) collective-permute-start(bf16[32,1,8,512]{3,2,1,0:T(8,128)(2,1)S(1)} %collective-permute-done.14.refs_2_), channel_id=1, source_target_pairs={{0,1},{1,0},{2,3},{3,2},{4,5},{5,4},{6,7},{7,6},{8,9},{9,8},{10,11... | collective-permute-start | bytes 786440 | tf_op jit(solution)/shard_map/ppermute | solution.py:21
  123.1 17.4 %collective-permute-start.27 = (bf16[32,1,8,512]{3,2,1,0:T(8,128)(2,1)S(1)}, bf16[32,1,8,512]{3,2,1,0:T(8,128)(2,1)S(1)}, u32[]{:S(2)}, u32[]{:S(2)}) collective-permute-start(bf16[32,1,8,512]{3,2,1,0:T(8,128)(2,1)S(1)} %collective-permute-done.26.refs_14_), channel_id=1, source_target_pairs={{0,1},{1,0},{2,3},{3,2},{4,5},{5,4},{6,7},{7,6},{8,9},{9,8},{10,11... | collective-permute-start | bytes 786440 | tf_op jit(solution)/shard_map/ppermute | solution.py:21
  123.5 43.7 %copy-start.23 = (bf16[32,1,8,512]{3,2,1,0:T(8,128)(2,1)}, bf16[32,1,8,512]{3,2,1,0:T(8,128)(2,1)S(1)}, u32[]{:S(2)}) copy-start(bf16[32,1,8,512]{3,2,1,0:T(8,128)(2,1)S(1)} %collective-permute-done.21.refs_9_) | copy-start | bytes 786436
  123.5 19.8 %collective-permute-start.23 = (bf16[32,1,8,512]{3,2,1,0:T(8,128)(2,1)S(1)}, bf16[32,1,8,512]{3,2,1,0:T(8,128)(2,1)}, u32[]{:S(2)}, u32[]{:S(2)}) collective-permute-start(bf16[32,1,8,512]{3,2,1,0:T(8,128)(2,1)S(1)} %collective-permute-done.22.refs_10_), channel_id=1, source_target_pairs={{0,1},{1,0},{2,3},{3,2},{4,5},{5,4},{6,7},{7,6},{8,9},{9,8},{10,11... | collective-permute-start | bytes 786440 | tf_op jit(solution)/shard_map/ppermute | solution.py:21
  123.6 43.7 %copy-start.24 = (bf16[32,1,8,512]{3,2,1,0:T(8,128)(2,1)}, bf16[32,1,8,512]{3,2,1,0:T(8,128)(2,1)S(1)}, u32[]{:S(2)}) copy-start(bf16[32,1,8,512]{3,2,1,0:T(8,128)(2,1)S(1)} %collective-permute-done.18.refs_6_) | copy-start | bytes 786436
  123.6 19.7 %collective-permute-start.19 = (bf16[32,1,8,512]{3,2,1,0:T(8,128)(2,1)S(1)}, bf16[32,1,8,512]{3,2,1,0:T(8,128)(2,1)}, u32[]{:S(2)}, u32[]{:S(2)}) collective-permute-start(bf16[32,1,8,512]{3,2,1,0:T(8,128)(2,1)S(1)} %collective-permute-done.18.refs_6_), channel_id=1, source_target_pairs={{0,1},{1,0},{2,3},{3,2},{4,5},{5,4},{6,7},{7,6},{8,9},{9,8},{10,11... | collective-permute-start | bytes 786440 | tf_op jit(solution)/shard_map/ppermute | solution.py:21
  138.7 11.4 %collective-permute-start.39 = (bf16[32,1,8,512]{3,2,1,0:T(8,128)(2,1)}, bf16[32,1,8,512]{3,2,1,0:T(8,128)(2,1)S(1)}, u32[]{:S(2)}, u32[]{:S(2)}) collective-permute-start(bf16[32,1,8,512]{3,2,1,0:T(8,128)(2,1)} %convolve.3.refs_0_), channel_id=1, source_target_pairs={{0,12},{1,13},{2,14},{3,15},{4,8},{5,9},{6,10},{7,11},{8,4},{9,5},... | collective-permute-start | bytes 786440 | tf_op jit(solution)/shard_map/ppermute | solution.py:21
  139.7 24.4 %collective-permute-start.35 = (bf16[32,1,8,512]{3,2,1,0:T(8,128)(2,1)}, bf16[32,1,8,512]{3,2,1,0:T(8,128)(2,1)S(1)}, u32[]{:S(2)}, u32[]{:S(2)}) collective-permute-start(bf16[32,1,8,512]{3,2,1,0:T(8,128)(2,1)} %convolve.3.refs_0_), channel_id=1, source_target_pairs={{0,8},{1,9},{2,10},{3,11},{4,12},{5,13},{6,14},{7,15},{8,0},{9,1},... | collective-permute-start | bytes 786440 | tf_op jit(solution)/shard_map/ppermute | solution.py:21
  140.4 23.7 %collective-permute-start.31 = (bf16[32,1,8,512]{3,2,1,0:T(8,128)(2,1)}, bf16[32,1,8,512]{3,2,1,0:T(8,128)(2,1)S(1)}, u32[]{:S(2)}, u32[]{:S(2)}) collective-permute-start(bf16[32,1,8,512]{3,2,1,0:T(8,128)(2,1)} %convolve.3.refs_0_), channel_id=1, source_target_pairs={{0,4},{1,5},{2,6},{3,7},{4,0},{5,1},{6,2},{7,3},{8,12},{9,13},{10,... | collective-permute-start | bytes 786440 | tf_op jit(solution)/shard_map/ppermute | solution.py:21
  143.3 21.7 %collective-permute-start.29 = (bf16[32,1,8,512]{3,2,1,0:T(8,128)(2,1)}, bf16[32,1,8,512]{3,2,1,0:T(8,128)(2,1)S(1)}, u32[]{:S(2)}, u32[]{:S(2)}) collective-permute-start(bf16[32,1,8,512]{3,2,1,0:T(8,128)(2,1)} %convolve.3.refs_0_), channel_id=1, source_target_pairs={{0,2},{1,3},{2,0},{3,1},{4,6},{5,7},{6,4},{7,5},{8,10},{9,11},{10,... | collective-permute-start | bytes 786440 | tf_op jit(solution)/shard_map/ppermute | solution.py:21
  143.3 22.0 %collective-permute-start.28 = (bf16[32,1,8,512]{3,2,1,0:T(8,128)(2,1)}, bf16[32,1,8,512]{3,2,1,0:T(8,128)(2,1)S(1)}, u32[]{:S(2)}, u32[]{:S(2)}) collective-permute-start(bf16[32,1,8,512]{3,2,1,0:T(8,128)(2,1)} %convolve.3.refs_0_), channel_id=1, source_target_pairs={{0,1},{1,0},{2,3},{3,2},{4,5},{5,4},{6,7},{7,6},{8,9},{9,8},{10,11... | collective-permute-start | bytes 786440 | tf_op jit(solution)/shard_map/ppermute | solution.py:21
  150.0 17.1 %collective-permute-start.41 = (bf16[32,1,8,512]{3,2,1,0:T(8,128)(2,1)S(1)}, bf16[32,1,8,512]{3,2,1,0:T(8,128)(2,1)S(1)}, u32[]{:S(2)}, u32[]{:S(2)}) collective-permute-start(bf16[32,1,8,512]{3,2,1,0:T(8,128)(2,1)S(1)} %collective-permute-done.39.refs_12_), channel_id=1, source_target_pairs={{0,2},{1,3},{2,0},{3,1},{4,6},{5,7},{6,4},{7,5},{8,10},{9,11},{10,... | collective-permute-start | bytes 786440 | tf_op jit(solution)/shard_map/ppermute | solution.py:21
  164.2 3.1 %collective-permute-start.40 = (bf16[32,1,8,512]{3,2,1,0:T(8,128)(2,1)S(1)}, bf16[32,1,8,512]{3,2,1,0:T(8,128)(2,1)S(1)}, u32[]{:S(2)}, u32[]{:S(2)}) collective-permute-start(bf16[32,1,8,512]{3,2,1,0:T(8,128)(2,1)S(1)} %collective-permute-done.39.refs_12_), channel_id=1, source_target_pairs={{0,1},{1,0},{2,3},{3,2},{4,5},{5,4},{6,7},{7,6},{8,9},{9,8},{10,11... | collective-permute-start | bytes 786440 | tf_op jit(solution)/shard_map/ppermute | solution.py:21
  164.2 9.2 %collective-permute-start.37 = (bf16[32,1,8,512]{3,2,1,0:T(8,128)(2,1)S(1)}, bf16[32,1,8,512]{3,2,1,0:T(8,128)(2,1)S(1)}, u32[]{:S(2)}, u32[]{:S(2)}) collective-permute-start(bf16[32,1,8,512]{3,2,1,0:T(8,128)(2,1)S(1)} %collective-permute-done.35.refs_8_), channel_id=1, source_target_pairs={{0,2},{1,3},{2,0},{3,1},{4,6},{5,7},{6,4},{7,5},{8,10},{9,11},{10,... | collective-permute-start | bytes 786440 | tf_op jit(solution)/shard_map/ppermute | solution.py:21
  165.0 8.4 %collective-permute-start.36 = (bf16[32,1,8,512]{3,2,1,0:T(8,128)(2,1)S(1)}, bf16[32,1,8,512]{3,2,1,0:T(8,128)(2,1)S(1)}, u32[]{:S(2)}, u32[]{:S(2)}) collective-permute-start(bf16[32,1,8,512]{3,2,1,0:T(8,128)(2,1)S(1)} %collective-permute-done.35.refs_8_), channel_id=1, source_target_pairs={{0,1},{1,0},{2,3},{3,2},{4,5},{5,4},{6,7},{7,6},{8,9},{9,8},{10,11... | collective-permute-start | bytes 786440 | tf_op jit(solution)/shard_map/ppermute | solution.py:21
  165.3 13.3 %collective-permute-start.33 = (bf16[32,1,8,512]{3,2,1,0:T(8,128)(2,1)S(1)}, bf16[32,1,8,512]{3,2,1,0:T(8,128)(2,1)S(1)}, u32[]{:S(2)}, u32[]{:S(2)}) collective-permute-start(bf16[32,1,8,512]{3,2,1,0:T(8,128)(2,1)S(1)} %collective-permute-done.31.refs_4_), channel_id=1, source_target_pairs={{0,2},{1,3},{2,0},{3,1},{4,6},{5,7},{6,4},{7,5},{8,10},{9,11},{10,... | collective-permute-start | bytes 786440 | tf_op jit(solution)/shard_map/ppermute | solution.py:21
  167.1 24.6 %collective-permute-start.32 = (bf16[32,1,8,512]{3,2,1,0:T(8,128)(2,1)S(1)}, bf16[32,1,8,512]{3,2,1,0:T(8,128)(2,1)S(1)}, u32[]{:S(2)}, u32[]{:S(2)}) collective-permute-start(bf16[32,1,8,512]{3,2,1,0:T(8,128)(2,1)S(1)} %collective-permute-done.31.refs_4_), channel_id=1, source_target_pairs={{0,1},{1,0},{2,3},{3,2},{4,5},{5,4},{6,7},{7,6},{8,9},{9,8},{10,11... | collective-permute-start | bytes 786440 | tf_op jit(solution)/shard_map/ppermute | solution.py:21
  167.3 24.5 %collective-permute-start.30 = (bf16[32,1,8,512]{3,2,1,0:T(8,128)(2,1)S(1)}, bf16[32,1,8,512]{3,2,1,0:T(8,128)(2,1)S(1)}, u32[]{:S(2)}, u32[]{:S(2)}) collective-permute-start(bf16[32,1,8,512]{3,2,1,0:T(8,128)(2,1)S(1)} %collective-permute-done.29.refs_2_), channel_id=1, source_target_pairs={{0,1},{1,0},{2,3},{3,2},{4,5},{5,4},{6,7},{7,6},{8,9},{9,8},{10,11... | collective-permute-start | bytes 786440 | tf_op jit(solution)/shard_map/ppermute | solution.py:21
  173.4 18.4 %collective-permute-start.42 = (bf16[32,1,8,512]{3,2,1,0:T(8,128)(2,1)S(1)}, bf16[32,1,8,512]{3,2,1,0:T(8,128)(2,1)S(1)}, u32[]{:S(2)}, u32[]{:S(2)}) collective-permute-start(bf16[32,1,8,512]{3,2,1,0:T(8,128)(2,1)S(1)} %collective-permute-done.41.refs_14_), channel_id=1, source_target_pairs={{0,1},{1,0},{2,3},{3,2},{4,5},{5,4},{6,7},{7,6},{8,9},{9,8},{10,11... | collective-permute-start | bytes 786440 | tf_op jit(solution)/shard_map/ppermute | solution.py:21
  173.4 18.4 %collective-permute-start.38 = (bf16[32,1,8,512]{3,2,1,0:T(8,128)(2,1)S(1)}, bf16[32,1,8,512]{3,2,1,0:T(8,128)(2,1)}, u32[]{:S(2)}, u32[]{:S(2)}) collective-permute-start(bf16[32,1,8,512]{3,2,1,0:T(8,128)(2,1)S(1)} %collective-permute-done.37.refs_10_), channel_id=1, source_target_pairs={{0,1},{1,0},{2,3},{3,2},{4,5},{5,4},{6,7},{7,6},{8,9},{9,8},{10,11... | collective-permute-start | bytes 786440 | tf_op jit(solution)/shard_map/ppermute | solution.py:21
  178.6 13.2 %collective-permute-start.34 = (bf16[32,1,8,512]{3,2,1,0:T(8,128)(2,1)S(1)}, bf16[32,1,8,512]{3,2,1,0:T(8,128)(2,1)}, u32[]{:S(2)}, u32[]{:S(2)}) collective-permute-start(bf16[32,1,8,512]{3,2,1,0:T(8,128)(2,1)S(1)} %collective-permute-done.33.refs_6_), channel_id=1, source_target_pairs={{0,1},{1,0},{2,3},{3,2},{4,5},{5,4},{6,7},{7,6},{8,9},{9,8},{10,11... | collective-permute-start | bytes 786440 | tf_op jit(solution)/shard_map/ppermute | solution.py:21
  (34 other events, 597.5 us)

commit v2 on v1

v2 whole, which is shorter than its diff:
```python
import functools
import math

import jax
import jax.numpy as jnp
from jax import lax
from jax.experimental import pallas as pl
from jax.experimental.pallas import tpu as pltpu
from jax.sharding import PartitionSpec as P

ONSET_TOP = 767
VMEM_LIMIT = 56 << 20


def pitch(v):
    return v + 4


def after(x, *deps):
    return lax.optimization_barrier((x,) + deps)[0]


def params():
    return pltpu.CompilerParams(vmem_limit_bytes=VMEM_LIMIT)


def swap(x, stride):
    n = lax.axis_size("freq")
    return lax.ppermute(x, "freq", [(i, i ^ stride) for i in range(n)])


def cos_table(bins, rows_quarter, times, ntime):
    phase = (bins * times + rows_quarter) % ntime
    angle = phase.astype(jnp.float32) * jnp.float32(2.0 * math.pi / ntime)
    return jnp.cos(angle)


def points_major(x):
    t, v, s = x.shape
    sb = 128

    def kernel(x_ref, o_ref, scr):
        for i in range(t):
            scr[i * pitch(v) : i * pitch(v) + v, :] = x_ref[i].astype(jnp.float32)
        for i in range(v):
            o_ref[i] = scr[pl.ds(i, t, stride=pitch(v)), :].astype(jnp.bfloat16)

    return pl.pallas_call(
        kernel,
        grid=(s // sb,),
        in_specs=[pl.BlockSpec((t, v, sb), lambda i: (0, 0, i))],
        out_specs=pl.BlockSpec((v, t, sb), lambda i: (0, 0, i)),
        out_shape=jax.ShapeDtypeStruct((v, t, s), x.dtype),
        scratch_shapes=[pltpu.VMEM((t * pitch(v), sb), jnp.float32)],
        compiler_params=params(),
        name="points_major",
    )(x)


def partial_spectra(table, own, other, rb, nq, g, chunks):
    rows, _ = table.shape
    v, t, s = own.shape
    v //= chunks
    ndest = rows // rb
    c = s // nq
    vb = 4
    steps = v // vb

    def kernel(tab_ref, own_ref, other_ref, *outs):
        for i in range(vb):
            x = jnp.concatenate([own_ref[i], other_ref[i]], axis=0)
            res = jnp.dot(tab_ref[...], x, preferred_element_type=jnp.float32)
            for j in range(ndest):
                part = res[j * rb : (j + 1) * rb].astype(jnp.bfloat16)
                for q in range(nq):
                    outs[j][i, q] = part[:, q * c : (q + 1) * c]

    field = pl.BlockSpec((vb, t, s), lambda i: (g * steps + i, 0, 0))
    return pl.pallas_call(
        kernel,
        grid=(steps,),
        in_specs=[pl.BlockSpec((rows, 2 * t), lambda i: (0, 0)), field, field],
        out_specs=[pl.BlockSpec((vb, nq, rb, c), lambda i: (i, 0, 0, 0))] * ndest,
        out_shape=[jax.ShapeDtypeStruct((v, nq, rb, c), jnp.bfloat16)] * ndest,
        compiler_params=params(),
        name="partial_spectra",
    )(table, own, other)


def convolve(parts, scale, refl, sign):
    v, nq, rb, c = parts[0].shape
    nf, _, r, s = refl.shape
    nparts = len(parts)

    def kernel(*refs):
        part_refs = refs[:nparts]
        scale_ref = None if scale is None else refs[nparts]
        refl_ref, out_ref, x_scr, y_scr = refs[-4:]
        k = pl.program_id(0)

        @pl.when(k == 0)
        def _():
            for i in range(v):
                for q in range(nq):
                    x = part_refs[0][i, q].astype(jnp.float32)
                    for ref in part_refs[1:]:
                        x = x + ref[i, q].astype(jnp.float32)
                    for b in range(c // 128):
                        lanes = x[:, b * 128 : (b + 1) * 128]
                        at = q * (c // 128) + b
                        if scale_ref is not None:
                            block = at * 128 * scale.shape[1] // s
                            lanes = lanes * scale_ref[:, block : block + 1]
                        x_scr[at, pl.ds(i, rb, stride=pitch(v)), :] = lanes

        real = pl.ds(pl.multiple_of(2 * k * pitch(v), 8), v)
        imag = pl.ds((2 * k + 1) * pitch(v), v)
        x = jnp.concatenate(
            [
                jnp.concatenate([x_scr[b, real, :], x_scr[b, imag, :]], axis=0)
                for b in range(s // 128)
            ],
            axis=1,
        ).astype(jnp.bfloat16)
        dims = (((1,), (1,)), ((), ()))
        a = lax.dot_general(x, refl_ref[0, 0], dims, preferred_element_type=jnp.float32)
        b = lax.dot_general(x, refl_ref[0, 1], dims, preferred_element_type=jnp.float32)
        yr = a[:v] - sign * b[v:]
        yi = a[v:] + sign * b[:v]
        for b in range(r // 128):
            y_scr[b, real, :] = yr[:, b * 128 : (b + 1) * 128]
            y_scr[b, imag, :] = yi[:, b * 128 : (b + 1) * 128]

        @pl.when(k == nf - 1)
        def _():
            for i in range(v):
                for q in range(nq):
                    for b in range(c // 128):
                        y = y_scr[q * (c // 128) + b, pl.ds(i, rb, stride=pitch(v)), :]
                        out_ref[i, q, :, b * 128 : (b + 1) * 128] = y.astype(jnp.bfloat16)

    whole = pl.BlockSpec((v, nq, rb, c), lambda k: (0, 0, 0, 0))
    args = list(parts)
    specs = [whole] * nparts
    if scale is not None:
        args.append(scale)
        specs.append(pl.BlockSpec(scale.shape, lambda k: (0, 0)))
    args.append(refl)
    specs.append(pl.BlockSpec((1, 2, r, s), lambda k: (k, 0, 0, 0)))
    return pl.pallas_call(
        kernel,
        grid=(nf,),
        in_specs=specs,
        out_specs=whole,
        out_shape=jax.ShapeDtypeStruct((v, nq, rb, c), jnp.bfloat16),
        scratch_shapes=[
            pltpu.VMEM((s // 128, rb * pitch(v), 128), jnp.float32),
            pltpu.VMEM((r // 128, rb * pitch(v), 128), jnp.float32),
        ],
        compiler_params=params(),
        name="convolve",
    )(*args)


def window_columns(pieces, me, table, onset, factor):
    n = len(pieces)
    v, nq, rb, c = pieces[0].shape
    h = max(v // n, 1)
    rows = n * rb
    half = table.shape[1]
    tb = 256

    def kernel(me_ref, *refs):
        piece_refs = refs[:n]
        table_ref, onset_ref, out_ref = refs[n:]
        step = lax.broadcasted_iota(jnp.int32, (tb, c), 0)
        odd = lax.broadcasted_iota(jnp.int32, (rows, 1), 0) % 2
        sign = (1 - 2 * odd).astype(jnp.float32)
        first_dims = (((0,), (0,)), ((), ()))
        for i in range(h):
            spec = jnp.concatenate([ref[i, 0] for ref in piece_refs], axis=0)
            turned = (spec.astype(jnp.float32) * sign).astype(jnp.bfloat16)
            both = jnp.concatenate([spec, turned], axis=1)
            acc = jnp.zeros((rows, 2 * c), jnp.float32)
            for k in range(half // tb):
                tab = table_ref[:, k * tb : (k + 1) * tb]
                trace = lax.dot_general(
                    tab, both, first_dims, preferred_element_type=jnp.float32
                )
                kept = step < onset_ref[i, 0] - k * tb
                late = kept & (step > 0) if k == 0 else kept
                trace = jnp.where(jnp.concatenate([kept, late], axis=1), trace, 0.0)
                acc += jnp.dot(
                    tab, trace.astype(jnp.bfloat16), preferred_element_type=jnp.float32
                )
            acc = (acc[:, :c] + sign * acc[:, c:]) * factor
            for j in range(n):
                part = acc[j * rb : (j + 1) * rb].astype(jnp.bfloat16)
                out_ref[me_ref[0] ^ j, i] = part

    if v >= n:
        column = lambda i, me: (me[0], 0, 0, 0)
    else:
        column = lambda i, me: (me[0] // nq, me[0] % nq, 0, 0)
    whole = lambda x: pl.BlockSpec(x.shape, lambda i, me: (0,) * x.ndim)
    out_shape = jax.ShapeDtypeStruct((n, h, rb, c), jnp.bfloat16)
    return pl.pallas_call(
        kernel,
        grid_spec=pltpu.PrefetchScalarGridSpec(
            num_scalar_prefetch=1,
            grid=(1,),
            in_specs=[pl.BlockSpec((h, 1, rb, c), column)] * n
            + [whole(table), whole(onset)],
            out_specs=whole(out_shape),
        ),
        out_shape=out_shape,
        compiler_params=params(),
        name="window_columns",
    )(me[None], *pieces, table, onset)


def time_block(pieces, table, first, onset, direct, ntime, g, into):
    v, nq, rb, c = pieces[0].shape
    npieces = len(pieces)
    t = table.shape[0]
    s = nq * c
    sb = 128
    vb = 2 if v % 2 == 0 else 1
    tb = 8

    def kernel(*refs):
        piece_refs = refs[:npieces]
        tab_ref, first_ref, onset_ref = refs[npieces : npieces + 3]
        direct_ref = None if direct is None else refs[npieces + 3]
        out_ref, scr = refs[-2:]
        times = first_ref[0] + lax.broadcasted_iota(jnp.int32, (t, sb), 0)
        absq = jnp.where(times < ntime // 2, times, ntime - times)
        for i in range(0, v, vb):
            spec = jnp.concatenate(
                [
                    jnp.concatenate([ref[i + j, 0] for ref in piece_refs], axis=0)
                    for j in range(vb)
                ],
                axis=1,
            )
            res = jnp.dot(tab_ref[...], spec, preferred_element_type=jnp.float32)
            for j in range(vb):
                kept = absq < onset_ref[i + j : i + j + 1, :]
                y = jnp.where(kept, res[:, j * sb : (j + 1) * sb], 0.0)
                scr[pl.ds(i + j, t, stride=pitch(v)), :] = y

        @pl.loop(0, t // tb)
        def _(k):
            for j in range(tb):
                at = k * tb + j
                y = scr[pl.ds(at * pitch(v), v), :].astype(jnp.bfloat16)
                if direct_ref is None:
                    out_ref[at] = y
                else:
                    out_ref[at] = direct_ref[at].astype(jnp.float32) + y.astype(jnp.float32)

    per = c // sb
    piece_spec = pl.BlockSpec((v, 1, rb, sb), lambda i: (0, i // per, 0, i % per))
    field_spec = pl.BlockSpec((t, v, sb), lambda i: (0, g, i))
    args = list(pieces) + [table, first, onset]
    specs = [piece_spec] * npieces + [
        pl.BlockSpec(table.shape, lambda i: (0, 0)),
        pl.BlockSpec(memory_space=pltpu.SMEM),
        pl.BlockSpec((v, sb), lambda i: (g, i)),
    ]
    if direct is not None:
        args.append(direct)
        specs.append(field_spec)
    dtype = jnp.bfloat16 if direct is None else jnp.float32
    aliases = {}
    if into is not None:
        aliases = {len(args): 0}
        args.append(into)
        specs.append(pl.BlockSpec(memory_space=pl.ANY))
    return pl.pallas_call(
        kernel,
        grid=(s // sb,),
        in_specs=specs,
        out_specs=field_spec,
        out_shape=jax.ShapeDtypeStruct((t, onset.shape[0], s), dtype),
        scratch_shapes=[pltpu.VMEM((t * pitch(v), sb), jnp.float32)],
        input_output_aliases=aliases,
        compiler_params=params(),
        name="time_block",
    )(*args)


def local(refl, refl_scale, freq_index, fd_plus, onset):
    nf = refl.shape[0]
    nrec = refl.shape[2]
    t, v, _ = fd_plus.shape
    n = lax.axis_size("freq")
    me = lax.axis_index("freq")
    nz = n // 4
    ntime = t * n
    columns = v * nrec
    width = columns // n
    c = min(width, nrec)
    nq = nrec // c
    rb = 2 * nf
    quarter = ntime // 4

    def along(x):
        return jnp.stack([x] + [swap(x, 4 * d) for d in range(1, nz)])

    def across(x):
        return jnp.stack([x, swap(x, 2)], axis=1)

    def twins(x):
        x = jnp.stack([x, swap(x, 1)], axis=2)
        return x.reshape((n,) + x.shape[3:])

    raw = swap(fd_plus, 1)
    mine = points_major(fd_plus)
    theirs = points_major(raw)
    even = across(after(along(freq_index), mine, theirs))
    scale_own = jnp.repeat(refl_scale, 2, axis=0)

    ri = jnp.arange(2, dtype=jnp.int32) * quarter
    def bin_rows(b):
        return jnp.broadcast_to(b.reshape(-1, 1), (b.size, 2)).reshape(-1)
    def quarters(b):
        return jnp.broadcast_to(ri[None, :], (b.size, 2)).reshape(-1)

    own_t = me * t + jnp.arange(t, dtype=jnp.int32)
    other_t = (me ^ 1) * t + jnp.arange(t, dtype=jnp.int32)
    table_part = cos_table(
        bin_rows(even)[:, None],
        quarters(even)[:, None],
        jnp.concatenate([own_t, other_t])[None, :],
        ntime,
    ).astype(jnp.bfloat16)
    first_own = (me * t)[None]

    def add(*parts):
        total = parts[0].astype(jnp.float32)
        for p in parts[1:]:
            total = total + p.astype(jnp.float32)
        return total.astype(jnp.bfloat16)

    def reduce(part):
        moved = {}
        for d in range(nz - 1, -1, -1):
            x = part[2 * d + 1]
            moved[d] = swap(after(x, moved[d + 2]) if d + 2 in moved else x, 2)
        held = {d: [part[2 * d], moved[d]] for d in range(nz)}
        stride = 1
        while stride < nz:
            last = None
            for d in range(nz - 1, -1, -1):
                if d in held and d & stride:
                    total = add(*held.pop(d))
                    total = total if last is None else after(total, last)
                    to = d ^ stride
                    held[to].append(swap(total, 4 * stride))
                    if to:
                        last = add(*held[to])
                        held[to] = [last]
            stride *= 2
        return held[0], moved[min(1, nz - 1)]

    def gather(y):
        line = {0: y}
        over = {0: swap(y, 2)}
        stride = nz // 2
        far = y
        while stride:
            for d, p in list(line.items()):
                line[d ^ stride] = swap(p, 4 * stride)
                if d == 0 and stride == 1:
                    over[1] = swap(line[1], 2)
                    for k in line:
                        if k > 1:
                            line[k] = far = after(line[k], over[1])
            stride //= 2
        chip = []
        for d in range(nz):
            chip += [line[d], over[d] if d in over else swap(line[d], 2)]
        return [p for a in chip for p in (a, swap(a, 1))], far

    part = partial_spectra(table_part, mine, theirs, rb, nq, 0, 1)
    held, moved = reduce(part)
    bins_rel = after(twins(after(even, part[0])), moved)
    inv_scale = jnp.float32(2.0 / ntime)
    table_time = (
        cos_table(
            bin_rows(bins_rel)[None, :], quarters(bins_rel)[None, :], own_t[:, None], ntime
        ).astype(jnp.bfloat16)
        * inv_scale.astype(jnp.bfloat16)
    )
    half = min(-(-ONSET_TOP // 256) * 256, ntime // 2)
    table_cols = cos_table(
        bin_rows(bins_rel)[:, None],
        quarters(bins_rel)[:, None],
        jnp.arange(half, dtype=jnp.int32)[None, :],
        ntime,
    ).astype(jnp.bfloat16)

    held[0] = after(held[0], table_cols, table_time)
    y1 = convolve(held, scale_own, refl, 1.0)
    pieces, far = gather(y1)
    onset_own = onset.reshape(-1, 1, 1, c)
    x2 = window_columns(pieces, me, table_cols, onset_own, 2.0 / ntime)
    x2 = lax.all_to_all(x2, "freq", split_axis=0, concat_axis=0, tiled=True)
    onset_all = twins(across(along(after(onset.reshape(-1, 128), far)))).reshape(n, width)
    ids = jnp.arange(n, dtype=jnp.int32)
    chosen = (ids[:, None] ^ me) == ids[None, :]
    onset_all = jnp.sum(jnp.where(chosen[:, :, None], onset_all[None], 0), axis=1)
    onset_all = onset_all.reshape(v, nrec)
    minus = time_block(pieces, table_time, first_own, onset_all, None, ntime, 0, None)
    x2 = after(x2, minus).reshape(v, nq, rb, c)
    y2 = convolve([x2], scale_own, refl, -1.0)
    pieces, _ = gather(y2)
    plus = time_block(pieces, table_time, first_own, onset_all, fd_plus, ntime, 0, None)
    return minus, plus


def solution(mesh):
    return jax.shard_map(
        local,
        mesh=mesh,
        in_specs=(
            P(("groups", "freq"), None, None, None),
            P(("groups", "freq"), None),
            P(("groups", "freq")),
            P(("groups", "freq"), None, None),
            P(("groups", "freq")),
        ),
        out_specs=(P(("groups", "freq"), None, None), P(("groups", "freq"), None, None)),
        check_vma=False,
    )
```

time: 205 us -> 171 us (0.83)
  waiting for transfers between devices: 81.5 us -> 69.8 us
  other arithmetic: 15.7 us -> 7.6 us
  Pallas kernels: 53.3 us -> 46.6 us
  local copies, waits for them, and re-layouts: 10.1 us -> 4.34 us
    all_to_all x2 -> x1, waiting for transfers between devices: 8.51 us -> 1.55 us  [local(): x2 = lax.all_to_all(x2, 'freq', split_axis=0, concat_axis=0, tiled=True)]
    pallas_call x2, Pallas kernels: 20 us -> 14.6 us  [time_block(): pl.pallas_call(kernel, grid=(s // sb,), in_specs=specs, out_specs=field_s...]
    all_to_all x2 -> x1, starting transfers between devices: 8.59 us -> 3.72 us  [local(): x2 = lax.all_to_all(x2, 'freq', split_axis=0, concat_axis=0, tiled=True)]
    ppermute x43 -> x48, waiting for transfers between devices: 73 us -> 68.2 us  [swap(): return lax.ppermute(x, 'freq', [(i, i ^ stride) for i in range(n)])]
    mul x1 -> x0, other arithmetic: 4.07 us -> none  [local(): cos_table(bin_rows(bins_abs)[None, :], quarters(bins_abs)[None, :], times...]
    ppermute x43 -> x48, starting transfers between devices: 33.1 us -> 36.2 us  [swap(): return lax.ppermute(x, 'freq', [(i, i ^ stride) for i in range(n)])]
    convert_element_type x9 -> x4, other arithmetic: 6.85 us -> 5.34 us  [the longest x3 3.09 us: add(): return total.astype(jnp.bfloat16)]
    pallas_call x1 -> x2, Pallas kernels: 9.26 us -> 10.2 us  [points_major(): pl.pallas_call(kernel, grid=(s // sb,), in_specs=[pl.BlockSpec((t, v, sb)...]
  transfers between devices with their start and end apart: 45 -> 49, of which waited for: 14 -> 24; matrix products, arithmetic and copies ran while one was open for 11% -> 5% of each run, Pallas kernels for 10% -> 9%
where the time goes in v2:
time: 171 us; the launch traced here: 170 us
  waiting for transfers between devices  69.8 us (41%)
  Pallas kernels  46.6 us (27%)
  starting transfers between devices  39.9 us (23%)
  other arithmetic  7.6 us (4%)
  local copies, waits for them, and re-layouts  4.34 us (3%)
    ppermute x48, waiting for transfers between devices, swap(): return lax.ppermute(x, 'freq', [(i, i ^ stride) for i in range(n)])  68.2 us
    ppermute x48, starting transfers between devices, swap(): return lax.ppermute(x, 'freq', [(i, i ^ stride) for i in range(n)])  36.2 us
    pallas_call x2, Pallas kernels, time_block(): pl.pallas_call(kernel, grid=(s // sb,), in_specs=specs, out_specs=field_s...  14.6 us
    pallas_call x2, Pallas kernels, points_major(): pl.pallas_call(kernel, grid=(s // sb,), in_specs=[pl.BlockSpec((t, v, sb)...  10.2 us
    pallas_call x2, Pallas kernels, convolve(): pl.pallas_call(kernel, grid=(nf,), in_specs=specs, out_specs=whole, out_s...  10.1 us
    pallas_call x1, Pallas kernels, partial_spectra(): pl.pallas_call(kernel, grid=(steps,), in_specs=[pl.BlockSpec((rows, 2 * t...  7.83 us
    pallas_call x1, Pallas kernels, window_columns(): pl.pallas_call(kernel, grid_spec=pltpu.PrefetchScalarGridSpec(num_scalar_...  3.87 us
    all_to_all x1, starting transfers between devices, local(): x2 = lax.all_to_all(x2, 'freq', split_axis=0, concat_axis=0, tiled=True)  3.72 us
  transfers between devices with their start and end apart: 49, of which 24 were waited for; matrix products, arithmetic and copies ran while one was open for 5% of the time, Pallas kernels for 9%

profile of v2, /device:TPU:0, one launch (start us, length us, event | category | flops | bytes accessed | tf_op | source)
XLA Modules:
  0.0 169.6 jit_solution(14682928011312076751)
XLA Ops:
  1.1 2.7 %collective-permute-start = (s32[4]{0:T(128)}, s32[4]{0:T(128)S(1)}, u32[]{:S(2)}, u32[]{:S(2)}) collective-permute-start(s32[4]{0:T(128)} %param.7), channel_id=1, source_target_pairs={{0,4},{1,5},{2,6},{3,7},{4,0},{5,1},{6,2},{7,3},{8,12},{9,13},{10,... | collective-permute-start | bytes 56 | tf_op jit(solution)/shard_map/ppermute | solution.py:29
  3.8 2.5 %collective-permute-start.2 = (s32[4]{0:T(128)}, s32[4]{0:T(128)S(1)}, u32[]{:S(2)}, u32[]{:S(2)}) collective-permute-start(s32[4]{0:T(128)} %param.7), channel_id=1, source_target_pairs={{0,12},{1,13},{2,14},{3,15},{4,8},{5,9},{6,10},{7,11},{8,4},{9,5},... | collective-permute-start | bytes 56 | tf_op jit(solution)/shard_map/ppermute | solution.py:29
  6.4 5.1 %points_major.2.own_ref = bf16[32,128,512]{2,1,0:T(8,128)(2,1)} custom-call(bf16[128,32,512]{2,1,0:T(8,128)(2,1)} %refs_19_.1), custom_call_target="tpu_custom_call" | custom-call | tf_op jit(solution)/shard_map/points_major/pallas_call | solution.py:48
  11.6 5.1 %points_major.3.other_ref = bf16[32,128,512]{2,1,0:T(8,128)(2,1)} custom-call(bf16[128,32,512]{2,1,0:T(8,128)(2,1)} %collective-permute-done.3.x_ref), custom_call_target="tpu_custom_call" | custom-call | tf_op jit(solution)/shard_map/points_major/pallas_call | solution.py:48
  16.6 1.5 collective-permute-start.4
  18.2 2.0 %collective-permute-done.4 = s32[4,4]{1,0:T(4,128)S(1)} collective-permute-done((s32[4,4]{1,0:T(4,128)S(1)}, s32[4,4]{1,0:T(4,128)S(1)}, u32[]{:S(2)}, u32[]{:S(2)}) %collective-permute-start.4) | collective-permute-done | bytes 96 | tf_op jit(solution)/shard_map/ppermute | solution.py:29
  21.5 7.8 %partial_spectra.1 = (bf16[32,1,8,512]{3,2,1,0:T(8,128)(2,1)}, bf16[32,1,8,512]{3,2,1,0:T(8,128)(2,1)}, bf16[32,1,8,512]{3,2,1,0:T(8,128)(2,1)}, bf16[32,1,8,512...) custom-call(bf16[64,256]{1,0:T(8,128)(2,1)} %fusion.9.tab_ref, ...), custom_call_target="tpu_custom_call" | custom-call | tf_op jit(solution)/shard_map/partial_spectra/pallas_call | solution.py:79
  29.3 1.5 collective-permute-start.6
  31.4 7.4 %collective-permute-done.6 = bf16[32,1,8,512]{3,2,1,0:T(8,128)(2,1)S(1)} collective-permute-done((bf16[32,1,8,512]{3,2,1,0:T(8,128)(2,1)}, bf16[32,1,8,512]{3,2,1,0:T(8,128)(2,1)S(1)}, u32[]{:S(2)}, u32[]{:S(2)}) %collective-permute-start.6) | collective-permute-done | bytes 262176 | tf_op jit(solution)/shard_map/ppermute | solution.py:29
  38.8 1.5 collective-permute-start.7
  40.3 1.0 add_convert_fusion.1
  41.3 1.9 %collective-permute-start.10 = (bf16[32,1,8,512]{3,2,1,0:T(8,128)(2,1)S(1)}, bf16[32,1,8,512]{3,2,1,0:T(8,128)(2,1)S(1)}, u32[]{:S(2)}, u32[]{:S(2)}) collective-permute-start(bf16[32,1,8,512]{3,2,1,0:T(8,128)(2,1)S(1)} %add_convert_fusion.1), channel_id=1, source_target_pairs={{0,4},{1,5},{2,6},{3,7},{4,0},{5,1},{6,2},{7,3},{8,12},{9,13},{10,... | collective-permute-start | bytes 786440 | tf_op jit(solution)/shard_map/ppermute | solution.py:29
  43.3 1.0 collective-permute-done.5
  44.4 1.5 collective-permute-start.9
  45.9 2.1 %collective-permute-done.7 = bf16[32,1,8,512]{3,2,1,0:T(8,128)(2,1)S(1)} collective-permute-done((bf16[32,1,8,512]{3,2,1,0:T(8,128)(2,1)}, bf16[32,1,8,512]{3,2,1,0:T(8,128)(2,1)S(1)}, u32[]{:S(2)}, u32[]{:S(2)}) %collective-permute-start.7) | collective-permute-done | bytes 262176 | tf_op jit(solution)/shard_map/ppermute | solution.py:29
  48.4 1.1 add_convert_fusion
  49.4 3.4 %collective-permute-start.12 = (bf16[32,1,8,512]{3,2,1,0:T(8,128)(2,1)S(1)}, bf16[32,1,8,512]{3,2,1,0:T(8,128)(2,1)S(1)}, u32[]{:S(2)}, u32[]{:S(2)}) collective-permute-start(bf16[32,1,8,512]{3,2,1,0:T(8,128)(2,1)S(1)} %add_convert_fusion), channel_id=1, source_target_pairs={{0,8},{1,9},{2,10},{3,11},{4,12},{5,13},{6,14},{7,15},{8,0},{9,1},... | collective-permute-start | bytes 786440 | tf_op jit(solution)/shard_map/ppermute | solution.py:29
  52.9 1.0 add_convert_fusion.2
  54.9 2.2 %fusion.4.refs_16_ = bf16[128,768]{1,0:T(8,128)(2,1)} fusion(s32[128]{0:T(128)S(1)} %add.84, s32[128]{0:T(128)S(1)} %mul.94), kind=kLoop, calls=%fused_computation.11 | loop fusion | flops 1572864 | bytes 197632 | tf_op jit(solution)/shard_map/convert_element_type | solution.py:402
  57.1 5.9 %collective-permute-done.11.refs_2_ = bf16[32,1,8,512]{3,2,1,0:T(8,128)(2,1)S(1)} collective-permute-done((bf16[32,1,8,512]{3,2,1,0:T(8,128)(2,1)S(1)}, bf16[32,1,8,512]{3,2,1,0:T(8,128)(2,1)S(1)}, u32[]{:S(2)}, u32[]{:S(2)}) %collective-permute-start.11) | collective-permute-done | bytes 262176 | tf_op jit(solution)/shard_map/ppermute | solution.py:29
  63.9 5.2 %convolve.2.refs_0_ = bf16[32,1,8,512]{3,2,1,0:T(8,128)(2,1)} custom-call(bf16[32,1,8,512]{3,2,1,0:T(8,128)(2,1)} %get-tuple-element.28.refs_0_, bf16[32,1,8,512]{3,2,1,0:T(8,128)(2,1)} %copy-done.31, bf16[32,1,8,512]{3,2,1,0:T(8,128)(2,1)} %copy-done.33, bf16[32,1,8,512]{3,2,1,0:T(8,128)(2,1)} %copy-done.32, f32[8,4]{1,0:T(8,128)} %bitcast.41, ...), custom_call_target="tpu_custom_call" | custom-call | tf_op jit(solution)/shard_map/convolve/pallas_call | solution.py:150
  69.1 2.0 %collective-permute-start.20 = (bf16[32,1,8,512]{3,2,1,0:T(8,128)(2,1)}, bf16[32,1,8,512]{3,2,1,0:T(8,128)(2,1)S(1)}, u32[]{:S(2)}, u32[]{:S(2)}) collective-permute-start(bf16[32,1,8,512]{3,2,1,0:T(8,128)(2,1)} %convolve.2.refs_0_), channel_id=1, source_target_pairs={{0,8},{1,9},{2,10},{3,11},{4,12},{5,13},{6,14},{7,15},{8,0},{9,1},... | collective-permute-start | bytes 786440 | tf_op jit(solution)/shard_map/ppermute | solution.py:29
  71.2 1.8 %collective-permute-start.14 = (bf16[32,1,8,512]{3,2,1,0:T(8,128)(2,1)}, bf16[32,1,8,512]{3,2,1,0:T(8,128)(2,1)S(1)}, u32[]{:S(2)}, u32[]{:S(2)}) collective-permute-start(bf16[32,1,8,512]{3,2,1,0:T(8,128)(2,1)} %convolve.2.refs_0_), channel_id=1, source_target_pairs={{0,2},{1,3},{2,0},{3,1},{4,6},{5,7},{6,4},{7,5},{8,10},{9,11},{10,... | collective-permute-start | bytes 786440 | tf_op jit(solution)/shard_map/ppermute | solution.py:29
  72.9 7.1 %collective-permute-done.16.refs_4_ = bf16[32,1,8,512]{3,2,1,0:T(8,128)(2,1)S(1)} collective-permute-done((bf16[32,1,8,512]{3,2,1,0:T(8,128)(2,1)}, bf16[32,1,8,512]{3,2,1,0:T(8,128)(2,1)S(1)}, u32[]{:S(2)}, u32[]{:S(2)}) %collective-permute-start.16) | collective-permute-done | bytes 262176 | tf_op jit(solution)/shard_map/ppermute | solution.py:29
  80.0 1.9 %collective-permute-done.20.refs_8_ = bf16[32,1,8,512]{3,2,1,0:T(8,128)(2,1)S(1)} collective-permute-done((bf16[32,1,8,512]{3,2,1,0:T(8,128)(2,1)}, bf16[32,1,8,512]{3,2,1,0:T(8,128)(2,1)S(1)}, u32[]{:S(2)}, u32[]{:S(2)}) %collective-permute-start.20) | collective-permute-done | bytes 262176 | tf_op jit(solution)/shard_map/ppermute | solution.py:29
  82.5 4.7 %collective-permute-done.18.refs_6_ = bf16[32,1,8,512]{3,2,1,0:T(8,128)(2,1)S(1)} collective-permute-done((bf16[32,1,8,512]{3,2,1,0:T(8,128)(2,1)S(1)}, bf16[32,1,8,512]{3,2,1,0:T(8,128)(2,1)S(1)}, u32[]{:S(2)}, u32[]{:S(2)}) %collective-permute-start.18) | collective-permute-done | bytes 262176 | tf_op jit(solution)/shard_map/ppermute | solution.py:29
  87.3 1.1 collective-permute-done.24.refs_12_
  89.0 1.3 collective-permute-start.22
  90.4 2.1 %collective-permute-start.30 = (s32[8,128]{1,0:T(8,128)S(1)}, s32[8,128]{1,0:T(8,128)S(1)}, u32[]{:S(2)}, u32[]{:S(2)}) collective-permute-start(s32[8,128]{1,0:T(8,128)S(1)} %bitcast.49), channel_id=1, source_target_pairs={{0,12},{1,13},{2,14},{3,15},{4,8},{5,9},{6,10},{7,11},{8,4},{9,5},... | collective-permute-start | bytes 12296 | tf_op jit(solution)/shard_map/ppermute | solution.py:29
  92.5 3.4 %collective-permute-done.30 = s32[8,128]{1,0:T(8,128)S(1)} collective-permute-done((s32[8,128]{1,0:T(8,128)S(1)}, s32[8,128]{1,0:T(8,128)S(1)}, u32[]{:S(2)}, u32[]{:S(2)}) %collective-permute-start.30) | collective-permute-done | bytes 4128 | tf_op jit(solution)/shard_map/ppermute | solution.py:29
  95.9 1.1 collective-permute-done.29
  97.0 2.5 %collective-permute-done.28 = s32[8,128]{1,0:T(8,128)S(1)} collective-permute-done((s32[8,128]{1,0:T(8,128)S(1)}, s32[8,128]{1,0:T(8,128)S(1)}, u32[]{:S(2)}, u32[]{:S(2)}) %collective-permute-start.28) | collective-permute-done | bytes 4128 | tf_op jit(solution)/shard_map/ppermute | solution.py:29
  102.4 3.9 %window_columns.1 = bf16[16,2,8,512]{3,2,1,0:T(8,128)(2,1)} custom-call(s32[1]{0:T(128)} %bitcast.22.me_ref, bf16[32,1,8,512]{3,2,1,0:T(8,128)(2,1)} %convolve.2.refs_0_, bf16[32,1,8,512]{3,2,1,0:T(8,128)(2,1)} %copy-done.5, bf16[32,1,8,512]{3,2,1,0:T(8,128)(2,1)} %copy-done.2, bf16[32,1,8,512]{3,2,1,0:T(8,128)(2,1)} %copy-done.7, ...), custom_call_target="tpu_custom_call" | custom-call | tf_op jit(solution)/shard_map/window_columns/pallas_call | solution.py:207
  106.3 3.7 %all-to-all-start = ((bf16[16,2,8,512]{3,2,1,0:T(8,128)(2,1)}), bf16[16,2,8,512]{3,2,1,0:T(8,128)(2,1)S(1)}, u32[]{:S(2)}, u32[]{:S(2)}) async-start(bf16[16,2,8,512]{3,2,1,0:T(8,128)(2,1)} %window_columns.1), calls=%async_computation | async-start | bytes 524288 | tf_op jit(solution)/shard_map/all_to_all | solution.py:409
  112.3 6.1 %time_block.2 = bf16[128,32,512]{2,1,0:T(8,128)(2,1)} custom-call(bf16[32,1,8,512]{3,2,1,0:T(8,128)(2,1)} %convolve.2.refs_0_, bf16[32,1,8,512]{3,2,1,0:T(8,128)(2,1)} %copy-done.5, bf16[32,1,8,512]{3,2,1,0:T(8,128)(2,1)} %copy-done.2, bf16[32,1,8,512]{3,2,1,0:T(8,128)(2,1)} %copy-done.7, bf16[32,1,8,512]{3,2,1,0:T(8,128)(2,1)} %copy-done, ...), custom_call_target="tpu_custom_call" | custom-call | tf_op jit(solution)/shard_map/time_block/pallas_call | solution.py:280
  118.4 1.5 all-to-all-done
  120.6 4.9 %convolve.3.refs_0_ = bf16[32,1,8,512]{3,2,1,0:T(8,128)(2,1)} custom-call(bf16[32,1,8,512]{3,2,1,0:T(8,128)(2,1)} %bitcast.38, f32[8,4]{1,0:T(8,128)} %bitcast.42, bf16[4,2,512,512]{3,2,1,0:T(8,128)(2,1)} %refs_2_.1), custom_call_target="tpu_custom_call" | custom-call | tf_op jit(solution)/shard_map/convolve/pallas_call | solution.py:150
  125.8 2.4 %collective-permute-start.40 = (bf16[32,1,8,512]{3,2,1,0:T(8,128)(2,1)}, bf16[32,1,8,512]{3,2,1,0:T(8,128)(2,1)S(1)}, u32[]{:S(2)}, u32[]{:S(2)}) collective-permute-start(bf16[32,1,8,512]{3,2,1,0:T(8,128)(2,1)} %convolve.3.refs_0_), channel_id=1, source_target_pairs={{0,8},{1,9},{2,10},{3,11},{4,12},{5,13},{6,14},{7,15},{8,0},{9,1},... | collective-permute-start | bytes 786440 | tf_op jit(solution)/shard_map/ppermute | solution.py:29
  128.2 1.5 collective-permute-start.34
  129.6 9.3 %collective-permute-done.36.refs_4_ = bf16[32,1,8,512]{3,2,1,0:T(8,128)(2,1)S(1)} collective-permute-done((bf16[32,1,8,512]{3,2,1,0:T(8,128)(2,1)}, bf16[32,1,8,512]{3,2,1,0:T(8,128)(2,1)S(1)}, u32[]{:S(2)}, u32[]{:S(2)}) %collective-permute-start.36) | collective-permute-done | bytes 262176 | tf_op jit(solution)/shard_map/ppermute | solution.py:29
  139.9 1.1 collective-permute-done.40.refs_8_
  141.6 4.5 %collective-permute-done.38.refs_6_ = bf16[32,1,8,512]{3,2,1,0:T(8,128)(2,1)S(1)} collective-permute-done((bf16[32,1,8,512]{3,2,1,0:T(8,128)(2,1)S(1)}, bf16[32,1,8,512]{3,2,1,0:T(8,128)(2,1)S(1)}, u32[]{:S(2)}, u32[]{:S(2)}) %collective-permute-start.38) | collective-permute-done | bytes 262176 | tf_op jit(solution)/shard_map/ppermute | solution.py:29
  146.1 1.2 collective-permute-done.44.refs_12_
  147.4 1.1 collective-permute-start.46
  150.0 5.7 %collective-permute-done.46.refs_14_ = bf16[32,1,8,512]{3,2,1,0:T(8,128)(2,1)S(1)} collective-permute-done((bf16[32,1,8,512]{3,2,1,0:T(8,128)(2,1)S(1)}, bf16[32,1,8,512]{3,2,1,0:T(8,128)(2,1)S(1)}, u32[]{:S(2)}, u32[]{:S(2)}) %collective-permute-start.46) | collective-permute-done | bytes 262176 | tf_op jit(solution)/shard_map/ppermute | solution.py:29
  155.7 2.8 %collective-permute-done.42.refs_10_ = bf16[32,1,8,512]{3,2,1,0:T(8,128)(2,1)S(1)} collective-permute-done((bf16[32,1,8,512]{3,2,1,0:T(8,128)(2,1)S(1)}, bf16[32,1,8,512]{3,2,1,0:T(8,128)(2,1)S(1)}, u32[]{:S(2)}, u32[]{:S(2)}) %collective-permute-start.42) | collective-permute-done | bytes 262176 | tf_op jit(solution)/shard_map/ppermute | solution.py:29
  158.6 1.5 collective-permute-done.43.refs_11_
  160.9 8.5 %time_block.3 = f32[128,32,512]{2,1,0:T(8,128)} custom-call(bf16[32,1,8,512]{3,2,1,0:T(8,128)(2,1)} %convolve.3.refs_0_, bf16[32,1,8,512]{3,2,1,0:T(8,128)(2,1)} %copy-done.21, bf16[32,1,8,512]{3,2,1,0:T(8,128)(2,1)} %copy-done.18, bf16[32,1,8,512]{3,2,1,0:T(8,128)(2,1)} %copy-done.23, bf16[32,1,8,512]{3,2,1,0:T(8,128)(2,1)} %copy-done.16, ...), custom_call_target="tpu_custom_call" | custom-call | tf_op jit(solution)/shard_map/time_block/pallas_call | solution.py:280
  (168 shorter events, 16.0 us)
Async XLA Ops:
  0.6 10.9 %collective-permute-start.3 = (bf16[128,32,512]{2,1,0:T(8,128)(2,1)}, bf16[128,32,512]{2,1,0:T(8,128)(2,1)}, u32[]{:S(2)}, u32[]{:S(2)}) collective-permute-start(bf16[128,32,512]{2,1,0:T(8,128)(2,1)} %refs_19_.1), channel_id=1, source_target_pairs={{0,1},{1,0},{2,3},{3,2},{4,5},{5,4},{6,7},{7,6},{8,9},{9,8},{10,11... | collective-permute-start | bytes 12582920 | tf_op jit(solution)/shard_map/ppermute | solution.py:29
  1.1 10.4 %collective-permute-start = (s32[4]{0:T(128)}, s32[4]{0:T(128)S(1)}, u32[]{:S(2)}, u32[]{:S(2)}) collective-permute-start(s32[4]{0:T(128)} %param.7), channel_id=1, source_target_pairs={{0,4},{1,5},{2,6},{3,7},{4,0},{5,1},{6,2},{7,3},{8,12},{9,13},{10,... | collective-permute-start | bytes 56 | tf_op jit(solution)/shard_map/ppermute | solution.py:29
  3.8 7.7 %collective-permute-start.2 = (s32[4]{0:T(128)}, s32[4]{0:T(128)S(1)}, u32[]{:S(2)}, u32[]{:S(2)}) collective-permute-start(s32[4]{0:T(128)} %param.7), channel_id=1, source_target_pairs={{0,12},{1,13},{2,14},{3,15},{4,8},{5,9},{6,10},{7,11},{8,4},{9,5},... | collective-permute-start | bytes 56 | tf_op jit(solution)/shard_map/ppermute | solution.py:29
  6.3 5.2 %collective-permute-start.1 = (s32[4]{0:T(128)}, s32[4]{0:T(128)S(1)}, u32[]{:S(2)}, u32[]{:S(2)}) collective-permute-start(s32[4]{0:T(128)} %param.7), channel_id=1, source_target_pairs={{0,8},{1,9},{2,10},{3,11},{4,12},{5,13},{6,14},{7,15},{8,0},{9,1},... | collective-permute-start | bytes 56 | tf_op jit(solution)/shard_map/ppermute | solution.py:29
  16.6 3.6 %collective-permute-start.4 = (s32[4,4]{1,0:T(4,128)S(1)}, s32[4,4]{1,0:T(4,128)S(1)}, u32[]{:S(2)}, u32[]{:S(2)}) collective-permute-start(s32[4,4]{1,0:T(4,128)S(1)} %pad_add_fusion.5), channel_id=1, source_target_pairs={{0,2},{1,3},{2,0},{3,1},{4,6},{5,7},{6,4},{7,5},{8,10},{9,11},{10,... | collective-permute-start | bytes 200 | tf_op jit(solution)/shard_map/ppermute | solution.py:29
  29.3 9.5 %collective-permute-start.6 = (bf16[32,1,8,512]{3,2,1,0:T(8,128)(2,1)}, bf16[32,1,8,512]{3,2,1,0:T(8,128)(2,1)S(1)}, u32[]{:S(2)}, u32[]{:S(2)}) collective-permute-start(bf16[32,1,8,512]{3,2,1,0:T(8,128)(2,1)} %get-tuple-element.25), channel_id=1, source_target_pairs={{0,2},{1,3},{2,0},{3,1},{4,6},{5,7},{6,4},{7,5},{8,10},{9,11},{10,... | collective-permute-start | bytes 786440 | tf_op jit(solution)/shard_map/ppermute | solution.py:29
  30.8 13.6 %collective-permute-start.8 = (bf16[32,1,8,512]{3,2,1,0:T(8,128)(2,1)}, bf16[32,1,8,512]{3,2,1,0:T(8,128)(2,1)S(1)}, u32[]{:S(2)}, u32[]{:S(2)}) collective-permute-start(bf16[32,1,8,512]{3,2,1,0:T(8,128)(2,1)} %get-tuple-element.30), channel_id=1, source_target_pairs={{0,2},{1,3},{2,0},{3,1},{4,6},{5,7},{6,4},{7,5},{8,10},{9,11},{10,... | collective-permute-start | bytes 786440 | tf_op jit(solution)/shard_map/ppermute | solution.py:29
  38.8 9.2 %collective-permute-start.7 = (bf16[32,1,8,512]{3,2,1,0:T(8,128)(2,1)}, bf16[32,1,8,512]{3,2,1,0:T(8,128)(2,1)S(1)}, u32[]{:S(2)}, u32[]{:S(2)}) collective-permute-start(bf16[32,1,8,512]{3,2,1,0:T(8,128)(2,1)} %get-tuple-element.26), channel_id=1, source_target_pairs={{0,2},{1,3},{2,0},{3,1},{4,6},{5,7},{6,4},{7,5},{8,10},{9,11},{10,... | collective-permute-start | bytes 786440 | tf_op jit(solution)/shard_map/ppermute | solution.py:29
  41.3 7.0 %collective-permute-start.10 = (bf16[32,1,8,512]{3,2,1,0:T(8,128)(2,1)S(1)}, bf16[32,1,8,512]{3,2,1,0:T(8,128)(2,1)S(1)}, u32[]{:S(2)}, u32[]{:S(2)}) collective-permute-start(bf16[32,1,8,512]{3,2,1,0:T(8,128)(2,1)S(1)} %add_convert_fusion.1), channel_id=1, source_target_pairs={{0,4},{1,5},{2,6},{3,7},{4,0},{5,1},{6,2},{7,3},{8,12},{9,13},{10,... | collective-permute-start | bytes 786440 | tf_op jit(solution)/shard_map/ppermute | solution.py:29
  44.4 12.7 %collective-permute-start.9 = (bf16[32,1,8,512]{3,2,1,0:T(8,128)(2,1)}, bf16[32,1,8,512]{3,2,1,0:T(8,128)(2,1)S(1)}, u32[]{:S(2)}, u32[]{:S(2)}) collective-permute-start(bf16[32,1,8,512]{3,2,1,0:T(8,128)(2,1)} %get-tuple-element.31), channel_id=1, source_target_pairs={{0,2},{1,3},{2,0},{3,1},{4,6},{5,7},{6,4},{7,5},{8,10},{9,11},{10,... | collective-permute-start | bytes 786440 | tf_op jit(solution)/shard_map/ppermute | solution.py:29
  49.4 13.7 %collective-permute-start.12 = (bf16[32,1,8,512]{3,2,1,0:T(8,128)(2,1)S(1)}, bf16[32,1,8,512]{3,2,1,0:T(8,128)(2,1)S(1)}, u32[]{:S(2)}, u32[]{:S(2)}) collective-permute-start(bf16[32,1,8,512]{3,2,1,0:T(8,128)(2,1)S(1)} %add_convert_fusion), channel_id=1, source_target_pairs={{0,8},{1,9},{2,10},{3,11},{4,12},{5,13},{6,14},{7,15},{8,0},{9,1},... | collective-permute-start | bytes 786440 | tf_op jit(solution)/shard_map/ppermute | solution.py:29
  53.9 9.2 %collective-permute-start.11 = (bf16[32,1,8,512]{3,2,1,0:T(8,128)(2,1)S(1)}, bf16[32,1,8,512]{3,2,1,0:T(8,128)(2,1)S(1)}, u32[]{:S(2)}, u32[]{:S(2)}) collective-permute-start(bf16[32,1,8,512]{3,2,1,0:T(8,128)(2,1)S(1)} %add_convert_fusion.2), channel_id=1, source_target_pairs={{0,4},{1,5},{2,6},{3,7},{4,0},{5,1},{6,2},{7,3},{8,12},{9,13},{10,... | collective-permute-start | bytes 786440 | tf_op jit(solution)/shard_map/ppermute | solution.py:29
  69.1 11.0 %collective-permute-start.16 = (bf16[32,1,8,512]{3,2,1,0:T(8,128)(2,1)}, bf16[32,1,8,512]{3,2,1,0:T(8,128)(2,1)S(1)}, u32[]{:S(2)}, u32[]{:S(2)}) collective-permute-start(bf16[32,1,8,512]{3,2,1,0:T(8,128)(2,1)} %convolve.2.refs_0_), channel_id=1, source_target_pairs={{0,4},{1,5},{2,6},{3,7},{4,0},{5,1},{6,2},{7,3},{8,12},{9,13},{10,... | collective-permute-start | bytes 786440 | tf_op jit(solution)/shard_map/ppermute | solution.py:29
  69.1 12.8 %collective-permute-start.20 = (bf16[32,1,8,512]{3,2,1,0:T(8,128)(2,1)}, bf16[32,1,8,512]{3,2,1,0:T(8,128)(2,1)S(1)}, u32[]{:S(2)}, u32[]{:S(2)}) collective-permute-start(bf16[32,1,8,512]{3,2,1,0:T(8,128)(2,1)} %convolve.2.refs_0_), channel_id=1, source_target_pairs={{0,8},{1,9},{2,10},{3,11},{4,12},{5,13},{6,14},{7,15},{8,0},{9,1},... | collective-permute-start | bytes 786440 | tf_op jit(solution)/shard_map/ppermute | solution.py:29
  71.2 11.3 %collective-permute-start.14 = (bf16[32,1,8,512]{3,2,1,0:T(8,128)(2,1)}, bf16[32,1,8,512]{3,2,1,0:T(8,128)(2,1)S(1)}, u32[]{:S(2)}, u32[]{:S(2)}) collective-permute-start(bf16[32,1,8,512]{3,2,1,0:T(8,128)(2,1)} %convolve.2.refs_0_), channel_id=1, source_target_pairs={{0,2},{1,3},{2,0},{3,1},{4,6},{5,7},{6,4},{7,5},{8,10},{9,11},{10,... | collective-permute-start | bytes 786440 | tf_op jit(solution)/shard_map/ppermute | solution.py:29
  80.0 7.2 %collective-permute-start.18 = (bf16[32,1,8,512]{3,2,1,0:T(8,128)(2,1)S(1)}, bf16[32,1,8,512]{3,2,1,0:T(8,128)(2,1)S(1)}, u32[]{:S(2)}, u32[]{:S(2)}) collective-permute-start(bf16[32,1,8,512]{3,2,1,0:T(8,128)(2,1)S(1)} %collective-permute-done.16.refs_4_), channel_id=1, source_target_pairs={{0,2},{1,3},{2,0},{3,1},{4,6},{5,7},{6,4},{7,5},{8,10},{9,11},{10,... | collective-permute-start | bytes 786440 | tf_op jit(solution)/shard_map/ppermute | solution.py:29
  82.0 6.4 %collective-permute-start.24 = (bf16[32,1,8,512]{3,2,1,0:T(8,128)(2,1)S(1)}, bf16[32,1,8,512]{3,2,1,0:T(8,128)(2,1)S(1)}, u32[]{:S(2)}, u32[]{:S(2)}) collective-permute-start(bf16[32,1,8,512]{3,2,1,0:T(8,128)(2,1)S(1)} %collective-permute-done.20.refs_8_), channel_id=1, source_target_pairs={{0,4},{1,5},{2,6},{3,7},{4,0},{5,1},{6,2},{7,3},{8,12},{9,13},{10,... | collective-permute-start | bytes 786440 | tf_op jit(solution)/shard_map/ppermute | solution.py:29
  82.0 8.4 %collective-permute-start.13 = (bf16[32,1,8,512]{3,2,1,0:T(8,128)(2,1)}, bf16[32,1,8,512]{3,2,1,0:T(8,128)(2,1)S(1)}, u32[]{:S(2)}, u32[]{:S(2)}) collective-permute-start(bf16[32,1,8,512]{3,2,1,0:T(8,128)(2,1)} %convolve.2.refs_0_), channel_id=1, source_target_pairs={{0,1},{1,0},{2,3},{3,2},{4,5},{5,4},{6,7},{7,6},{8,9},{9,8},{10,11... | collective-permute-start | bytes 786440 | tf_op jit(solution)/shard_map/ppermute | solution.py:29
  82.0 8.4 %collective-permute-start.17 = (bf16[32,1,8,512]{3,2,1,0:T(8,128)(2,1)S(1)}, bf16[32,1,8,512]{3,2,1,0:T(8,128)(2,1)S(1)}, u32[]{:S(2)}, u32[]{:S(2)}) collective-permute-start(bf16[32,1,8,512]{3,2,1,0:T(8,128)(2,1)S(1)} %collective-permute-done.16.refs_4_), channel_id=1, source_target_pairs={{0,1},{1,0},{2,3},{3,2},{4,5},{5,4},{6,7},{7,6},{8,9},{9,8},{10,11... | collective-permute-start | bytes 786440 | tf_op jit(solution)/shard_map/ppermute | solution.py:29
  82.5 10.0 %collective-permute-start.15 = (bf16[32,1,8,512]{3,2,1,0:T(8,128)(2,1)S(1)}, bf16[32,1,8,512]{3,2,1,0:T(8,128)(2,1)S(1)}, u32[]{:S(2)}, u32[]{:S(2)}) collective-permute-start(bf16[32,1,8,512]{3,2,1,0:T(8,128)(2,1)S(1)} %collective-permute-done.14.refs_2_), channel_id=1, source_target_pairs={{0,1},{1,0},{2,3},{3,2},{4,5},{5,4},{6,7},{7,6},{8,9},{9,8},{10,11... | collective-permute-start | bytes 786440 | tf_op jit(solution)/shard_map/ppermute | solution.py:29
  88.3 11.2 %collective-permute-start.26 = (bf16[32,1,8,512]{3,2,1,0:T(8,128)(2,1)S(1)}, bf16[32,1,8,512]{3,2,1,0:T(8,128)(2,1)S(1)}, u32[]{:S(2)}, u32[]{:S(2)}) collective-permute-start(bf16[32,1,8,512]{3,2,1,0:T(8,128)(2,1)S(1)} %collective-permute-done.24.refs_12_), channel_id=1, source_target_pairs={{0,2},{1,3},{2,0},{3,1},{4,6},{5,7},{6,4},{7,5},{8,10},{9,11},{10,... | collective-permute-start | bytes 786440 | tf_op jit(solution)/shard_map/ppermute | solution.py:29
  89.0 11.0 %collective-permute-start.22 = (bf16[32,1,8,512]{3,2,1,0:T(8,128)(2,1)S(1)}, bf16[32,1,8,512]{3,2,1,0:T(8,128)(2,1)S(1)}, u32[]{:S(2)}, u32[]{:S(2)}) collective-permute-start(bf16[32,1,8,512]{3,2,1,0:T(8,128)(2,1)S(1)} %collective-permute-done.20.refs_8_), channel_id=1, source_target_pairs={{0,2},{1,3},{2,0},{3,1},{4,6},{5,7},{6,4},{7,5},{8,10},{9,11},{10,... | collective-permute-start | bytes 786440 | tf_op jit(solution)/shard_map/ppermute | solution.py:29
  90.4 9.7 %collective-permute-start.25 = (bf16[32,1,8,512]{3,2,1,0:T(8,128)(2,1)S(1)}, bf16[32,1,8,512]{3,2,1,0:T(8,128)(2,1)S(1)}, u32[]{:S(2)}, u32[]{:S(2)}) collective-permute-start(bf16[32,1,8,512]{3,2,1,0:T(8,128)(2,1)S(1)} %collective-permute-done.24.refs_12_), channel_id=1, source_target_pairs={{0,1},{1,0},{2,3},{3,2},{4,5},{5,4},{6,7},{7,6},{8,9},{9,8},{10,11... | collective-permute-start | bytes 786440 | tf_op jit(solution)/shard_map/ppermute | solution.py:29
  90.4 5.5 %collective-permute-start.30 = (s32[8,128]{1,0:T(8,128)S(1)}, s32[8,128]{1,0:T(8,128)S(1)}, u32[]{:S(2)}, u32[]{:S(2)}) collective-permute-start(s32[8,128]{1,0:T(8,128)S(1)} %bitcast.49), channel_id=1, source_target_pairs={{0,12},{1,13},{2,14},{3,15},{4,8},{5,9},{6,10},{7,11},{8,4},{9,5},... | collective-permute-start | bytes 12296 | tf_op jit(solution)/shard_map/ppermute | solution.py:29
  92.5 4.5 %collective-permute-start.29 = (s32[8,128]{1,0:T(8,128)S(1)}, s32[8,128]{1,0:T(8,128)S(1)}, u32[]{:S(2)}, u32[]{:S(2)}) collective-permute-start(s32[8,128]{1,0:T(8,128)S(1)} %bitcast.50), channel_id=1, source_target_pairs={{0,8},{1,9},{2,10},{3,11},{4,12},{5,13},{6,14},{7,15},{8,0},{9,1},... | collective-permute-start | bytes 12296 | tf_op jit(solution)/shard_map/ppermute | solution.py:29
  95.9 3.6 %collective-permute-start.28 = (s32[8,128]{1,0:T(8,128)S(1)}, s32[8,128]{1,0:T(8,128)S(1)}, u32[]{:S(2)}, u32[]{:S(2)}) collective-permute-start(s32[8,128]{1,0:T(8,128)S(1)} %bitcast.51), channel_id=1, source_target_pairs={{0,4},{1,5},{2,6},{3,7},{4,0},{5,1},{6,2},{7,3},{8,12},{9,13},{10,... | collective-permute-start | bytes 12296 | tf_op jit(solution)/shard_map/ppermute | solution.py:29
  97.0 3.8 %collective-permute-start.21 = (bf16[32,1,8,512]{3,2,1,0:T(8,128)(2,1)S(1)}, bf16[32,1,8,512]{3,2,1,0:T(8,128)(2,1)S(1)}, u32[]{:S(2)}, u32[]{:S(2)}) collective-permute-start(bf16[32,1,8,512]{3,2,1,0:T(8,128)(2,1)S(1)} %collective-permute-done.20.refs_8_), channel_id=1, source_target_pairs={{0,1},{1,0},{2,3},{3,2},{4,5},{5,4},{6,7},{7,6},{8,9},{9,8},{10,11... | collective-permute-start | bytes 786440 | tf_op jit(solution)/shard_map/ppermute | solution.py:29
  99.5 1.5 collective-permute-start.19
  99.5 1.9 %collective-permute-start.27 = (bf16[32,1,8,512]{3,2,1,0:T(8,128)(2,1)S(1)}, bf16[32,1,8,512]{3,2,1,0:T(8,128)(2,1)S(1)}, u32[]{:S(2)}, u32[]{:S(2)}) collective-permute-start(bf16[32,1,8,512]{3,2,1,0:T(8,128)(2,1)S(1)} %collective-permute-done.26.refs_14_), channel_id=1, source_target_pairs={{0,1},{1,0},{2,3},{3,2},{4,5},{5,4},{6,7},{7,6},{8,9},{9,8},{10,11... | collective-permute-start | bytes 786440 | tf_op jit(solution)/shard_map/ppermute | solution.py:29
  100.0 1.8 %collective-permute-start.23 = (bf16[32,1,8,512]{3,2,1,0:T(8,128)(2,1)S(1)}, bf16[32,1,8,512]{3,2,1,0:T(8,128)(2,1)S(1)}, u32[]{:S(2)}, u32[]{:S(2)}) collective-permute-start(bf16[32,1,8,512]{3,2,1,0:T(8,128)(2,1)S(1)} %collective-permute-done.22.refs_10_), channel_id=1, source_target_pairs={{0,1},{1,0},{2,3},{3,2},{4,5},{5,4},{6,7},{7,6},{8,9},{9,8},{10,11... | collective-permute-start | bytes 786440 | tf_op jit(solution)/shard_map/ppermute | solution.py:29
  100.1 10.0 %collective-permute-start.31 = (s32[4,8,128]{2,1,0:T(8,128)S(1)}, s32[4,8,128]{2,1,0:T(8,128)S(1)}, u32[]{:S(2)}, u32[]{:S(2)}) collective-permute-start(s32[4,8,128]{2,1,0:T(8,128)S(1)} %get-tuple-element.43), channel_id=1, source_target_pairs={{0,2},{1,3},{2,0},{3,1},{4,6},{5,7},{6,4},{7,5},{8,10},{9,11},{10,... | collective-permute-start | bytes 49160 | tf_op jit(solution)/shard_map/ppermute | solution.py:29
  106.3 13.6 %all-to-all-start = ((bf16[16,2,8,512]{3,2,1,0:T(8,128)(2,1)}), bf16[16,2,8,512]{3,2,1,0:T(8,128)(2,1)S(1)}, u32[]{:S(2)}, u32[]{:S(2)}) async-start(bf16[16,2,8,512]{3,2,1,0:T(8,128)(2,1)} %window_columns.1), calls=%async_computation | async-start | bytes 524288 | tf_op jit(solution)/shard_map/all_to_all | solution.py:409
  110.1 1.3 collective-permute-start.32
  125.6 13.3 %collective-permute-start.36 = (bf16[32,1,8,512]{3,2,1,0:T(8,128)(2,1)}, bf16[32,1,8,512]{3,2,1,0:T(8,128)(2,1)S(1)}, u32[]{:S(2)}, u32[]{:S(2)}) collective-permute-start(bf16[32,1,8,512]{3,2,1,0:T(8,128)(2,1)} %convolve.3.refs_0_), channel_id=1, source_target_pairs={{0,4},{1,5},{2,6},{3,7},{4,0},{5,1},{6,2},{7,3},{8,12},{9,13},{10,... | collective-permute-start | bytes 786440 | tf_op jit(solution)/shard_map/ppermute | solution.py:29
  125.8 15.2 %collective-permute-start.40 = (bf16[32,1,8,512]{3,2,1,0:T(8,128)(2,1)}, bf16[32,1,8,512]{3,2,1,0:T(8,128)(2,1)S(1)}, u32[]{:S(2)}, u32[]{:S(2)}) collective-permute-start(bf16[32,1,8,512]{3,2,1,0:T(8,128)(2,1)} %convolve.3.refs_0_), channel_id=1, source_target_pairs={{0,8},{1,9},{2,10},{3,11},{4,12},{5,13},{6,14},{7,15},{8,0},{9,1},... | collective-permute-start | bytes 786440 | tf_op jit(solution)/shard_map/ppermute | solution.py:29
  128.2 13.4 %collective-permute-start.34 = (bf16[32,1,8,512]{3,2,1,0:T(8,128)(2,1)}, bf16[32,1,8,512]{3,2,1,0:T(8,128)(2,1)S(1)}, u32[]{:S(2)}, u32[]{:S(2)}) collective-permute-start(bf16[32,1,8,512]{3,2,1,0:T(8,128)(2,1)} %convolve.3.refs_0_), channel_id=1, source_target_pairs={{0,2},{1,3},{2,0},{3,1},{4,6},{5,7},{6,4},{7,5},{8,10},{9,11},{10,... | collective-permute-start | bytes 786440 | tf_op jit(solution)/shard_map/ppermute | solution.py:29
  138.9 7.2 %collective-permute-start.38 = (bf16[32,1,8,512]{3,2,1,0:T(8,128)(2,1)S(1)}, bf16[32,1,8,512]{3,2,1,0:T(8,128)(2,1)S(1)}, u32[]{:S(2)}, u32[]{:S(2)}) collective-permute-start(bf16[32,1,8,512]{3,2,1,0:T(8,128)(2,1)S(1)} %collective-permute-done.36.refs_4_), channel_id=1, source_target_pairs={{0,2},{1,3},{2,0},{3,1},{4,6},{5,7},{6,4},{7,5},{8,10},{9,11},{10,... | collective-permute-start | bytes 786440 | tf_op jit(solution)/shard_map/ppermute | solution.py:29
  141.0 6.4 %collective-permute-start.44 = (bf16[32,1,8,512]{3,2,1,0:T(8,128)(2,1)S(1)}, bf16[32,1,8,512]{3,2,1,0:T(8,128)(2,1)S(1)}, u32[]{:S(2)}, u32[]{:S(2)}) collective-permute-start(bf16[32,1,8,512]{3,2,1,0:T(8,128)(2,1)S(1)} %collective-permute-done.40.refs_8_), channel_id=1, source_target_pairs={{0,4},{1,5},{2,6},{3,7},{4,0},{5,1},{6,2},{7,3},{8,12},{9,13},{10,... | collective-permute-start | bytes 786440 | tf_op jit(solution)/shard_map/ppermute | solution.py:29
  141.0 8.4 %collective-permute-start.33 = (bf16[32,1,8,512]{3,2,1,0:T(8,128)(2,1)}, bf16[32,1,8,512]{3,2,1,0:T(8,128)(2,1)S(1)}, u32[]{:S(2)}, u32[]{:S(2)}) collective-permute-start(bf16[32,1,8,512]{3,2,1,0:T(8,128)(2,1)} %convolve.3.refs_0_), channel_id=1, source_target_pairs={{0,1},{1,0},{2,3},{3,2},{4,5},{5,4},{6,7},{7,6},{8,9},{9,8},{10,11... | collective-permute-start | bytes 786440 | tf_op jit(solution)/shard_map/ppermute | solution.py:29
  141.0 8.4 %collective-permute-start.37 = (bf16[32,1,8,512]{3,2,1,0:T(8,128)(2,1)S(1)}, bf16[32,1,8,512]{3,2,1,0:T(8,128)(2,1)S(1)}, u32[]{:S(2)}, u32[]{:S(2)}) collective-permute-start(bf16[32,1,8,512]{3,2,1,0:T(8,128)(2,1)S(1)} %collective-permute-done.36.refs_4_), channel_id=1, source_target_pairs={{0,1},{1,0},{2,3},{3,2},{4,5},{5,4},{6,7},{7,6},{8,9},{9,8},{10,11... | collective-permute-start | bytes 786440 | tf_op jit(solution)/shard_map/ppermute | solution.py:29
  141.5 8.4 %collective-permute-start.35 = (bf16[32,1,8,512]{3,2,1,0:T(8,128)(2,1)S(1)}, bf16[32,1,8,512]{3,2,1,0:T(8,128)(2,1)S(1)}, u32[]{:S(2)}, u32[]{:S(2)}) collective-permute-start(bf16[32,1,8,512]{3,2,1,0:T(8,128)(2,1)S(1)} %collective-permute-done.34.refs_2_), channel_id=1, source_target_pairs={{0,1},{1,0},{2,3},{3,2},{4,5},{5,4},{6,7},{7,6},{8,9},{9,8},{10,11... | collective-permute-start | bytes 786440 | tf_op jit(solution)/shard_map/ppermute | solution.py:29
  147.4 8.3 %collective-permute-start.46 = (bf16[32,1,8,512]{3,2,1,0:T(8,128)(2,1)S(1)}, bf16[32,1,8,512]{3,2,1,0:T(8,128)(2,1)S(1)}, u32[]{:S(2)}, u32[]{:S(2)}) collective-permute-start(bf16[32,1,8,512]{3,2,1,0:T(8,128)(2,1)S(1)} %collective-permute-done.44.refs_12_), channel_id=1, source_target_pairs={{0,2},{1,3},{2,0},{3,1},{4,6},{5,7},{6,4},{7,5},{8,10},{9,11},{10,... | collective-permute-start | bytes 786440 | tf_op jit(solution)/shard_map/ppermute | solution.py:29
  148.5 10.0 %collective-permute-start.42 = (bf16[32,1,8,512]{3,2,1,0:T(8,128)(2,1)S(1)}, bf16[32,1,8,512]{3,2,1,0:T(8,128)(2,1)S(1)}, u32[]{:S(2)}, u32[]{:S(2)}) collective-permute-start(bf16[32,1,8,512]{3,2,1,0:T(8,128)(2,1)S(1)} %collective-permute-done.40.refs_8_), channel_id=1, source_target_pairs={{0,2},{1,3},{2,0},{3,1},{4,6},{5,7},{6,4},{7,5},{8,10},{9,11},{10,... | collective-permute-start | bytes 786440 | tf_op jit(solution)/shard_map/ppermute | solution.py:29
  149.4 9.1 %collective-permute-start.41 = (bf16[32,1,8,512]{3,2,1,0:T(8,128)(2,1)S(1)}, bf16[32,1,8,512]{3,2,1,0:T(8,128)(2,1)S(1)}, u32[]{:S(2)}, u32[]{:S(2)}) collective-permute-start(bf16[32,1,8,512]{3,2,1,0:T(8,128)(2,1)S(1)} %collective-permute-done.40.refs_8_), channel_id=1, source_target_pairs={{0,1},{1,0},{2,3},{3,2},{4,5},{5,4},{6,7},{7,6},{8,9},{9,8},{10,11... | collective-permute-start | bytes 786440 | tf_op jit(solution)/shard_map/ppermute | solution.py:29
  149.4 9.1 %collective-permute-start.45 = (bf16[32,1,8,512]{3,2,1,0:T(8,128)(2,1)S(1)}, bf16[32,1,8,512]{3,2,1,0:T(8,128)(2,1)S(1)}, u32[]{:S(2)}, u32[]{:S(2)}) collective-permute-start(bf16[32,1,8,512]{3,2,1,0:T(8,128)(2,1)S(1)} %collective-permute-done.44.refs_12_), channel_id=1, source_target_pairs={{0,1},{1,0},{2,3},{3,2},{4,5},{5,4},{6,7},{7,6},{8,9},{9,8},{10,11... | collective-permute-start | bytes 786440 | tf_op jit(solution)/shard_map/ppermute | solution.py:29
  149.9 8.6 %collective-permute-start.39 = (bf16[32,1,8,512]{3,2,1,0:T(8,128)(2,1)S(1)}, bf16[32,1,8,512]{3,2,1,0:T(8,128)(2,1)S(1)}, u32[]{:S(2)}, u32[]{:S(2)}) collective-permute-start(bf16[32,1,8,512]{3,2,1,0:T(8,128)(2,1)S(1)} %collective-permute-done.38.refs_6_), channel_id=1, source_target_pairs={{0,1},{1,0},{2,3},{3,2},{4,5},{5,4},{6,7},{7,6},{8,9},{9,8},{10,11... | collective-permute-start | bytes 786440 | tf_op jit(solution)/shard_map/ppermute | solution.py:29
  155.7 2.9 %collective-permute-start.47 = (bf16[32,1,8,512]{3,2,1,0:T(8,128)(2,1)S(1)}, bf16[32,1,8,512]{3,2,1,0:T(8,128)(2,1)S(1)}, u32[]{:S(2)}, u32[]{:S(2)}) collective-permute-start(bf16[32,1,8,512]{3,2,1,0:T(8,128)(2,1)S(1)} %collective-permute-done.46.refs_14_), channel_id=1, source_target_pairs={{0,1},{1,0},{2,3},{3,2},{4,5},{5,4},{6,7},{7,6},{8,9},{9,8},{10,11... | collective-permute-start | bytes 786440 | tf_op jit(solution)/shard_map/ppermute | solution.py:29
  158.5 1.5 collective-permute-start.43
  (38 other events, 367.1 us)

commit v3 on v2

--- a/solution.py
+++ b/solution.py
@@ -10,6 +10,8 @@
 
 ONSET_TOP = 767
 VMEM_LIMIT = 56 << 20
+SB = 256
+FB = 2
 
 
 def pitch(v):
@@ -63,7 +65,7 @@
     v //= chunks
     ndest = rows // rb
     c = s // nq
-    vb = 4
+    vb = math.gcd(v, 16)
     steps = v // vb
 
     def kernel(tab_ref, own_ref, other_ref, *outs):
@@ -91,47 +93,49 @@
     v, nq, rb, c = parts[0].shape
     nf, _, r, s = refl.shape
     nparts = len(parts)
+    fb = math.gcd(nf, FB)
 
     def kernel(*refs):
         part_refs = refs[:nparts]
-        scale_ref = None if scale is None else refs[nparts]
-        refl_ref, out_ref, x_scr, y_scr = refs[-4:]
+        scale_ref, refl_ref, out_ref, x_scr, y_scr = refs[-5:]
         k = pl.program_id(0)
 
         @pl.when(k == 0)
         def _():
+            factors = jnp.concatenate([scale_ref[j // 2 : j // 2 + 1] for j in range(rb)], axis=0)
             for i in range(v):
                 for q in range(nq):
                     x = part_refs[0][i, q].astype(jnp.float32)
                     for ref in part_refs[1:]:
                         x = x + ref[i, q].astype(jnp.float32)
                     for b in range(c // 128):
-                        lanes = x[:, b * 128 : (b + 1) * 128]
                         at = q * (c // 128) + b
-                        if scale_ref is not None:
-                            block = at * 128 * scale.shape[1] // s
-                            lanes = lanes * scale_ref[:, block : block + 1]
-                        x_scr[at, pl.ds(i, rb, stride=pitch(v)), :] = lanes
-
-        real = pl.ds(pl.multiple_of(2 * k * pitch(v), 8), v)
-        imag = pl.ds((2 * k + 1) * pitch(v), v)
-        x = jnp.concatenate(
-            [
-                jnp.concatenate([x_scr[b, real, :], x_scr[b, imag, :]], axis=0)
-                for b in range(s // 128)
-            ],
-            axis=1,
-        ).astype(jnp.bfloat16)
-        dims = (((1,), (1,)), ((), ()))
-        a = lax.dot_general(x, refl_ref[0, 0], dims, preferred_element_type=jnp.float32)
-        b = lax.dot_general(x, refl_ref[0, 1], dims, preferred_element_type=jnp.float32)
-        yr = a[:v] - sign * b[v:]
-        yi = a[v:] + sign * b[:v]
-        for b in range(r // 128):
-            y_scr[b, real, :] = yr[:, b * 128 : (b + 1) * 128]
-            y_scr[b, imag, :] = yi[:, b * 128 : (b + 1) * 128]
-
-        @pl.when(k == nf - 1)
+                        block = at * 128 * scale.shape[1] // s
+                        x_scr[at, pl.ds(i, rb, stride=pitch(v)), :] = (
+                            x[:, b * 128 : (b + 1) * 128] * factors[:, block : block + 1]
+                        )
+
+        for j in range(fb):
+            f = k * fb + j
+            real = pl.ds(pl.multiple_of(2 * f * pitch(v), 8), v)
+            imag = pl.ds((2 * f + 1) * pitch(v), v)
+            x = jnp.concatenate(
+                [
+                    jnp.concatenate([x_scr[b, real, :], x_scr[b, imag, :]], axis=0)
+                    for b in range(s // 128)
+                ],
+                axis=1,
+            ).astype(jnp.bfloat16)
+            dims = (((1,), (1,)), ((), ()))
+            a = lax.dot_general(x, refl_ref[j, 0], dims, preferred_element_type=jnp.float32)
+            b = lax.dot_general(x, refl_ref[j, 1], dims, preferred_element_type=jnp.float32)
+            yr = a[:v] - sign * b[v:]
+            yi = a[v:] + sign * b[:v]
+            for b in range(r // 128):
+                y_scr[b, real, :] = yr[:, b * 128 : (b + 1) * 128]
+                y_scr[b, imag, :] = yi[:, b * 128 : (b + 1) * 128]
+
+        @pl.when(k == nf // fb - 1)
         def _():
             for i in range(v):
                 for q in range(nq):
@@ -140,16 +144,13 @@
                         out_ref[i, q, :, b * 128 : (b + 1) * 128] = y.astype(jnp.bfloat16)
 
     whole = pl.BlockSpec((v, nq, rb, c), lambda k: (0, 0, 0, 0))
-    args = list(parts)
+    args = list(parts) + [scale, refl]
     specs = [whole] * nparts
-    if scale is not None:
-        args.append(scale)
-        specs.append(pl.BlockSpec(scale.shape, lambda k: (0, 0)))
-    args.append(refl)
-    specs.append(pl.BlockSpec((1, 2, r, s), lambda k: (k, 0, 0, 0)))
+    specs.append(pl.BlockSpec(scale.shape, lambda k: (0, 0)))
+    specs.append(pl.BlockSpec((fb, 2, r, s), lambda k: (k, 0, 0, 0)))
     return pl.pallas_call(
         kernel,
-        grid=(nf,),
+        grid=(nf // fb,),
         in_specs=specs,
         out_specs=whole,
         out_shape=jax.ShapeDtypeStruct((v, nq, rb, c), jnp.bfloat16),
@@ -224,7 +225,8 @@
     npieces = len(pieces)
     t = table.shape[0]
     s = nq * c
-    sb = 128
+    sb = min(SB, c)
+    per = c // sb
     vb = 2 if v % 2 == 0 else 1
     tb = 8
 
@@ -247,19 +249,21 @@
             for j in range(vb):
                 kept = absq < onset_ref[i + j : i + j + 1, :]
                 y = jnp.where(kept, res[:, j * sb : (j + 1) * sb], 0.0)
-                scr[pl.ds(i + j, t, stride=pitch(v)), :] = y
+                for b in range(sb // 128):
+                    scr[b, pl.ds(i + j, t, stride=pitch(v)), :] = y[:, b * 128 : (b + 1) * 128]
 
         @pl.loop(0, t // tb)
         def _(k):
             for j in range(tb):
                 at = k * tb + j
-                y = scr[pl.ds(at * pitch(v), v), :].astype(jnp.bfloat16)
+                y = jnp.concatenate(
+                    [scr[b, pl.ds(at * pitch(v), v), :] for b in range(sb // 128)], axis=1
+                ).astype(jnp.bfloat16)
                 if direct_ref is None:
                     out_ref[at] = y
                 else:
                     out_ref[at] = direct_ref[at].astype(jnp.float32) + y.astype(jnp.float32)
 
-    per = c // sb
     piece_spec = pl.BlockSpec((v, 1, rb, sb), lambda i: (0, i // per, 0, i % per))
     field_spec = pl.BlockSpec((t, v, sb), lambda i: (0, g, i))
     args = list(pieces) + [table, first, onset]
@@ -283,7 +287,7 @@
         in_specs=specs,
         out_specs=field_spec,
         out_shape=jax.ShapeDtypeStruct((t, onset.shape[0], s), dtype),
-        scratch_shapes=[pltpu.VMEM((t * pitch(v), sb), jnp.float32)],
+        scratch_shapes=[pltpu.VMEM((sb // 128, t * pitch(v), 128), jnp.float32)],
         input_output_aliases=aliases,
         compiler_params=params(),
         name="time_block",
@@ -319,7 +323,6 @@
     mine = points_major(fd_plus)
     theirs = points_major(raw)
     even = across(after(along(freq_index), mine, theirs))
-    scale_own = jnp.repeat(refl_scale, 2, axis=0)
 
     ri = jnp.arange(2, dtype=jnp.int32) * quarter
     def bin_rows(b):
@@ -402,7 +405,7 @@
     ).astype(jnp.bfloat16)
 
     held[0] = after(held[0], table_cols, table_time)
-    y1 = convolve(held, scale_own, refl, 1.0)
+    y1 = convolve(held, refl_scale, refl, 1.0)
     pieces, far = gather(y1)
     onset_own = onset.reshape(-1, 1, 1, c)
     x2 = window_columns(pieces, me, table_cols, onset_own, 2.0 / ntime)
@@ -414,7 +417,7 @@
     onset_all = onset_all.reshape(v, nrec)
     minus = time_block(pieces, table_time, first_own, onset_all, None, ntime, 0, None)
     x2 = after(x2, minus).reshape(v, nq, rb, c)
-    y2 = convolve([x2], scale_own, refl, -1.0)
+    y2 = convolve([x2], refl_scale, refl, -1.0)
     pieces, _ = gather(y2)
     plus = time_block(pieces, table_time, first_own, onset_all, fd_plus, ntime, 0, None)
     return minus, plus

time: 171 us -> 167 us (0.977)
  Pallas kernels: 46.6 us -> 39.6 us
  waiting for transfers between devices: 69.8 us -> 74.7 us
    ppermute x48, waiting for transfers between devices: 68.2 us -> 72.1 us  [swap(): return lax.ppermute(x, 'freq', [(i, i ^ stride) for i in range(n)])]
    pallas_call x2, Pallas kernels: 14.6 us -> 12.1 us  [time_block(): pl.pallas_call(kernel, grid=(s // sb,), in_specs=specs, out_specs=field_s...]
    pallas_call x1, Pallas kernels: 7.83 us -> 5.35 us  [partial_spectra(): pl.pallas_call(kernel, grid=(steps,), in_specs=[pl.BlockSpec((rows, 2 * t...]
    pallas_call x2, Pallas kernels: 10.1 us -> 8.18 us  [convolve(): pl.pallas_call(kernel, grid=(nf // fb,), in_specs=specs, out_specs=whole,...]
    unnamed x75 -> x73, local copies, waits for them, and re-layouts: 2.21 us -> 3.51 us
  transfers between devices with their start and end apart: 49 -> 49, of which waited for: 24 -> 24; matrix products, arithmetic and copies ran while one was open for 5% -> 5% of each run, Pallas kernels for 9% -> 8%
where the time goes in v3:
time: 167 us
  waiting for transfers between devices  74.7 us (45%)
  Pallas kernels  39.6 us (24%)
  starting transfers between devices  38.5 us (23%)
  other arithmetic  7.62 us (5%)
  local copies, waits for them, and re-layouts  4.99 us (3%)
    ppermute x48, waiting for transfers between devices, swap(): return lax.ppermute(x, 'freq', [(i, i ^ stride) for i in range(n)])  72.1 us
    ppermute x48, starting transfers between devices, swap(): return lax.ppermute(x, 'freq', [(i, i ^ stride) for i in range(n)])  34.7 us
    pallas_call x2, Pallas kernels, time_block(): pl.pallas_call(kernel, grid=(s // sb,), in_specs=specs, out_specs=field_s...  12.1 us
    pallas_call x2, Pallas kernels, points_major(): pl.pallas_call(kernel, grid=(s // sb,), in_specs=[pl.BlockSpec((t, v, sb)...  10.2 us
    pallas_call x2, Pallas kernels, convolve(): pl.pallas_call(kernel, grid=(nf // fb,), in_specs=specs, out_specs=whole,...  8.18 us
    pallas_call x1, Pallas kernels, partial_spectra(): pl.pallas_call(kernel, grid=(steps,), in_specs=[pl.BlockSpec((rows, 2 * t...  5.35 us
    pallas_call x1, Pallas kernels, window_columns(): pl.pallas_call(kernel, grid_spec=pltpu.PrefetchScalarGridSpec(num_scalar_...  3.87 us
    all_to_all x1, starting transfers between devices, local(): x2 = lax.all_to_all(x2, 'freq', split_axis=0, concat_axis=0, tiled=True)  3.73 us
  transfers between devices with their start and end apart: 49, of which 24 were waited for; matrix products, arithmetic and copies ran while one was open for 5% of the time, Pallas kernels for 8%

profile of v3, /device:TPU:0, one launch (start us, length us, event | category | flops | bytes accessed | tf_op | source)
XLA Modules:
  0.0 166.7 jit_solution(12359085499232388588)
XLA Ops:
  1.1 2.7 %collective-permute-start = (s32[4]{0:T(128)}, s32[4]{0:T(128)S(1)}, u32[]{:S(2)}, u32[]{:S(2)}) collective-permute-start(s32[4]{0:T(128)} %param.7), channel_id=1, source_target_pairs={{0,4},{1,5},{2,6},{3,7},{4,0},{5,1},{6,2},{7,3},{8,12},{9,13},{10,... | collective-permute-start | bytes 56 | tf_op jit(solution)/shard_map/ppermute | solution.py:31
  3.8 2.5 %collective-permute-start.2 = (s32[4]{0:T(128)}, s32[4]{0:T(128)S(1)}, u32[]{:S(2)}, u32[]{:S(2)}) collective-permute-start(s32[4]{0:T(128)} %param.7), channel_id=1, source_target_pairs={{0,12},{1,13},{2,14},{3,15},{4,8},{5,9},{6,10},{7,11},{8,4},{9,5},... | collective-permute-start | bytes 56 | tf_op jit(solution)/shard_map/ppermute | solution.py:31
  6.4 5.1 %points_major.2.own_ref = bf16[32,128,512]{2,1,0:T(8,128)(2,1)} custom-call(bf16[128,32,512]{2,1,0:T(8,128)(2,1)} %refs_19_.1), custom_call_target="tpu_custom_call" | custom-call | tf_op jit(solution)/shard_map/points_major/pallas_call | solution.py:50
  11.6 5.1 %points_major.3.other_ref = bf16[32,128,512]{2,1,0:T(8,128)(2,1)} custom-call(bf16[128,32,512]{2,1,0:T(8,128)(2,1)} %collective-permute-done.3.x_ref), custom_call_target="tpu_custom_call" | custom-call | tf_op jit(solution)/shard_map/points_major/pallas_call | solution.py:50
  16.6 1.5 collective-permute-start.4
  18.2 2.0 %collective-permute-done.4 = s32[4,4]{1,0:T(4,128)S(1)} collective-permute-done((s32[4,4]{1,0:T(4,128)S(1)}, s32[4,4]{1,0:T(4,128)S(1)}, u32[]{:S(2)}, u32[]{:S(2)}) %collective-permute-start.4) | collective-permute-done | bytes 96 | tf_op jit(solution)/shard_map/ppermute | solution.py:31
  21.5 5.4 %partial_spectra.1 = (bf16[32,1,8,512]{3,2,1,0:T(8,128)(2,1)}, bf16[32,1,8,512]{3,2,1,0:T(8,128)(2,1)}, bf16[32,1,8,512]{3,2,1,0:T(8,128)(2,1)}, bf16[32,1,8,512...) custom-call(bf16[64,256]{1,0:T(8,128)(2,1)} %fusion.9.tab_ref, ...), custom_call_target="tpu_custom_call" | custom-call | tf_op jit(solution)/shard_map/partial_spectra/pallas_call | solution.py:81
  26.8 1.5 collective-permute-start.6
  28.9 7.4 %collective-permute-done.6 = bf16[32,1,8,512]{3,2,1,0:T(8,128)(2,1)S(1)} collective-permute-done((bf16[32,1,8,512]{3,2,1,0:T(8,128)(2,1)}, bf16[32,1,8,512]{3,2,1,0:T(8,128)(2,1)S(1)}, u32[]{:S(2)}, u32[]{:S(2)}) %collective-permute-start.6) | collective-permute-done | bytes 262176 | tf_op jit(solution)/shard_map/ppermute | solution.py:31
  36.3 1.5 collective-permute-start.7
  37.8 1.0 add_convert_fusion.1
  38.8 1.9 %collective-permute-start.10 = (bf16[32,1,8,512]{3,2,1,0:T(8,128)(2,1)S(1)}, bf16[32,1,8,512]{3,2,1,0:T(8,128)(2,1)S(1)}, u32[]{:S(2)}, u32[]{:S(2)}) collective-permute-start(bf16[32,1,8,512]{3,2,1,0:T(8,128)(2,1)S(1)} %add_convert_fusion.1), channel_id=1, source_target_pairs={{0,4},{1,5},{2,6},{3,7},{4,0},{5,1},{6,2},{7,3},{8,12},{9,13},{10,... | collective-permute-start | bytes 786440 | tf_op jit(solution)/shard_map/ppermute | solution.py:31
  40.9 1.0 collective-permute-done.5
  41.9 1.5 collective-permute-start.9
  43.4 2.1 %collective-permute-done.7 = bf16[32,1,8,512]{3,2,1,0:T(8,128)(2,1)S(1)} collective-permute-done((bf16[32,1,8,512]{3,2,1,0:T(8,128)(2,1)}, bf16[32,1,8,512]{3,2,1,0:T(8,128)(2,1)S(1)}, u32[]{:S(2)}, u32[]{:S(2)}) %collective-permute-start.7) | collective-permute-done | bytes 262176 | tf_op jit(solution)/shard_map/ppermute | solution.py:31
  45.9 1.1 add_convert_fusion
  46.9 3.4 %collective-permute-start.12 = (bf16[32,1,8,512]{3,2,1,0:T(8,128)(2,1)S(1)}, bf16[32,1,8,512]{3,2,1,0:T(8,128)(2,1)S(1)}, u32[]{:S(2)}, u32[]{:S(2)}) collective-permute-start(bf16[32,1,8,512]{3,2,1,0:T(8,128)(2,1)S(1)} %add_convert_fusion), channel_id=1, source_target_pairs={{0,8},{1,9},{2,10},{3,11},{4,12},{5,13},{6,14},{7,15},{8,0},{9,1},... | collective-permute-start | bytes 786440 | tf_op jit(solution)/shard_map/ppermute | solution.py:31
  50.4 1.0 add_convert_fusion.2
  52.4 2.2 %fusion.4.refs_16_ = bf16[128,768]{1,0:T(8,128)(2,1)} fusion(s32[128]{0:T(128)S(1)} %add.84, s32[128]{0:T(128)S(1)} %mul.94), kind=kLoop, calls=%fused_computation.11 | loop fusion | flops 1572864 | bytes 197632 | tf_op jit(solution)/shard_map/convert_element_type | solution.py:405
  54.7 5.9 %collective-permute-done.11.refs_2_ = bf16[32,1,8,512]{3,2,1,0:T(8,128)(2,1)S(1)} collective-permute-done((bf16[32,1,8,512]{3,2,1,0:T(8,128)(2,1)S(1)}, bf16[32,1,8,512]{3,2,1,0:T(8,128)(2,1)S(1)}, u32[]{:S(2)}, u32[]{:S(2)}) %collective-permute-start.11) | collective-permute-done | bytes 262176 | tf_op jit(solution)/shard_map/ppermute | solution.py:31
  62.0 4.2 %convolve.2.refs_0_ = bf16[32,1,8,512]{3,2,1,0:T(8,128)(2,1)} custom-call(bf16[32,1,8,512]{3,2,1,0:T(8,128)(2,1)} %get-tuple-element.28.refs_0_, bf16[32,1,8,512]{3,2,1,0:T(8,128)(2,1)} %copy-done.31, bf16[32,1,8,512]{3,2,1,0:T(8,128)(2,1)} %copy-done.33, bf16[32,1,8,512]{3,2,1,0:T(8,128)(2,1)} %copy-done.32, f32[4,4]{1,0:T(4,128)} %refs_1_.1, ...), custom_call_target="tpu_custom_call" | custom-call | tf_op jit(solution)/shard_map/convolve/pallas_call | solution.py:151
  66.3 2.0 %collective-permute-start.20 = (bf16[32,1,8,512]{3,2,1,0:T(8,128)(2,1)}, bf16[32,1,8,512]{3,2,1,0:T(8,128)(2,1)S(1)}, u32[]{:S(2)}, u32[]{:S(2)}) collective-permute-start(bf16[32,1,8,512]{3,2,1,0:T(8,128)(2,1)} %convolve.2.refs_0_), channel_id=1, source_target_pairs={{0,8},{1,9},{2,10},{3,11},{4,12},{5,13},{6,14},{7,15},{8,0},{9,1},... | collective-permute-start | bytes 786440 | tf_op jit(solution)/shard_map/ppermute | solution.py:31
  68.3 1.8 %collective-permute-start.14 = (bf16[32,1,8,512]{3,2,1,0:T(8,128)(2,1)}, bf16[32,1,8,512]{3,2,1,0:T(8,128)(2,1)S(1)}, u32[]{:S(2)}, u32[]{:S(2)}) collective-permute-start(bf16[32,1,8,512]{3,2,1,0:T(8,128)(2,1)} %convolve.2.refs_0_), channel_id=1, source_target_pairs={{0,2},{1,3},{2,0},{3,1},{4,6},{5,7},{6,4},{7,5},{8,10},{9,11},{10,... | collective-permute-start | bytes 786440 | tf_op jit(solution)/shard_map/ppermute | solution.py:31
  70.1 6.4 %collective-permute-done.16.refs_4_ = bf16[32,1,8,512]{3,2,1,0:T(8,128)(2,1)S(1)} collective-permute-done((bf16[32,1,8,512]{3,2,1,0:T(8,128)(2,1)}, bf16[32,1,8,512]{3,2,1,0:T(8,128)(2,1)S(1)}, u32[]{:S(2)}, u32[]{:S(2)}) %collective-permute-start.16) | collective-permute-done | bytes 262176 | tf_op jit(solution)/shard_map/ppermute | solution.py:31
  77.0 1.6 collective-permute-done.20.refs_8_
  79.2 4.0 %collective-permute-done.18.refs_6_ = bf16[32,1,8,512]{3,2,1,0:T(8,128)(2,1)S(1)} collective-permute-done((bf16[32,1,8,512]{3,2,1,0:T(8,128)(2,1)S(1)}, bf16[32,1,8,512]{3,2,1,0:T(8,128)(2,1)S(1)}, u32[]{:S(2)}, u32[]{:S(2)}) %collective-permute-start.18) | collective-permute-done | bytes 262176 | tf_op jit(solution)/shard_map/ppermute | solution.py:31
  83.2 1.8 %collective-permute-done.24.refs_12_ = bf16[32,1,8,512]{3,2,1,0:T(8,128)(2,1)S(1)} collective-permute-done((bf16[32,1,8,512]{3,2,1,0:T(8,128)(2,1)S(1)}, bf16[32,1,8,512]{3,2,1,0:T(8,128)(2,1)S(1)}, u32[]{:S(2)}, u32[]{:S(2)}) %collective-permute-start.24) | collective-permute-done | bytes 262176 | tf_op jit(solution)/shard_map/ppermute | solution.py:31
  85.0 2.0 %collective-permute-start.22 = (bf16[32,1,8,512]{3,2,1,0:T(8,128)(2,1)S(1)}, bf16[32,1,8,512]{3,2,1,0:T(8,128)(2,1)S(1)}, u32[]{:S(2)}, u32[]{:S(2)}) collective-permute-start(bf16[32,1,8,512]{3,2,1,0:T(8,128)(2,1)S(1)} %collective-permute-done.20.refs_8_), channel_id=1, source_target_pairs={{0,2},{1,3},{2,0},{3,1},{4,6},{5,7},{6,4},{7,5},{8,10},{9,11},{10,... | collective-permute-start | bytes 786440 | tf_op jit(solution)/shard_map/ppermute | solution.py:31
  87.1 2.1 %collective-permute-start.30 = (s32[8,128]{1,0:T(8,128)S(1)}, s32[8,128]{1,0:T(8,128)S(1)}, u32[]{:S(2)}, u32[]{:S(2)}) collective-permute-start(s32[8,128]{1,0:T(8,128)S(1)} %bitcast.46), channel_id=1, source_target_pairs={{0,12},{1,13},{2,14},{3,15},{4,8},{5,9},{6,10},{7,11},{8,4},{9,5},... | collective-permute-start | bytes 12296 | tf_op jit(solution)/shard_map/ppermute | solution.py:31
  89.2 3.4 %collective-permute-done.30 = s32[8,128]{1,0:T(8,128)S(1)} collective-permute-done((s32[8,128]{1,0:T(8,128)S(1)}, s32[8,128]{1,0:T(8,128)S(1)}, u32[]{:S(2)}, u32[]{:S(2)}) %collective-permute-start.30) | collective-permute-done | bytes 4128 | tf_op jit(solution)/shard_map/ppermute | solution.py:31
  92.5 1.1 collective-permute-done.29
  93.7 2.5 %collective-permute-done.28 = s32[8,128]{1,0:T(8,128)S(1)} collective-permute-done((s32[8,128]{1,0:T(8,128)S(1)}, s32[8,128]{1,0:T(8,128)S(1)}, u32[]{:S(2)}, u32[]{:S(2)}) %collective-permute-start.28) | collective-permute-done | bytes 4128 | tf_op jit(solution)/shard_map/ppermute | solution.py:31
  99.1 3.9 %window_columns.1 = bf16[16,2,8,512]{3,2,1,0:T(8,128)(2,1)} custom-call(s32[1]{0:T(128)} %bitcast.21.me_ref, bf16[32,1,8,512]{3,2,1,0:T(8,128)(2,1)} %convolve.2.refs_0_, bf16[32,1,8,512]{3,2,1,0:T(8,128)(2,1)} %copy-done.5, bf16[32,1,8,512]{3,2,1,0:T(8,128)(2,1)} %copy-done.2, bf16[32,1,8,512]{3,2,1,0:T(8,128)(2,1)} %copy-done.7, ...), custom_call_target="tpu_custom_call" | custom-call | tf_op jit(solution)/shard_map/window_columns/pallas_call | solution.py:208
  103.0 3.7 %all-to-all-start = ((bf16[16,2,8,512]{3,2,1,0:T(8,128)(2,1)}), bf16[16,2,8,512]{3,2,1,0:T(8,128)(2,1)S(1)}, u32[]{:S(2)}, u32[]{:S(2)}) async-start(bf16[16,2,8,512]{3,2,1,0:T(8,128)(2,1)} %window_columns.1), calls=%async_computation | async-start | bytes 524288 | tf_op jit(solution)/shard_map/all_to_all | solution.py:412
  108.9 5.0 %time_block.2 = bf16[128,32,512]{2,1,0:T(8,128)(2,1)} custom-call(bf16[32,1,8,512]{3,2,1,0:T(8,128)(2,1)} %convolve.2.refs_0_, bf16[32,1,8,512]{3,2,1,0:T(8,128)(2,1)} %copy-done.5, bf16[32,1,8,512]{3,2,1,0:T(8,128)(2,1)} %copy-done.2, bf16[32,1,8,512]{3,2,1,0:T(8,128)(2,1)} %copy-done.7, bf16[32,1,8,512]{3,2,1,0:T(8,128)(2,1)} %copy-done, ...), custom_call_target="tpu_custom_call" | custom-call | tf_op jit(solution)/shard_map/time_block/pallas_call | solution.py:284
  114.0 2.6 %all-to-all-done = bf16[16,2,8,512]{3,2,1,0:T(8,128)(2,1)S(1)} async-done(((bf16[16,2,8,512]{3,2,1,0:T(8,128)(2,1)}), bf16[16,2,8,512]{3,2,1,0:T(8,128)(2,1)S(1)}, u32[]{:S(2)}, u32[]{:S(2)}) %all-to-all-start) | async-done | bytes 262176 | tf_op jit(solution)/shard_map/all_to_all | solution.py:412
  117.3 4.0 %convolve.3.refs_0_ = bf16[32,1,8,512]{3,2,1,0:T(8,128)(2,1)} custom-call(bf16[32,1,8,512]{3,2,1,0:T(8,128)(2,1)} %bitcast.37, f32[4,4]{1,0:T(4,128)} %refs_1_.1, bf16[4,2,512,512]{3,2,1,0:T(8,128)(2,1)} %refs_2_.1), custom_call_target="tpu_custom_call" | custom-call | tf_op jit(solution)/shard_map/convolve/pallas_call | solution.py:151
  121.3 1.5 collective-permute-start.40
  122.8 1.4 collective-permute-start.34
  124.2 9.7 %collective-permute-done.36.refs_4_ = bf16[32,1,8,512]{3,2,1,0:T(8,128)(2,1)S(1)} collective-permute-done((bf16[32,1,8,512]{3,2,1,0:T(8,128)(2,1)}, bf16[32,1,8,512]{3,2,1,0:T(8,128)(2,1)S(1)}, u32[]{:S(2)}, u32[]{:S(2)}) %collective-permute-start.36) | collective-permute-done | bytes 262176 | tf_op jit(solution)/shard_map/ppermute | solution.py:31
  134.7 2.1 %collective-permute-done.40.refs_8_ = bf16[32,1,8,512]{3,2,1,0:T(8,128)(2,1)S(1)} collective-permute-done((bf16[32,1,8,512]{3,2,1,0:T(8,128)(2,1)}, bf16[32,1,8,512]{3,2,1,0:T(8,128)(2,1)S(1)}, u32[]{:S(2)}, u32[]{:S(2)}) %collective-permute-start.40) | collective-permute-done | bytes 262176 | tf_op jit(solution)/shard_map/ppermute | solution.py:31
  137.3 4.1 %collective-permute-done.38.refs_6_ = bf16[32,1,8,512]{3,2,1,0:T(8,128)(2,1)S(1)} collective-permute-done((bf16[32,1,8,512]{3,2,1,0:T(8,128)(2,1)S(1)}, bf16[32,1,8,512]{3,2,1,0:T(8,128)(2,1)S(1)}, u32[]{:S(2)}, u32[]{:S(2)}) %collective-permute-start.38) | collective-permute-done | bytes 262176 | tf_op jit(solution)/shard_map/ppermute | solution.py:31
  141.4 3.2 %collective-permute-done.44.refs_12_ = bf16[32,1,8,512]{3,2,1,0:T(8,128)(2,1)S(1)} collective-permute-done((bf16[32,1,8,512]{3,2,1,0:T(8,128)(2,1)S(1)}, bf16[32,1,8,512]{3,2,1,0:T(8,128)(2,1)S(1)}, u32[]{:S(2)}, u32[]{:S(2)}) %collective-permute-start.44) | collective-permute-done | bytes 262176 | tf_op jit(solution)/shard_map/ppermute | solution.py:31
  144.6 2.0 %collective-permute-start.42 = (bf16[32,1,8,512]{3,2,1,0:T(8,128)(2,1)S(1)}, bf16[32,1,8,512]{3,2,1,0:T(8,128)(2,1)S(1)}, u32[]{:S(2)}, u32[]{:S(2)}) collective-permute-start(bf16[32,1,8,512]{3,2,1,0:T(8,128)(2,1)S(1)} %collective-permute-done.40.refs_8_), channel_id=1, source_target_pairs={{0,2},{1,3},{2,0},{3,1},{4,6},{5,7},{6,4},{7,5},{8,10},{9,11},{10,... | collective-permute-start | bytes 786440 | tf_op jit(solution)/shard_map/ppermute | solution.py:31
  147.2 6.6 %collective-permute-done.46.refs_14_ = bf16[32,1,8,512]{3,2,1,0:T(8,128)(2,1)S(1)} collective-permute-done((bf16[32,1,8,512]{3,2,1,0:T(8,128)(2,1)S(1)}, bf16[32,1,8,512]{3,2,1,0:T(8,128)(2,1)S(1)}, u32[]{:S(2)}, u32[]{:S(2)}) %collective-permute-start.46) | collective-permute-done | bytes 262176 | tf_op jit(solution)/shard_map/ppermute | solution.py:31
  153.8 3.3 %collective-permute-done.42.refs_10_ = bf16[32,1,8,512]{3,2,1,0:T(8,128)(2,1)S(1)} collective-permute-done((bf16[32,1,8,512]{3,2,1,0:T(8,128)(2,1)S(1)}, bf16[32,1,8,512]{3,2,1,0:T(8,128)(2,1)S(1)}, u32[]{:S(2)}, u32[]{:S(2)}) %collective-permute-start.42) | collective-permute-done | bytes 262176 | tf_op jit(solution)/shard_map/ppermute | solution.py:31
  157.2 1.5 collective-permute-done.43.refs_11_
  159.5 7.0 %time_block.3 = f32[128,32,512]{2,1,0:T(8,128)} custom-call(bf16[32,1,8,512]{3,2,1,0:T(8,128)(2,1)} %convolve.3.refs_0_, bf16[32,1,8,512]{3,2,1,0:T(8,128)(2,1)} %copy-done.21, bf16[32,1,8,512]{3,2,1,0:T(8,128)(2,1)} %copy-done.18, bf16[32,1,8,512]{3,2,1,0:T(8,128)(2,1)} %copy-done.23, bf16[32,1,8,512]{3,2,1,0:T(8,128)(2,1)} %copy-done.16, ...), custom_call_target="tpu_custom_call" | custom-call | tf_op jit(solution)/shard_map/time_block/pallas_call | solution.py:284
  (165 shorter events, 15.1 us)
Async XLA Ops:
  0.6 10.9 %collective-permute-start.3 = (bf16[128,32,512]{2,1,0:T(8,128)(2,1)}, bf16[128,32,512]{2,1,0:T(8,128)(2,1)}, u32[]{:S(2)}, u32[]{:S(2)}) collective-permute-start(bf16[128,32,512]{2,1,0:T(8,128)(2,1)} %refs_19_.1), channel_id=1, source_target_pairs={{0,1},{1,0},{2,3},{3,2},{4,5},{5,4},{6,7},{7,6},{8,9},{9,8},{10,11... | collective-permute-start | bytes 12582920 | tf_op jit(solution)/shard_map/ppermute | solution.py:31
  1.1 10.4 %collective-permute-start = (s32[4]{0:T(128)}, s32[4]{0:T(128)S(1)}, u32[]{:S(2)}, u32[]{:S(2)}) collective-permute-start(s32[4]{0:T(128)} %param.7), channel_id=1, source_target_pairs={{0,4},{1,5},{2,6},{3,7},{4,0},{5,1},{6,2},{7,3},{8,12},{9,13},{10,... | collective-permute-start | bytes 56 | tf_op jit(solution)/shard_map/ppermute | solution.py:31
  3.8 7.7 %collective-permute-start.2 = (s32[4]{0:T(128)}, s32[4]{0:T(128)S(1)}, u32[]{:S(2)}, u32[]{:S(2)}) collective-permute-start(s32[4]{0:T(128)} %param.7), channel_id=1, source_target_pairs={{0,12},{1,13},{2,14},{3,15},{4,8},{5,9},{6,10},{7,11},{8,4},{9,5},... | collective-permute-start | bytes 56 | tf_op jit(solution)/shard_map/ppermute | solution.py:31
  6.3 5.2 %collective-permute-start.1 = (s32[4]{0:T(128)}, s32[4]{0:T(128)S(1)}, u32[]{:S(2)}, u32[]{:S(2)}) collective-permute-start(s32[4]{0:T(128)} %param.7), channel_id=1, source_target_pairs={{0,8},{1,9},{2,10},{3,11},{4,12},{5,13},{6,14},{7,15},{8,0},{9,1},... | collective-permute-start | bytes 56 | tf_op jit(solution)/shard_map/ppermute | solution.py:31
  16.6 3.6 %collective-permute-start.4 = (s32[4,4]{1,0:T(4,128)S(1)}, s32[4,4]{1,0:T(4,128)S(1)}, u32[]{:S(2)}, u32[]{:S(2)}) collective-permute-start(s32[4,4]{1,0:T(4,128)S(1)} %pad_add_fusion.5), channel_id=1, source_target_pairs={{0,2},{1,3},{2,0},{3,1},{4,6},{5,7},{6,4},{7,5},{8,10},{9,11},{10,... | collective-permute-start | bytes 200 | tf_op jit(solution)/shard_map/ppermute | solution.py:31
  26.8 9.5 %collective-permute-start.6 = (bf16[32,1,8,512]{3,2,1,0:T(8,128)(2,1)}, bf16[32,1,8,512]{3,2,1,0:T(8,128)(2,1)S(1)}, u32[]{:S(2)}, u32[]{:S(2)}) collective-permute-start(bf16[32,1,8,512]{3,2,1,0:T(8,128)(2,1)} %get-tuple-element.25), channel_id=1, source_target_pairs={{0,2},{1,3},{2,0},{3,1},{4,6},{5,7},{6,4},{7,5},{8,10},{9,11},{10,... | collective-permute-start | bytes 786440 | tf_op jit(solution)/shard_map/ppermute | solution.py:31
  28.4 13.6 %collective-permute-start.8 = (bf16[32,1,8,512]{3,2,1,0:T(8,128)(2,1)}, bf16[32,1,8,512]{3,2,1,0:T(8,128)(2,1)S(1)}, u32[]{:S(2)}, u32[]{:S(2)}) collective-permute-start(bf16[32,1,8,512]{3,2,1,0:T(8,128)(2,1)} %get-tuple-element.30), channel_id=1, source_target_pairs={{0,2},{1,3},{2,0},{3,1},{4,6},{5,7},{6,4},{7,5},{8,10},{9,11},{10,... | collective-permute-start | bytes 786440 | tf_op jit(solution)/shard_map/ppermute | solution.py:31
  36.3 9.2 %collective-permute-start.7 = (bf16[32,1,8,512]{3,2,1,0:T(8,128)(2,1)}, bf16[32,1,8,512]{3,2,1,0:T(8,128)(2,1)S(1)}, u32[]{:S(2)}, u32[]{:S(2)}) collective-permute-start(bf16[32,1,8,512]{3,2,1,0:T(8,128)(2,1)} %get-tuple-element.26), channel_id=1, source_target_pairs={{0,2},{1,3},{2,0},{3,1},{4,6},{5,7},{6,4},{7,5},{8,10},{9,11},{10,... | collective-permute-start | bytes 786440 | tf_op jit(solution)/shard_map/ppermute | solution.py:31
  38.8 7.0 %collective-permute-start.10 = (bf16[32,1,8,512]{3,2,1,0:T(8,128)(2,1)S(1)}, bf16[32,1,8,512]{3,2,1,0:T(8,128)(2,1)S(1)}, u32[]{:S(2)}, u32[]{:S(2)}) collective-permute-start(bf16[32,1,8,512]{3,2,1,0:T(8,128)(2,1)S(1)} %add_convert_fusion.1), channel_id=1, source_target_pairs={{0,4},{1,5},{2,6},{3,7},{4,0},{5,1},{6,2},{7,3},{8,12},{9,13},{10,... | collective-permute-start | bytes 786440 | tf_op jit(solution)/shard_map/ppermute | solution.py:31
  41.9 12.7 %collective-permute-start.9 = (bf16[32,1,8,512]{3,2,1,0:T(8,128)(2,1)}, bf16[32,1,8,512]{3,2,1,0:T(8,128)(2,1)S(1)}, u32[]{:S(2)}, u32[]{:S(2)}) collective-permute-start(bf16[32,1,8,512]{3,2,1,0:T(8,128)(2,1)} %get-tuple-element.31), channel_id=1, source_target_pairs={{0,2},{1,3},{2,0},{3,1},{4,6},{5,7},{6,4},{7,5},{8,10},{9,11},{10,... | collective-permute-start | bytes 786440 | tf_op jit(solution)/shard_map/ppermute | solution.py:31
  46.9 13.7 %collective-permute-start.12 = (bf16[32,1,8,512]{3,2,1,0:T(8,128)(2,1)S(1)}, bf16[32,1,8,512]{3,2,1,0:T(8,128)(2,1)S(1)}, u32[]{:S(2)}, u32[]{:S(2)}) collective-permute-start(bf16[32,1,8,512]{3,2,1,0:T(8,128)(2,1)S(1)} %add_convert_fusion), channel_id=1, source_target_pairs={{0,8},{1,9},{2,10},{3,11},{4,12},{5,13},{6,14},{7,15},{8,0},{9,1},... | collective-permute-start | bytes 786440 | tf_op jit(solution)/shard_map/ppermute | solution.py:31
  51.4 9.2 %collective-permute-start.11 = (bf16[32,1,8,512]{3,2,1,0:T(8,128)(2,1)S(1)}, bf16[32,1,8,512]{3,2,1,0:T(8,128)(2,1)S(1)}, u32[]{:S(2)}, u32[]{:S(2)}) collective-permute-start(bf16[32,1,8,512]{3,2,1,0:T(8,128)(2,1)S(1)} %add_convert_fusion.2), channel_id=1, source_target_pairs={{0,4},{1,5},{2,6},{3,7},{4,0},{5,1},{6,2},{7,3},{8,12},{9,13},{10,... | collective-permute-start | bytes 786440 | tf_op jit(solution)/shard_map/ppermute | solution.py:31
  66.2 10.3 %collective-permute-start.16 = (bf16[32,1,8,512]{3,2,1,0:T(8,128)(2,1)}, bf16[32,1,8,512]{3,2,1,0:T(8,128)(2,1)S(1)}, u32[]{:S(2)}, u32[]{:S(2)}) collective-permute-start(bf16[32,1,8,512]{3,2,1,0:T(8,128)(2,1)} %convolve.2.refs_0_), channel_id=1, source_target_pairs={{0,4},{1,5},{2,6},{3,7},{4,0},{5,1},{6,2},{7,3},{8,12},{9,13},{10,... | collective-permute-start | bytes 786440 | tf_op jit(solution)/shard_map/ppermute | solution.py:31
  66.3 12.3 %collective-permute-start.20 = (bf16[32,1,8,512]{3,2,1,0:T(8,128)(2,1)}, bf16[32,1,8,512]{3,2,1,0:T(8,128)(2,1)S(1)}, u32[]{:S(2)}, u32[]{:S(2)}) collective-permute-start(bf16[32,1,8,512]{3,2,1,0:T(8,128)(2,1)} %convolve.2.refs_0_), channel_id=1, source_target_pairs={{0,8},{1,9},{2,10},{3,11},{4,12},{5,13},{6,14},{7,15},{8,0},{9,1},... | collective-permute-start | bytes 786440 | tf_op jit(solution)/shard_map/ppermute | solution.py:31
  68.3 10.8 %collective-permute-start.14 = (bf16[32,1,8,512]{3,2,1,0:T(8,128)(2,1)}, bf16[32,1,8,512]{3,2,1,0:T(8,128)(2,1)S(1)}, u32[]{:S(2)}, u32[]{:S(2)}) collective-permute-start(bf16[32,1,8,512]{3,2,1,0:T(8,128)(2,1)} %convolve.2.refs_0_), channel_id=1, source_target_pairs={{0,2},{1,3},{2,0},{3,1},{4,6},{5,7},{6,4},{7,5},{8,10},{9,11},{10,... | collective-permute-start | bytes 786440 | tf_op jit(solution)/shard_map/ppermute | solution.py:31
  76.5 6.6 %collective-permute-start.18 = (bf16[32,1,8,512]{3,2,1,0:T(8,128)(2,1)S(1)}, bf16[32,1,8,512]{3,2,1,0:T(8,128)(2,1)S(1)}, u32[]{:S(2)}, u32[]{:S(2)}) collective-permute-start(bf16[32,1,8,512]{3,2,1,0:T(8,128)(2,1)S(1)} %collective-permute-done.16.refs_4_), channel_id=1, source_target_pairs={{0,2},{1,3},{2,0},{3,1},{4,6},{5,7},{6,4},{7,5},{8,10},{9,11},{10,... | collective-permute-start | bytes 786440 | tf_op jit(solution)/shard_map/ppermute | solution.py:31
  78.6 6.4 %collective-permute-start.24 = (bf16[32,1,8,512]{3,2,1,0:T(8,128)(2,1)S(1)}, bf16[32,1,8,512]{3,2,1,0:T(8,128)(2,1)S(1)}, u32[]{:S(2)}, u32[]{:S(2)}) collective-permute-start(bf16[32,1,8,512]{3,2,1,0:T(8,128)(2,1)S(1)} %collective-permute-done.20.refs_8_), channel_id=1, source_target_pairs={{0,4},{1,5},{2,6},{3,7},{4,0},{5,1},{6,2},{7,3},{8,12},{9,13},{10,... | collective-permute-start | bytes 786440 | tf_op jit(solution)/shard_map/ppermute | solution.py:31
  78.6 8.4 %collective-permute-start.13 = (bf16[32,1,8,512]{3,2,1,0:T(8,128)(2,1)}, bf16[32,1,8,512]{3,2,1,0:T(8,128)(2,1)S(1)}, u32[]{:S(2)}, u32[]{:S(2)}) collective-permute-start(bf16[32,1,8,512]{3,2,1,0:T(8,128)(2,1)} %convolve.2.refs_0_), channel_id=1, source_target_pairs={{0,1},{1,0},{2,3},{3,2},{4,5},{5,4},{6,7},{7,6},{8,9},{9,8},{10,11... | collective-permute-start | bytes 786440 | tf_op jit(solution)/shard_map/ppermute | solution.py:31
  78.6 8.4 %collective-permute-start.17 = (bf16[32,1,8,512]{3,2,1,0:T(8,128)(2,1)S(1)}, bf16[32,1,8,512]{3,2,1,0:T(8,128)(2,1)S(1)}, u32[]{:S(2)}, u32[]{:S(2)}) collective-permute-start(bf16[32,1,8,512]{3,2,1,0:T(8,128)(2,1)S(1)} %collective-permute-done.16.refs_4_), channel_id=1, source_target_pairs={{0,1},{1,0},{2,3},{3,2},{4,5},{5,4},{6,7},{7,6},{8,9},{9,8},{10,11... | collective-permute-start | bytes 786440 | tf_op jit(solution)/shard_map/ppermute | solution.py:31
  79.1 10.0 %collective-permute-start.15 = (bf16[32,1,8,512]{3,2,1,0:T(8,128)(2,1)S(1)}, bf16[32,1,8,512]{3,2,1,0:T(8,128)(2,1)S(1)}, u32[]{:S(2)}, u32[]{:S(2)}) collective-permute-start(bf16[32,1,8,512]{3,2,1,0:T(8,128)(2,1)S(1)} %collective-permute-done.14.refs_2_), channel_id=1, source_target_pairs={{0,1},{1,0},{2,3},{3,2},{4,5},{5,4},{6,7},{7,6},{8,9},{9,8},{10,11... | collective-permute-start | bytes 786440 | tf_op jit(solution)/shard_map/ppermute | solution.py:31
  85.0 11.2 %collective-permute-start.26 = (bf16[32,1,8,512]{3,2,1,0:T(8,128)(2,1)S(1)}, bf16[32,1,8,512]{3,2,1,0:T(8,128)(2,1)S(1)}, u32[]{:S(2)}, u32[]{:S(2)}) collective-permute-start(bf16[32,1,8,512]{3,2,1,0:T(8,128)(2,1)S(1)} %collective-permute-done.24.refs_12_), channel_id=1, source_target_pairs={{0,2},{1,3},{2,0},{3,1},{4,6},{5,7},{6,4},{7,5},{8,10},{9,11},{10,... | collective-permute-start | bytes 786440 | tf_op jit(solution)/shard_map/ppermute | solution.py:31
  85.0 11.7 %collective-permute-start.22 = (bf16[32,1,8,512]{3,2,1,0:T(8,128)(2,1)S(1)}, bf16[32,1,8,512]{3,2,1,0:T(8,128)(2,1)S(1)}, u32[]{:S(2)}, u32[]{:S(2)}) collective-permute-start(bf16[32,1,8,512]{3,2,1,0:T(8,128)(2,1)S(1)} %collective-permute-done.20.refs_8_), channel_id=1, source_target_pairs={{0,2},{1,3},{2,0},{3,1},{4,6},{5,7},{6,4},{7,5},{8,10},{9,11},{10,... | collective-permute-start | bytes 786440 | tf_op jit(solution)/shard_map/ppermute | solution.py:31
  87.0 9.7 %collective-permute-start.25 = (bf16[32,1,8,512]{3,2,1,0:T(8,128)(2,1)S(1)}, bf16[32,1,8,512]{3,2,1,0:T(8,128)(2,1)S(1)}, u32[]{:S(2)}, u32[]{:S(2)}) collective-permute-start(bf16[32,1,8,512]{3,2,1,0:T(8,128)(2,1)S(1)} %collective-permute-done.24.refs_12_), channel_id=1, source_target_pairs={{0,1},{1,0},{2,3},{3,2},{4,5},{5,4},{6,7},{7,6},{8,9},{9,8},{10,11... | collective-permute-start | bytes 786440 | tf_op jit(solution)/shard_map/ppermute | solution.py:31
  87.1 5.5 %collective-permute-start.30 = (s32[8,128]{1,0:T(8,128)S(1)}, s32[8,128]{1,0:T(8,128)S(1)}, u32[]{:S(2)}, u32[]{:S(2)}) collective-permute-start(s32[8,128]{1,0:T(8,128)S(1)} %bitcast.46), channel_id=1, source_target_pairs={{0,12},{1,13},{2,14},{3,15},{4,8},{5,9},{6,10},{7,11},{8,4},{9,5},... | collective-permute-start | bytes 12296 | tf_op jit(solution)/shard_map/ppermute | solution.py:31
  89.2 4.5 %collective-permute-start.29 = (s32[8,128]{1,0:T(8,128)S(1)}, s32[8,128]{1,0:T(8,128)S(1)}, u32[]{:S(2)}, u32[]{:S(2)}) collective-permute-start(s32[8,128]{1,0:T(8,128)S(1)} %bitcast.47), channel_id=1, source_target_pairs={{0,8},{1,9},{2,10},{3,11},{4,12},{5,13},{6,14},{7,15},{8,0},{9,1},... | collective-permute-start | bytes 12296 | tf_op jit(solution)/shard_map/ppermute | solution.py:31
  92.5 3.6 %collective-permute-start.28 = (s32[8,128]{1,0:T(8,128)S(1)}, s32[8,128]{1,0:T(8,128)S(1)}, u32[]{:S(2)}, u32[]{:S(2)}) collective-permute-start(s32[8,128]{1,0:T(8,128)S(1)} %bitcast.48), channel_id=1, source_target_pairs={{0,4},{1,5},{2,6},{3,7},{4,0},{5,1},{6,2},{7,3},{8,12},{9,13},{10,... | collective-permute-start | bytes 12296 | tf_op jit(solution)/shard_map/ppermute | solution.py:31
  93.7 3.2 %collective-permute-start.21 = (bf16[32,1,8,512]{3,2,1,0:T(8,128)(2,1)S(1)}, bf16[32,1,8,512]{3,2,1,0:T(8,128)(2,1)S(1)}, u32[]{:S(2)}, u32[]{:S(2)}) collective-permute-start(bf16[32,1,8,512]{3,2,1,0:T(8,128)(2,1)S(1)} %collective-permute-done.20.refs_8_), channel_id=1, source_target_pairs={{0,1},{1,0},{2,3},{3,2},{4,5},{5,4},{6,7},{7,6},{8,9},{9,8},{10,11... | collective-permute-start | bytes 786440 | tf_op jit(solution)/shard_map/ppermute | solution.py:31
  96.1 1.5 collective-permute-start.19
  96.1 1.9 %collective-permute-start.27 = (bf16[32,1,8,512]{3,2,1,0:T(8,128)(2,1)S(1)}, bf16[32,1,8,512]{3,2,1,0:T(8,128)(2,1)S(1)}, u32[]{:S(2)}, u32[]{:S(2)}) collective-permute-start(bf16[32,1,8,512]{3,2,1,0:T(8,128)(2,1)S(1)} %collective-permute-done.26.refs_14_), channel_id=1, source_target_pairs={{0,1},{1,0},{2,3},{3,2},{4,5},{5,4},{6,7},{7,6},{8,9},{9,8},{10,11... | collective-permute-start | bytes 786440 | tf_op jit(solution)/shard_map/ppermute | solution.py:31
  96.7 1.8 %collective-permute-start.23 = (bf16[32,1,8,512]{3,2,1,0:T(8,128)(2,1)S(1)}, bf16[32,1,8,512]{3,2,1,0:T(8,128)(2,1)S(1)}, u32[]{:S(2)}, u32[]{:S(2)}) collective-permute-start(bf16[32,1,8,512]{3,2,1,0:T(8,128)(2,1)S(1)} %collective-permute-done.22.refs_10_), channel_id=1, source_target_pairs={{0,1},{1,0},{2,3},{3,2},{4,5},{5,4},{6,7},{7,6},{8,9},{9,8},{10,11... | collective-permute-start | bytes 786440 | tf_op jit(solution)/shard_map/ppermute | solution.py:31
  96.8 10.0 %collective-permute-start.31 = (s32[4,8,128]{2,1,0:T(8,128)S(1)}, s32[4,8,128]{2,1,0:T(8,128)S(1)}, u32[]{:S(2)}, u32[]{:S(2)}) collective-permute-start(s32[4,8,128]{2,1,0:T(8,128)S(1)} %get-tuple-element.43), channel_id=1, source_target_pairs={{0,2},{1,3},{2,0},{3,1},{4,6},{5,7},{6,4},{7,5},{8,10},{9,11},{10,... | collective-permute-start | bytes 49160 | tf_op jit(solution)/shard_map/ppermute | solution.py:31
  103.0 13.6 %all-to-all-start = ((bf16[16,2,8,512]{3,2,1,0:T(8,128)(2,1)}), bf16[16,2,8,512]{3,2,1,0:T(8,128)(2,1)S(1)}, u32[]{:S(2)}, u32[]{:S(2)}) async-start(bf16[16,2,8,512]{3,2,1,0:T(8,128)(2,1)} %window_columns.1), calls=%async_computation | async-start | bytes 524288 | tf_op jit(solution)/shard_map/all_to_all | solution.py:412
  106.7 1.3 collective-permute-start.32
  121.3 12.6 %collective-permute-start.36 = (bf16[32,1,8,512]{3,2,1,0:T(8,128)(2,1)}, bf16[32,1,8,512]{3,2,1,0:T(8,128)(2,1)S(1)}, u32[]{:S(2)}, u32[]{:S(2)}) collective-permute-start(bf16[32,1,8,512]{3,2,1,0:T(8,128)(2,1)} %convolve.3.refs_0_), channel_id=1, source_target_pairs={{0,4},{1,5},{2,6},{3,7},{4,0},{5,1},{6,2},{7,3},{8,12},{9,13},{10,... | collective-permute-start | bytes 786440 | tf_op jit(solution)/shard_map/ppermute | solution.py:31
  121.3 15.4 %collective-permute-start.40 = (bf16[32,1,8,512]{3,2,1,0:T(8,128)(2,1)}, bf16[32,1,8,512]{3,2,1,0:T(8,128)(2,1)S(1)}, u32[]{:S(2)}, u32[]{:S(2)}) collective-permute-start(bf16[32,1,8,512]{3,2,1,0:T(8,128)(2,1)} %convolve.3.refs_0_), channel_id=1, source_target_pairs={{0,8},{1,9},{2,10},{3,11},{4,12},{5,13},{6,14},{7,15},{8,0},{9,1},... | collective-permute-start | bytes 786440 | tf_op jit(solution)/shard_map/ppermute | solution.py:31
  122.8 14.4 %collective-permute-start.34 = (bf16[32,1,8,512]{3,2,1,0:T(8,128)(2,1)}, bf16[32,1,8,512]{3,2,1,0:T(8,128)(2,1)S(1)}, u32[]{:S(2)}, u32[]{:S(2)}) collective-permute-start(bf16[32,1,8,512]{3,2,1,0:T(8,128)(2,1)} %convolve.3.refs_0_), channel_id=1, source_target_pairs={{0,2},{1,3},{2,0},{3,1},{4,6},{5,7},{6,4},{7,5},{8,10},{9,11},{10,... | collective-permute-start | bytes 786440 | tf_op jit(solution)/shard_map/ppermute | solution.py:31
  133.9 7.5 %collective-permute-start.38 = (bf16[32,1,8,512]{3,2,1,0:T(8,128)(2,1)S(1)}, bf16[32,1,8,512]{3,2,1,0:T(8,128)(2,1)S(1)}, u32[]{:S(2)}, u32[]{:S(2)}) collective-permute-start(bf16[32,1,8,512]{3,2,1,0:T(8,128)(2,1)S(1)} %collective-permute-done.36.refs_4_), channel_id=1, source_target_pairs={{0,2},{1,3},{2,0},{3,1},{4,6},{5,7},{6,4},{7,5},{8,10},{9,11},{10,... | collective-permute-start | bytes 786440 | tf_op jit(solution)/shard_map/ppermute | solution.py:31
  136.7 7.8 %collective-permute-start.44 = (bf16[32,1,8,512]{3,2,1,0:T(8,128)(2,1)S(1)}, bf16[32,1,8,512]{3,2,1,0:T(8,128)(2,1)S(1)}, u32[]{:S(2)}, u32[]{:S(2)}) collective-permute-start(bf16[32,1,8,512]{3,2,1,0:T(8,128)(2,1)S(1)} %collective-permute-done.40.refs_8_), channel_id=1, source_target_pairs={{0,4},{1,5},{2,6},{3,7},{4,0},{5,1},{6,2},{7,3},{8,12},{9,13},{10,... | collective-permute-start | bytes 786440 | tf_op jit(solution)/shard_map/ppermute | solution.py:31
  136.7 9.9 %collective-permute-start.33 = (bf16[32,1,8,512]{3,2,1,0:T(8,128)(2,1)}, bf16[32,1,8,512]{3,2,1,0:T(8,128)(2,1)S(1)}, u32[]{:S(2)}, u32[]{:S(2)}) collective-permute-start(bf16[32,1,8,512]{3,2,1,0:T(8,128)(2,1)} %convolve.3.refs_0_), channel_id=1, source_target_pairs={{0,1},{1,0},{2,3},{3,2},{4,5},{5,4},{6,7},{7,6},{8,9},{9,8},{10,11... | collective-permute-start | bytes 786440 | tf_op jit(solution)/shard_map/ppermute | solution.py:31
  136.7 9.9 %collective-permute-start.37 = (bf16[32,1,8,512]{3,2,1,0:T(8,128)(2,1)S(1)}, bf16[32,1,8,512]{3,2,1,0:T(8,128)(2,1)S(1)}, u32[]{:S(2)}, u32[]{:S(2)}) collective-permute-start(bf16[32,1,8,512]{3,2,1,0:T(8,128)(2,1)S(1)} %collective-permute-done.36.refs_4_), channel_id=1, source_target_pairs={{0,1},{1,0},{2,3},{3,2},{4,5},{5,4},{6,7},{7,6},{8,9},{9,8},{10,11... | collective-permute-start | bytes 786440 | tf_op jit(solution)/shard_map/ppermute | solution.py:31
  137.2 9.9 %collective-permute-start.35 = (bf16[32,1,8,512]{3,2,1,0:T(8,128)(2,1)S(1)}, bf16[32,1,8,512]{3,2,1,0:T(8,128)(2,1)S(1)}, u32[]{:S(2)}, u32[]{:S(2)}) collective-permute-start(bf16[32,1,8,512]{3,2,1,0:T(8,128)(2,1)S(1)} %collective-permute-done.34.refs_2_), channel_id=1, source_target_pairs={{0,1},{1,0},{2,3},{3,2},{4,5},{5,4},{6,7},{7,6},{8,9},{9,8},{10,11... | collective-permute-start | bytes 786440 | tf_op jit(solution)/shard_map/ppermute | solution.py:31
  144.6 9.2 %collective-permute-start.46 = (bf16[32,1,8,512]{3,2,1,0:T(8,128)(2,1)S(1)}, bf16[32,1,8,512]{3,2,1,0:T(8,128)(2,1)S(1)}, u32[]{:S(2)}, u32[]{:S(2)}) collective-permute-start(bf16[32,1,8,512]{3,2,1,0:T(8,128)(2,1)S(1)} %collective-permute-done.44.refs_12_), channel_id=1, source_target_pairs={{0,2},{1,3},{2,0},{3,1},{4,6},{5,7},{6,4},{7,5},{8,10},{9,11},{10,... | collective-permute-start | bytes 786440 | tf_op jit(solution)/shard_map/ppermute | solution.py:31
  144.6 12.6 %collective-permute-start.42 = (bf16[32,1,8,512]{3,2,1,0:T(8,128)(2,1)S(1)}, bf16[32,1,8,512]{3,2,1,0:T(8,128)(2,1)S(1)}, u32[]{:S(2)}, u32[]{:S(2)}) collective-permute-start(bf16[32,1,8,512]{3,2,1,0:T(8,128)(2,1)S(1)} %collective-permute-done.40.refs_8_), channel_id=1, source_target_pairs={{0,2},{1,3},{2,0},{3,1},{4,6},{5,7},{6,4},{7,5},{8,10},{9,11},{10,... | collective-permute-start | bytes 786440 | tf_op jit(solution)/shard_map/ppermute | solution.py:31
  146.6 10.6 %collective-permute-start.41 = (bf16[32,1,8,512]{3,2,1,0:T(8,128)(2,1)S(1)}, bf16[32,1,8,512]{3,2,1,0:T(8,128)(2,1)S(1)}, u32[]{:S(2)}, u32[]{:S(2)}) collective-permute-start(bf16[32,1,8,512]{3,2,1,0:T(8,128)(2,1)S(1)} %collective-permute-done.40.refs_8_), channel_id=1, source_target_pairs={{0,1},{1,0},{2,3},{3,2},{4,5},{5,4},{6,7},{7,6},{8,9},{9,8},{10,11... | collective-permute-start | bytes 786440 | tf_op jit(solution)/shard_map/ppermute | solution.py:31
  146.6 10.5 %collective-permute-start.45 = (bf16[32,1,8,512]{3,2,1,0:T(8,128)(2,1)S(1)}, bf16[32,1,8,512]{3,2,1,0:T(8,128)(2,1)S(1)}, u32[]{:S(2)}, u32[]{:S(2)}) collective-permute-start(bf16[32,1,8,512]{3,2,1,0:T(8,128)(2,1)S(1)} %collective-permute-done.44.refs_12_), channel_id=1, source_target_pairs={{0,1},{1,0},{2,3},{3,2},{4,5},{5,4},{6,7},{7,6},{8,9},{9,8},{10,11... | collective-permute-start | bytes 786440 | tf_op jit(solution)/shard_map/ppermute | solution.py:31
  147.1 10.1 %collective-permute-start.39 = (bf16[32,1,8,512]{3,2,1,0:T(8,128)(2,1)S(1)}, bf16[32,1,8,512]{3,2,1,0:T(8,128)(2,1)S(1)}, u32[]{:S(2)}, u32[]{:S(2)}) collective-permute-start(bf16[32,1,8,512]{3,2,1,0:T(8,128)(2,1)S(1)} %collective-permute-done.38.refs_6_), channel_id=1, source_target_pairs={{0,1},{1,0},{2,3},{3,2},{4,5},{5,4},{6,7},{7,6},{8,9},{9,8},{10,11... | collective-permute-start | bytes 786440 | tf_op jit(solution)/shard_map/ppermute | solution.py:31
  153.8 3.4 %collective-permute-start.47 = (bf16[32,1,8,512]{3,2,1,0:T(8,128)(2,1)S(1)}, bf16[32,1,8,512]{3,2,1,0:T(8,128)(2,1)S(1)}, u32[]{:S(2)}, u32[]{:S(2)}) collective-permute-start(bf16[32,1,8,512]{3,2,1,0:T(8,128)(2,1)S(1)} %collective-permute-done.46.refs_14_), channel_id=1, source_target_pairs={{0,1},{1,0},{2,3},{3,2},{4,5},{5,4},{6,7},{7,6},{8,9},{9,8},{10,11... | collective-permute-start | bytes 786440 | tf_op jit(solution)/shard_map/ppermute | solution.py:31
  157.1 1.5 collective-permute-start.43
  (37 other events, 344.4 us)

commit v4 on v3

--- a/solution.py
+++ b/solution.py
@@ -367,7 +367,7 @@
             stride *= 2
         return held[0], moved[min(1, nz - 1)]
 
-    def gather(y):
+    def gather(y, in_turn):
         line = {0: y}
         over = {0: swap(y, 2)}
         stride = nz // 2
@@ -376,14 +376,16 @@
             for d, p in list(line.items()):
                 line[d ^ stride] = swap(p, 4 * stride)
                 if d == 0 and stride == 1:
-                    over[1] = swap(line[1], 2)
+                    over[1] = swap(after(line[1], over[0]) if in_turn else line[1], 2)
                     for k in line:
                         if k > 1:
                             line[k] = far = after(line[k], over[1])
             stride //= 2
         chip = []
         for d in range(nz):
-            chip += [line[d], over[d] if d in over else swap(line[d], 2)]
+            if d not in over:
+                over[d] = swap(after(line[d], over[d - 1]) if in_turn else line[d], 2)
+            chip += [line[d], over[d]]
         return [p for a in chip for p in (a, swap(a, 1))], far
 
     part = partial_spectra(table_part, mine, theirs, rb, nq, 0, 1)
@@ -406,7 +408,7 @@
 
     held[0] = after(held[0], table_cols, table_time)
     y1 = convolve(held, refl_scale, refl, 1.0)
-    pieces, far = gather(y1)
+    pieces, far = gather(y1, False)
     onset_own = onset.reshape(-1, 1, 1, c)
     x2 = window_columns(pieces, me, table_cols, onset_own, 2.0 / ntime)
     x2 = lax.all_to_all(x2, "freq", split_axis=0, concat_axis=0, tiled=True)
@@ -418,7 +420,7 @@
     minus = time_block(pieces, table_time, first_own, onset_all, None, ntime, 0, None)
     x2 = after(x2, minus).reshape(v, nq, rb, c)
     y2 = convolve([x2], refl_scale, refl, -1.0)
-    pieces, _ = gather(y2)
+    pieces, _ = gather(y2, True)
     plus = time_block(pieces, table_time, first_own, onset_all, fd_plus, ntime, 0, None)
     return minus, plus
 

time: 167 us -> 165 us (0.988)
  waiting for transfers between devices: 74.7 us -> 71.4 us
    ppermute x48, waiting for transfers between devices: 72.1 us -> 68.8 us  [swap(): return lax.ppermute(x, 'freq', [(i, i ^ stride) for i in range(n)])]
  transfers between devices with their start and end apart: 49 -> 49, of which waited for: 24 -> 24; matrix products, arithmetic and copies ran while one was open for 5% -> 5% of each run, Pallas kernels for 8% -> 9%
where the time goes in v4:
time: 165 us; the launch traced here: 164 us
  waiting for transfers between devices  71.4 us (43%)
  Pallas kernels  39.6 us (24%)
  starting transfers between devices  39.4 us (24%)
  other arithmetic  7.62 us (5%)
  local copies, waits for them, and re-layouts  4.99 us (3%)
    ppermute x48, waiting for transfers between devices, swap(): return lax.ppermute(x, 'freq', [(i, i ^ stride) for i in range(n)])  68.8 us
    ppermute x48, starting transfers between devices, swap(): return lax.ppermute(x, 'freq', [(i, i ^ stride) for i in range(n)])  35.7 us
    pallas_call x2, Pallas kernels, time_block(): pl.pallas_call(kernel, grid=(s // sb,), in_specs=specs, out_specs=field_s...  12.1 us
    pallas_call x2, Pallas kernels, points_major(): pl.pallas_call(kernel, grid=(s // sb,), in_specs=[pl.BlockSpec((t, v, sb)...  10.2 us
    pallas_call x2, Pallas kernels, convolve(): pl.pallas_call(kernel, grid=(nf // fb,), in_specs=specs, out_specs=whole,...  8.18 us
    pallas_call x1, Pallas kernels, partial_spectra(): pl.pallas_call(kernel, grid=(steps,), in_specs=[pl.BlockSpec((rows, 2 * t...  5.35 us
    pallas_call x1, Pallas kernels, window_columns(): pl.pallas_call(kernel, grid_spec=pltpu.PrefetchScalarGridSpec(num_scalar_...  3.87 us
    all_to_all x1, starting transfers between devices, local(): x2 = lax.all_to_all(x2, 'freq', split_axis=0, concat_axis=0, tiled=True)  3.73 us
  transfers between devices with their start and end apart: 49, of which 24 were waited for; matrix products, arithmetic and copies ran while one was open for 5% of the time, Pallas kernels for 9%

profile of v4, /device:TPU:0, one launch (start us, length us, event | category | flops | bytes accessed | tf_op | source)
XLA Modules:
  0.0 164.4 jit_solution(7092793119714413057)
XLA Ops:
  1.1 2.7 %collective-permute-start = (s32[4]{0:T(128)}, s32[4]{0:T(128)S(1)}, u32[]{:S(2)}, u32[]{:S(2)}) collective-permute-start(s32[4]{0:T(128)} %param.7), channel_id=1, source_target_pairs={{0,4},{1,5},{2,6},{3,7},{4,0},{5,1},{6,2},{7,3},{8,12},{9,13},{10,... | collective-permute-start | bytes 56 | tf_op jit(solution)/shard_map/ppermute | solution.py:31
  3.8 2.5 %collective-permute-start.2 = (s32[4]{0:T(128)}, s32[4]{0:T(128)S(1)}, u32[]{:S(2)}, u32[]{:S(2)}) collective-permute-start(s32[4]{0:T(128)} %param.7), channel_id=1, source_target_pairs={{0,12},{1,13},{2,14},{3,15},{4,8},{5,9},{6,10},{7,11},{8,4},{9,5},... | collective-permute-start | bytes 56 | tf_op jit(solution)/shard_map/ppermute | solution.py:31
  6.4 5.1 %points_major.2.own_ref = bf16[32,128,512]{2,1,0:T(8,128)(2,1)} custom-call(bf16[128,32,512]{2,1,0:T(8,128)(2,1)} %refs_19_.1), custom_call_target="tpu_custom_call" | custom-call | tf_op jit(solution)/shard_map/points_major/pallas_call | solution.py:50
  11.6 5.1 %points_major.3.other_ref = bf16[32,128,512]{2,1,0:T(8,128)(2,1)} custom-call(bf16[128,32,512]{2,1,0:T(8,128)(2,1)} %collective-permute-done.3.x_ref), custom_call_target="tpu_custom_call" | custom-call | tf_op jit(solution)/shard_map/points_major/pallas_call | solution.py:50
  16.6 1.5 collective-permute-start.4
  18.2 2.0 %collective-permute-done.4 = s32[4,4]{1,0:T(4,128)S(1)} collective-permute-done((s32[4,4]{1,0:T(4,128)S(1)}, s32[4,4]{1,0:T(4,128)S(1)}, u32[]{:S(2)}, u32[]{:S(2)}) %collective-permute-start.4) | collective-permute-done | bytes 96 | tf_op jit(solution)/shard_map/ppermute | solution.py:31
  21.5 5.4 %partial_spectra.1 = (bf16[32,1,8,512]{3,2,1,0:T(8,128)(2,1)}, bf16[32,1,8,512]{3,2,1,0:T(8,128)(2,1)}, bf16[32,1,8,512]{3,2,1,0:T(8,128)(2,1)}, bf16[32,1,8,512...) custom-call(bf16[64,256]{1,0:T(8,128)(2,1)} %fusion.9.tab_ref, ...), custom_call_target="tpu_custom_call" | custom-call | tf_op jit(solution)/shard_map/partial_spectra/pallas_call | solution.py:81
  26.8 1.5 collective-permute-start.6
  28.9 7.4 %collective-permute-done.6 = bf16[32,1,8,512]{3,2,1,0:T(8,128)(2,1)S(1)} collective-permute-done((bf16[32,1,8,512]{3,2,1,0:T(8,128)(2,1)}, bf16[32,1,8,512]{3,2,1,0:T(8,128)(2,1)S(1)}, u32[]{:S(2)}, u32[]{:S(2)}) %collective-permute-start.6) | collective-permute-done | bytes 262176 | tf_op jit(solution)/shard_map/ppermute | solution.py:31
  36.3 1.5 collective-permute-start.7
  37.8 1.0 add_convert_fusion.1
  38.8 1.9 %collective-permute-start.10 = (bf16[32,1,8,512]{3,2,1,0:T(8,128)(2,1)S(1)}, bf16[32,1,8,512]{3,2,1,0:T(8,128)(2,1)S(1)}, u32[]{:S(2)}, u32[]{:S(2)}) collective-permute-start(bf16[32,1,8,512]{3,2,1,0:T(8,128)(2,1)S(1)} %add_convert_fusion.1), channel_id=1, source_target_pairs={{0,4},{1,5},{2,6},{3,7},{4,0},{5,1},{6,2},{7,3},{8,12},{9,13},{10,... | collective-permute-start | bytes 786440 | tf_op jit(solution)/shard_map/ppermute | solution.py:31
  41.9 1.5 collective-permute-start.9
  43.4 2.1 %collective-permute-done.7 = bf16[32,1,8,512]{3,2,1,0:T(8,128)(2,1)S(1)} collective-permute-done((bf16[32,1,8,512]{3,2,1,0:T(8,128)(2,1)}, bf16[32,1,8,512]{3,2,1,0:T(8,128)(2,1)S(1)}, u32[]{:S(2)}, u32[]{:S(2)}) %collective-permute-start.7) | collective-permute-done | bytes 262176 | tf_op jit(solution)/shard_map/ppermute | solution.py:31
  45.9 1.1 add_convert_fusion
  46.9 3.4 %collective-permute-start.12 = (bf16[32,1,8,512]{3,2,1,0:T(8,128)(2,1)S(1)}, bf16[32,1,8,512]{3,2,1,0:T(8,128)(2,1)S(1)}, u32[]{:S(2)}, u32[]{:S(2)}) collective-permute-start(bf16[32,1,8,512]{3,2,1,0:T(8,128)(2,1)S(1)} %add_convert_fusion), channel_id=1, source_target_pairs={{0,8},{1,9},{2,10},{3,11},{4,12},{5,13},{6,14},{7,15},{8,0},{9,1},... | collective-permute-start | bytes 786440 | tf_op jit(solution)/shard_map/ppermute | solution.py:31
  50.4 1.0 add_convert_fusion.2
  52.4 2.2 %fusion.4.refs_16_ = bf16[128,768]{1,0:T(8,128)(2,1)} fusion(s32[128]{0:T(128)S(1)} %add.84, s32[128]{0:T(128)S(1)} %mul.94), kind=kLoop, calls=%fused_computation.11 | loop fusion | flops 1572864 | bytes 197632 | tf_op jit(solution)/shard_map/convert_element_type | solution.py:407
  54.7 5.9 %collective-permute-done.11.refs_2_ = bf16[32,1,8,512]{3,2,1,0:T(8,128)(2,1)S(1)} collective-permute-done((bf16[32,1,8,512]{3,2,1,0:T(8,128)(2,1)S(1)}, bf16[32,1,8,512]{3,2,1,0:T(8,128)(2,1)S(1)}, u32[]{:S(2)}, u32[]{:S(2)}) %collective-permute-start.11) | collective-permute-done | bytes 262176 | tf_op jit(solution)/shard_map/ppermute | solution.py:31
  62.0 4.2 %convolve.2.refs_0_ = bf16[32,1,8,512]{3,2,1,0:T(8,128)(2,1)} custom-call(bf16[32,1,8,512]{3,2,1,0:T(8,128)(2,1)} %get-tuple-element.31.refs_0_, bf16[32,1,8,512]{3,2,1,0:T(8,128)(2,1)} %copy-done.31, bf16[32,1,8,512]{3,2,1,0:T(8,128)(2,1)} %copy-done.33, bf16[32,1,8,512]{3,2,1,0:T(8,128)(2,1)} %copy-done.32, f32[4,4]{1,0:T(4,128)} %refs_1_.1, ...), custom_call_target="tpu_custom_call" | custom-call | tf_op jit(solution)/shard_map/convolve/pallas_call | solution.py:151
  66.3 2.0 %collective-permute-start.20 = (bf16[32,1,8,512]{3,2,1,0:T(8,128)(2,1)}, bf16[32,1,8,512]{3,2,1,0:T(8,128)(2,1)S(1)}, u32[]{:S(2)}, u32[]{:S(2)}) collective-permute-start(bf16[32,1,8,512]{3,2,1,0:T(8,128)(2,1)} %convolve.2.refs_0_), channel_id=1, source_target_pairs={{0,8},{1,9},{2,10},{3,11},{4,12},{5,13},{6,14},{7,15},{8,0},{9,1},... | collective-permute-start | bytes 786440 | tf_op jit(solution)/shard_map/ppermute | solution.py:31
  68.3 1.8 %collective-permute-start.14 = (bf16[32,1,8,512]{3,2,1,0:T(8,128)(2,1)}, bf16[32,1,8,512]{3,2,1,0:T(8,128)(2,1)S(1)}, u32[]{:S(2)}, u32[]{:S(2)}) collective-permute-start(bf16[32,1,8,512]{3,2,1,0:T(8,128)(2,1)} %convolve.2.refs_0_), channel_id=1, source_target_pairs={{0,2},{1,3},{2,0},{3,1},{4,6},{5,7},{6,4},{7,5},{8,10},{9,11},{10,... | collective-permute-start | bytes 786440 | tf_op jit(solution)/shard_map/ppermute | solution.py:31
  70.1 6.4 %collective-permute-done.16.refs_4_ = bf16[32,1,8,512]{3,2,1,0:T(8,128)(2,1)S(1)} collective-permute-done((bf16[32,1,8,512]{3,2,1,0:T(8,128)(2,1)}, bf16[32,1,8,512]{3,2,1,0:T(8,128)(2,1)S(1)}, u32[]{:S(2)}, u32[]{:S(2)}) %collective-permute-start.16) | collective-permute-done | bytes 262176 | tf_op jit(solution)/shard_map/ppermute | solution.py:31
  77.0 1.6 collective-permute-done.20.refs_8_
  79.2 4.0 %collective-permute-done.18.refs_6_ = bf16[32,1,8,512]{3,2,1,0:T(8,128)(2,1)S(1)} collective-permute-done((bf16[32,1,8,512]{3,2,1,0:T(8,128)(2,1)S(1)}, bf16[32,1,8,512]{3,2,1,0:T(8,128)(2,1)S(1)}, u32[]{:S(2)}, u32[]{:S(2)}) %collective-permute-start.18) | collective-permute-done | bytes 262176 | tf_op jit(solution)/shard_map/ppermute | solution.py:31
  83.2 1.8 %collective-permute-done.24.refs_12_ = bf16[32,1,8,512]{3,2,1,0:T(8,128)(2,1)S(1)} collective-permute-done((bf16[32,1,8,512]{3,2,1,0:T(8,128)(2,1)S(1)}, bf16[32,1,8,512]{3,2,1,0:T(8,128)(2,1)S(1)}, u32[]{:S(2)}, u32[]{:S(2)}) %collective-permute-start.24) | collective-permute-done | bytes 262176 | tf_op jit(solution)/shard_map/ppermute | solution.py:31
  85.0 2.0 %collective-permute-start.22 = (bf16[32,1,8,512]{3,2,1,0:T(8,128)(2,1)S(1)}, bf16[32,1,8,512]{3,2,1,0:T(8,128)(2,1)S(1)}, u32[]{:S(2)}, u32[]{:S(2)}) collective-permute-start(bf16[32,1,8,512]{3,2,1,0:T(8,128)(2,1)S(1)} %collective-permute-done.20.refs_8_), channel_id=1, source_target_pairs={{0,2},{1,3},{2,0},{3,1},{4,6},{5,7},{6,4},{7,5},{8,10},{9,11},{10,... | collective-permute-start | bytes 786440 | tf_op jit(solution)/shard_map/ppermute | solution.py:31
  87.1 2.1 %collective-permute-start.30 = (s32[8,128]{1,0:T(8,128)S(1)}, s32[8,128]{1,0:T(8,128)S(1)}, u32[]{:S(2)}, u32[]{:S(2)}) collective-permute-start(s32[8,128]{1,0:T(8,128)S(1)} %bitcast.46), channel_id=1, source_target_pairs={{0,12},{1,13},{2,14},{3,15},{4,8},{5,9},{6,10},{7,11},{8,4},{9,5},... | collective-permute-start | bytes 12296 | tf_op jit(solution)/shard_map/ppermute | solution.py:31
  89.2 3.4 %collective-permute-done.30 = s32[8,128]{1,0:T(8,128)S(1)} collective-permute-done((s32[8,128]{1,0:T(8,128)S(1)}, s32[8,128]{1,0:T(8,128)S(1)}, u32[]{:S(2)}, u32[]{:S(2)}) %collective-permute-start.30) | collective-permute-done | bytes 4128 | tf_op jit(solution)/shard_map/ppermute | solution.py:31
  92.5 1.1 collective-permute-done.29
  93.7 2.5 %collective-permute-done.28 = s32[8,128]{1,0:T(8,128)S(1)} collective-permute-done((s32[8,128]{1,0:T(8,128)S(1)}, s32[8,128]{1,0:T(8,128)S(1)}, u32[]{:S(2)}, u32[]{:S(2)}) %collective-permute-start.28) | collective-permute-done | bytes 4128 | tf_op jit(solution)/shard_map/ppermute | solution.py:31
  99.1 3.9 %window_columns.1 = bf16[16,2,8,512]{3,2,1,0:T(8,128)(2,1)} custom-call(s32[1]{0:T(128)} %bitcast.21.me_ref, bf16[32,1,8,512]{3,2,1,0:T(8,128)(2,1)} %convolve.2.refs_0_, bf16[32,1,8,512]{3,2,1,0:T(8,128)(2,1)} %copy-done.5, bf16[32,1,8,512]{3,2,1,0:T(8,128)(2,1)} %copy-done.2, bf16[32,1,8,512]{3,2,1,0:T(8,128)(2,1)} %copy-done.7, ...), custom_call_target="tpu_custom_call" | custom-call | tf_op jit(solution)/shard_map/window_columns/pallas_call | solution.py:208
  103.0 3.7 %all-to-all-start = ((bf16[16,2,8,512]{3,2,1,0:T(8,128)(2,1)}), bf16[16,2,8,512]{3,2,1,0:T(8,128)(2,1)S(1)}, u32[]{:S(2)}, u32[]{:S(2)}) async-start(bf16[16,2,8,512]{3,2,1,0:T(8,128)(2,1)} %window_columns.1), calls=%async_computation | async-start | bytes 524288 | tf_op jit(solution)/shard_map/all_to_all | solution.py:414
  108.9 5.0 %time_block.2 = bf16[128,32,512]{2,1,0:T(8,128)(2,1)} custom-call(bf16[32,1,8,512]{3,2,1,0:T(8,128)(2,1)} %convolve.2.refs_0_, bf16[32,1,8,512]{3,2,1,0:T(8,128)(2,1)} %copy-done.5, bf16[32,1,8,512]{3,2,1,0:T(8,128)(2,1)} %copy-done.2, bf16[32,1,8,512]{3,2,1,0:T(8,128)(2,1)} %copy-done.7, bf16[32,1,8,512]{3,2,1,0:T(8,128)(2,1)} %copy-done, ...), custom_call_target="tpu_custom_call" | custom-call | tf_op jit(solution)/shard_map/time_block/pallas_call | solution.py:284
  114.0 2.6 %all-to-all-done = bf16[16,2,8,512]{3,2,1,0:T(8,128)(2,1)S(1)} async-done(((bf16[16,2,8,512]{3,2,1,0:T(8,128)(2,1)}), bf16[16,2,8,512]{3,2,1,0:T(8,128)(2,1)S(1)}, u32[]{:S(2)}, u32[]{:S(2)}) %all-to-all-start) | async-done | bytes 262176 | tf_op jit(solution)/shard_map/all_to_all | solution.py:414
  117.3 4.0 %convolve.3.refs_0_ = bf16[32,1,8,512]{3,2,1,0:T(8,128)(2,1)} custom-call(bf16[32,1,8,512]{3,2,1,0:T(8,128)(2,1)} %bitcast.37, f32[4,4]{1,0:T(4,128)} %refs_1_.1, bf16[4,2,512,512]{3,2,1,0:T(8,128)(2,1)} %refs_2_.1), custom_call_target="tpu_custom_call" | custom-call | tf_op jit(solution)/shard_map/convolve/pallas_call | solution.py:151
  121.3 1.1 collective-permute-start.34
  122.4 1.8 %collective-permute-start.40 = (bf16[32,1,8,512]{3,2,1,0:T(8,128)(2,1)}, bf16[32,1,8,512]{3,2,1,0:T(8,128)(2,1)S(1)}, u32[]{:S(2)}, u32[]{:S(2)}) collective-permute-start(bf16[32,1,8,512]{3,2,1,0:T(8,128)(2,1)} %convolve.3.refs_0_), channel_id=1, source_target_pairs={{0,8},{1,9},{2,10},{3,11},{4,12},{5,13},{6,14},{7,15},{8,0},{9,1},... | collective-permute-start | bytes 786440 | tf_op jit(solution)/shard_map/ppermute | solution.py:31
  124.2 9.2 %collective-permute-done.36.refs_4_ = bf16[32,1,8,512]{3,2,1,0:T(8,128)(2,1)S(1)} collective-permute-done((bf16[32,1,8,512]{3,2,1,0:T(8,128)(2,1)}, bf16[32,1,8,512]{3,2,1,0:T(8,128)(2,1)S(1)}, u32[]{:S(2)}, u32[]{:S(2)}) %collective-permute-start.36) | collective-permute-done | bytes 262176 | tf_op jit(solution)/shard_map/ppermute | solution.py:31
  133.7 3.5 %collective-permute-done.40.refs_8_ = bf16[32,1,8,512]{3,2,1,0:T(8,128)(2,1)S(1)} collective-permute-done((bf16[32,1,8,512]{3,2,1,0:T(8,128)(2,1)}, bf16[32,1,8,512]{3,2,1,0:T(8,128)(2,1)S(1)}, u32[]{:S(2)}, u32[]{:S(2)}) %collective-permute-start.40) | collective-permute-done | bytes 262176 | tf_op jit(solution)/shard_map/ppermute | solution.py:31
  137.2 3.6 %collective-permute-done.38.refs_6_ = bf16[32,1,8,512]{3,2,1,0:T(8,128)(2,1)S(1)} collective-permute-done((bf16[32,1,8,512]{3,2,1,0:T(8,128)(2,1)S(1)}, bf16[32,1,8,512]{3,2,1,0:T(8,128)(2,1)S(1)}, u32[]{:S(2)}, u32[]{:S(2)}) %collective-permute-start.38) | collective-permute-done | bytes 262176 | tf_op jit(solution)/shard_map/ppermute | solution.py:31
  140.8 1.4 collective-permute-start.42
  142.7 1.6 collective-permute-done.44.refs_12_
  144.3 3.8 %collective-permute-done.42.refs_10_ = bf16[32,1,8,512]{3,2,1,0:T(8,128)(2,1)S(1)} collective-permute-done((bf16[32,1,8,512]{3,2,1,0:T(8,128)(2,1)S(1)}, bf16[32,1,8,512]{3,2,1,0:T(8,128)(2,1)S(1)}, u32[]{:S(2)}, u32[]{:S(2)}) %collective-permute-start.42) | collective-permute-done | bytes 262176 | tf_op jit(solution)/shard_map/ppermute | solution.py:31
  148.1 1.7 %collective-permute-start.46 = (bf16[32,1,8,512]{3,2,1,0:T(8,128)(2,1)S(1)}, bf16[32,1,8,512]{3,2,1,0:T(8,128)(2,1)S(1)}, u32[]{:S(2)}, u32[]{:S(2)}) collective-permute-start(bf16[32,1,8,512]{3,2,1,0:T(8,128)(2,1)S(1)} %collective-permute-done.44.refs_12_), channel_id=1, source_target_pairs={{0,2},{1,3},{2,0},{3,1},{4,6},{5,7},{6,4},{7,5},{8,10},{9,11},{10,... | collective-permute-start | bytes 786440 | tf_op jit(solution)/shard_map/ppermute | solution.py:31
  150.9 4.0 %collective-permute-done.46.refs_14_ = bf16[32,1,8,512]{3,2,1,0:T(8,128)(2,1)S(1)} collective-permute-done((bf16[32,1,8,512]{3,2,1,0:T(8,128)(2,1)S(1)}, bf16[32,1,8,512]{3,2,1,0:T(8,128)(2,1)S(1)}, u32[]{:S(2)}, u32[]{:S(2)}) %collective-permute-start.46) | collective-permute-done | bytes 262176 | tf_op jit(solution)/shard_map/ppermute | solution.py:31
  154.9 1.5 collective-permute-done.47.refs_15_
  157.2 7.0 %time_block.3 = f32[128,32,512]{2,1,0:T(8,128)} custom-call(bf16[32,1,8,512]{3,2,1,0:T(8,128)(2,1)} %convolve.3.refs_0_, bf16[32,1,8,512]{3,2,1,0:T(8,128)(2,1)} %copy-done.22, bf16[32,1,8,512]{3,2,1,0:T(8,128)(2,1)} %copy-done.17, bf16[32,1,8,512]{3,2,1,0:T(8,128)(2,1)} %copy-done.24, bf16[32,1,8,512]{3,2,1,0:T(8,128)(2,1)} %copy-done.16, ...), custom_call_target="tpu_custom_call" | custom-call | tf_op jit(solution)/shard_map/time_block/pallas_call | solution.py:284
  (165 shorter events, 16.0 us)
Async XLA Ops:
  0.6 10.9 %collective-permute-start.3 = (bf16[128,32,512]{2,1,0:T(8,128)(2,1)}, bf16[128,32,512]{2,1,0:T(8,128)(2,1)}, u32[]{:S(2)}, u32[]{:S(2)}) collective-permute-start(bf16[128,32,512]{2,1,0:T(8,128)(2,1)} %refs_19_.1), channel_id=1, source_target_pairs={{0,1},{1,0},{2,3},{3,2},{4,5},{5,4},{6,7},{7,6},{8,9},{9,8},{10,11... | collective-permute-start | bytes 12582920 | tf_op jit(solution)/shard_map/ppermute | solution.py:31
  1.1 10.4 %collective-permute-start = (s32[4]{0:T(128)}, s32[4]{0:T(128)S(1)}, u32[]{:S(2)}, u32[]{:S(2)}) collective-permute-start(s32[4]{0:T(128)} %param.7), channel_id=1, source_target_pairs={{0,4},{1,5},{2,6},{3,7},{4,0},{5,1},{6,2},{7,3},{8,12},{9,13},{10,... | collective-permute-start | bytes 56 | tf_op jit(solution)/shard_map/ppermute | solution.py:31
  3.8 7.7 %collective-permute-start.2 = (s32[4]{0:T(128)}, s32[4]{0:T(128)S(1)}, u32[]{:S(2)}, u32[]{:S(2)}) collective-permute-start(s32[4]{0:T(128)} %param.7), channel_id=1, source_target_pairs={{0,12},{1,13},{2,14},{3,15},{4,8},{5,9},{6,10},{7,11},{8,4},{9,5},... | collective-permute-start | bytes 56 | tf_op jit(solution)/shard_map/ppermute | solution.py:31
  6.3 5.2 %collective-permute-start.1 = (s32[4]{0:T(128)}, s32[4]{0:T(128)S(1)}, u32[]{:S(2)}, u32[]{:S(2)}) collective-permute-start(s32[4]{0:T(128)} %param.7), channel_id=1, source_target_pairs={{0,8},{1,9},{2,10},{3,11},{4,12},{5,13},{6,14},{7,15},{8,0},{9,1},... | collective-permute-start | bytes 56 | tf_op jit(solution)/shard_map/ppermute | solution.py:31
  16.6 3.6 %collective-permute-start.4 = (s32[4,4]{1,0:T(4,128)S(1)}, s32[4,4]{1,0:T(4,128)S(1)}, u32[]{:S(2)}, u32[]{:S(2)}) collective-permute-start(s32[4,4]{1,0:T(4,128)S(1)} %pad_add_fusion.5), channel_id=1, source_target_pairs={{0,2},{1,3},{2,0},{3,1},{4,6},{5,7},{6,4},{7,5},{8,10},{9,11},{10,... | collective-permute-start | bytes 200 | tf_op jit(solution)/shard_map/ppermute | solution.py:31
  26.8 9.5 %collective-permute-start.6 = (bf16[32,1,8,512]{3,2,1,0:T(8,128)(2,1)}, bf16[32,1,8,512]{3,2,1,0:T(8,128)(2,1)S(1)}, u32[]{:S(2)}, u32[]{:S(2)}) collective-permute-start(bf16[32,1,8,512]{3,2,1,0:T(8,128)(2,1)} %get-tuple-element.28), channel_id=1, source_target_pairs={{0,2},{1,3},{2,0},{3,1},{4,6},{5,7},{6,4},{7,5},{8,10},{9,11},{10,... | collective-permute-start | bytes 786440 | tf_op jit(solution)/shard_map/ppermute | solution.py:31
  28.4 13.6 %collective-permute-start.8 = (bf16[32,1,8,512]{3,2,1,0:T(8,128)(2,1)}, bf16[32,1,8,512]{3,2,1,0:T(8,128)(2,1)S(1)}, u32[]{:S(2)}, u32[]{:S(2)}) collective-permute-start(bf16[32,1,8,512]{3,2,1,0:T(8,128)(2,1)} %get-tuple-element.33), channel_id=1, source_target_pairs={{0,2},{1,3},{2,0},{3,1},{4,6},{5,7},{6,4},{7,5},{8,10},{9,11},{10,... | collective-permute-start | bytes 786440 | tf_op jit(solution)/shard_map/ppermute | solution.py:31
  36.3 9.2 %collective-permute-start.7 = (bf16[32,1,8,512]{3,2,1,0:T(8,128)(2,1)}, bf16[32,1,8,512]{3,2,1,0:T(8,128)(2,1)S(1)}, u32[]{:S(2)}, u32[]{:S(2)}) collective-permute-start(bf16[32,1,8,512]{3,2,1,0:T(8,128)(2,1)} %get-tuple-element.29), channel_id=1, source_target_pairs={{0,2},{1,3},{2,0},{3,1},{4,6},{5,7},{6,4},{7,5},{8,10},{9,11},{10,... | collective-permute-start | bytes 786440 | tf_op jit(solution)/shard_map/ppermute | solution.py:31
  38.8 7.0 %collective-permute-start.10 = (bf16[32,1,8,512]{3,2,1,0:T(8,128)(2,1)S(1)}, bf16[32,1,8,512]{3,2,1,0:T(8,128)(2,1)S(1)}, u32[]{:S(2)}, u32[]{:S(2)}) collective-permute-start(bf16[32,1,8,512]{3,2,1,0:T(8,128)(2,1)S(1)} %add_convert_fusion.1), channel_id=1, source_target_pairs={{0,4},{1,5},{2,6},{3,7},{4,0},{5,1},{6,2},{7,3},{8,12},{9,13},{10,... | collective-permute-start | bytes 786440 | tf_op jit(solution)/shard_map/ppermute | solution.py:31
  41.9 12.7 %collective-permute-start.9 = (bf16[32,1,8,512]{3,2,1,0:T(8,128)(2,1)}, bf16[32,1,8,512]{3,2,1,0:T(8,128)(2,1)S(1)}, u32[]{:S(2)}, u32[]{:S(2)}) collective-permute-start(bf16[32,1,8,512]{3,2,1,0:T(8,128)(2,1)} %get-tuple-element.34), channel_id=1, source_target_pairs={{0,2},{1,3},{2,0},{3,1},{4,6},{5,7},{6,4},{7,5},{8,10},{9,11},{10,... | collective-permute-start | bytes 786440 | tf_op jit(solution)/shard_map/ppermute | solution.py:31
  46.9 13.7 %collective-permute-start.12 = (bf16[32,1,8,512]{3,2,1,0:T(8,128)(2,1)S(1)}, bf16[32,1,8,512]{3,2,1,0:T(8,128)(2,1)S(1)}, u32[]{:S(2)}, u32[]{:S(2)}) collective-permute-start(bf16[32,1,8,512]{3,2,1,0:T(8,128)(2,1)S(1)} %add_convert_fusion), channel_id=1, source_target_pairs={{0,8},{1,9},{2,10},{3,11},{4,12},{5,13},{6,14},{7,15},{8,0},{9,1},... | collective-permute-start | bytes 786440 | tf_op jit(solution)/shard_map/ppermute | solution.py:31
  51.4 9.2 %collective-permute-start.11 = (bf16[32,1,8,512]{3,2,1,0:T(8,128)(2,1)S(1)}, bf16[32,1,8,512]{3,2,1,0:T(8,128)(2,1)S(1)}, u32[]{:S(2)}, u32[]{:S(2)}) collective-permute-start(bf16[32,1,8,512]{3,2,1,0:T(8,128)(2,1)S(1)} %add_convert_fusion.2), channel_id=1, source_target_pairs={{0,4},{1,5},{2,6},{3,7},{4,0},{5,1},{6,2},{7,3},{8,12},{9,13},{10,... | collective-permute-start | bytes 786440 | tf_op jit(solution)/shard_map/ppermute | solution.py:31
  66.2 10.3 %collective-permute-start.16 = (bf16[32,1,8,512]{3,2,1,0:T(8,128)(2,1)}, bf16[32,1,8,512]{3,2,1,0:T(8,128)(2,1)S(1)}, u32[]{:S(2)}, u32[]{:S(2)}) collective-permute-start(bf16[32,1,8,512]{3,2,1,0:T(8,128)(2,1)} %convolve.2.refs_0_), channel_id=1, source_target_pairs={{0,4},{1,5},{2,6},{3,7},{4,0},{5,1},{6,2},{7,3},{8,12},{9,13},{10,... | collective-permute-start | bytes 786440 | tf_op jit(solution)/shard_map/ppermute | solution.py:31
  66.3 12.3 %collective-permute-start.20 = (bf16[32,1,8,512]{3,2,1,0:T(8,128)(2,1)}, bf16[32,1,8,512]{3,2,1,0:T(8,128)(2,1)S(1)}, u32[]{:S(2)}, u32[]{:S(2)}) collective-permute-start(bf16[32,1,8,512]{3,2,1,0:T(8,128)(2,1)} %convolve.2.refs_0_), channel_id=1, source_target_pairs={{0,8},{1,9},{2,10},{3,11},{4,12},{5,13},{6,14},{7,15},{8,0},{9,1},... | collective-permute-start | bytes 786440 | tf_op jit(solution)/shard_map/ppermute | solution.py:31
  68.3 10.8 %collective-permute-start.14 = (bf16[32,1,8,512]{3,2,1,0:T(8,128)(2,1)}, bf16[32,1,8,512]{3,2,1,0:T(8,128)(2,1)S(1)}, u32[]{:S(2)}, u32[]{:S(2)}) collective-permute-start(bf16[32,1,8,512]{3,2,1,0:T(8,128)(2,1)} %convolve.2.refs_0_), channel_id=1, source_target_pairs={{0,2},{1,3},{2,0},{3,1},{4,6},{5,7},{6,4},{7,5},{8,10},{9,11},{10,... | collective-permute-start | bytes 786440 | tf_op jit(solution)/shard_map/ppermute | solution.py:31
  76.5 6.6 %collective-permute-start.18 = (bf16[32,1,8,512]{3,2,1,0:T(8,128)(2,1)S(1)}, bf16[32,1,8,512]{3,2,1,0:T(8,128)(2,1)S(1)}, u32[]{:S(2)}, u32[]{:S(2)}) collective-permute-start(bf16[32,1,8,512]{3,2,1,0:T(8,128)(2,1)S(1)} %collective-permute-done.16.refs_4_), channel_id=1, source_target_pairs={{0,2},{1,3},{2,0},{3,1},{4,6},{5,7},{6,4},{7,5},{8,10},{9,11},{10,... | collective-permute-start | bytes 786440 | tf_op jit(solution)/shard_map/ppermute | solution.py:31
  78.6 6.4 %collective-permute-start.24 = (bf16[32,1,8,512]{3,2,1,0:T(8,128)(2,1)S(1)}, bf16[32,1,8,512]{3,2,1,0:T(8,128)(2,1)S(1)}, u32[]{:S(2)}, u32[]{:S(2)}) collective-permute-start(bf16[32,1,8,512]{3,2,1,0:T(8,128)(2,1)S(1)} %collective-permute-done.20.refs_8_), channel_id=1, source_target_pairs={{0,4},{1,5},{2,6},{3,7},{4,0},{5,1},{6,2},{7,3},{8,12},{9,13},{10,... | collective-permute-start | bytes 786440 | tf_op jit(solution)/shard_map/ppermute | solution.py:31
  78.6 8.4 %collective-permute-start.13 = (bf16[32,1,8,512]{3,2,1,0:T(8,128)(2,1)}, bf16[32,1,8,512]{3,2,1,0:T(8,128)(2,1)S(1)}, u32[]{:S(2)}, u32[]{:S(2)}) collective-permute-start(bf16[32,1,8,512]{3,2,1,0:T(8,128)(2,1)} %convolve.2.refs_0_), channel_id=1, source_target_pairs={{0,1},{1,0},{2,3},{3,2},{4,5},{5,4},{6,7},{7,6},{8,9},{9,8},{10,11... | collective-permute-start | bytes 786440 | tf_op jit(solution)/shard_map/ppermute | solution.py:31
  78.6 8.4 %collective-permute-start.17 = (bf16[32,1,8,512]{3,2,1,0:T(8,128)(2,1)S(1)}, bf16[32,1,8,512]{3,2,1,0:T(8,128)(2,1)S(1)}, u32[]{:S(2)}, u32[]{:S(2)}) collective-permute-start(bf16[32,1,8,512]{3,2,1,0:T(8,128)(2,1)S(1)} %collective-permute-done.16.refs_4_), channel_id=1, source_target_pairs={{0,1},{1,0},{2,3},{3,2},{4,5},{5,4},{6,7},{7,6},{8,9},{9,8},{10,11... | collective-permute-start | bytes 786440 | tf_op jit(solution)/shard_map/ppermute | solution.py:31
  79.1 10.0 %collective-permute-start.15 = (bf16[32,1,8,512]{3,2,1,0:T(8,128)(2,1)S(1)}, bf16[32,1,8,512]{3,2,1,0:T(8,128)(2,1)S(1)}, u32[]{:S(2)}, u32[]{:S(2)}) collective-permute-start(bf16[32,1,8,512]{3,2,1,0:T(8,128)(2,1)S(1)} %collective-permute-done.14.refs_2_), channel_id=1, source_target_pairs={{0,1},{1,0},{2,3},{3,2},{4,5},{5,4},{6,7},{7,6},{8,9},{9,8},{10,11... | collective-permute-start | bytes 786440 | tf_op jit(solution)/shard_map/ppermute | solution.py:31
  85.0 11.2 %collective-permute-start.26 = (bf16[32,1,8,512]{3,2,1,0:T(8,128)(2,1)S(1)}, bf16[32,1,8,512]{3,2,1,0:T(8,128)(2,1)S(1)}, u32[]{:S(2)}, u32[]{:S(2)}) collective-permute-start(bf16[32,1,8,512]{3,2,1,0:T(8,128)(2,1)S(1)} %collective-permute-done.24.refs_12_), channel_id=1, source_target_pairs={{0,2},{1,3},{2,0},{3,1},{4,6},{5,7},{6,4},{7,5},{8,10},{9,11},{10,... | collective-permute-start | bytes 786440 | tf_op jit(solution)/shard_map/ppermute | solution.py:31
  85.0 11.7 %collective-permute-start.22 = (bf16[32,1,8,512]{3,2,1,0:T(8,128)(2,1)S(1)}, bf16[32,1,8,512]{3,2,1,0:T(8,128)(2,1)S(1)}, u32[]{:S(2)}, u32[]{:S(2)}) collective-permute-start(bf16[32,1,8,512]{3,2,1,0:T(8,128)(2,1)S(1)} %collective-permute-done.20.refs_8_), channel_id=1, source_target_pairs={{0,2},{1,3},{2,0},{3,1},{4,6},{5,7},{6,4},{7,5},{8,10},{9,11},{10,... | collective-permute-start | bytes 786440 | tf_op jit(solution)/shard_map/ppermute | solution.py:31
  87.0 9.7 %collective-permute-start.25 = (bf16[32,1,8,512]{3,2,1,0:T(8,128)(2,1)S(1)}, bf16[32,1,8,512]{3,2,1,0:T(8,128)(2,1)S(1)}, u32[]{:S(2)}, u32[]{:S(2)}) collective-permute-start(bf16[32,1,8,512]{3,2,1,0:T(8,128)(2,1)S(1)} %collective-permute-done.24.refs_12_), channel_id=1, source_target_pairs={{0,1},{1,0},{2,3},{3,2},{4,5},{5,4},{6,7},{7,6},{8,9},{9,8},{10,11... | collective-permute-start | bytes 786440 | tf_op jit(solution)/shard_map/ppermute | solution.py:31
  87.1 5.5 %collective-permute-start.30 = (s32[8,128]{1,0:T(8,128)S(1)}, s32[8,128]{1,0:T(8,128)S(1)}, u32[]{:S(2)}, u32[]{:S(2)}) collective-permute-start(s32[8,128]{1,0:T(8,128)S(1)} %bitcast.46), channel_id=1, source_target_pairs={{0,12},{1,13},{2,14},{3,15},{4,8},{5,9},{6,10},{7,11},{8,4},{9,5},... | collective-permute-start | bytes 12296 | tf_op jit(solution)/shard_map/ppermute | solution.py:31
  89.2 4.5 %collective-permute-start.29 = (s32[8,128]{1,0:T(8,128)S(1)}, s32[8,128]{1,0:T(8,128)S(1)}, u32[]{:S(2)}, u32[]{:S(2)}) collective-permute-start(s32[8,128]{1,0:T(8,128)S(1)} %bitcast.47), channel_id=1, source_target_pairs={{0,8},{1,9},{2,10},{3,11},{4,12},{5,13},{6,14},{7,15},{8,0},{9,1},... | collective-permute-start | bytes 12296 | tf_op jit(solution)/shard_map/ppermute | solution.py:31
  92.5 3.6 %collective-permute-start.28 = (s32[8,128]{1,0:T(8,128)S(1)}, s32[8,128]{1,0:T(8,128)S(1)}, u32[]{:S(2)}, u32[]{:S(2)}) collective-permute-start(s32[8,128]{1,0:T(8,128)S(1)} %bitcast.48), channel_id=1, source_target_pairs={{0,4},{1,5},{2,6},{3,7},{4,0},{5,1},{6,2},{7,3},{8,12},{9,13},{10,... | collective-permute-start | bytes 12296 | tf_op jit(solution)/shard_map/ppermute | solution.py:31
  93.7 3.2 %collective-permute-start.21 = (bf16[32,1,8,512]{3,2,1,0:T(8,128)(2,1)S(1)}, bf16[32,1,8,512]{3,2,1,0:T(8,128)(2,1)S(1)}, u32[]{:S(2)}, u32[]{:S(2)}) collective-permute-start(bf16[32,1,8,512]{3,2,1,0:T(8,128)(2,1)S(1)} %collective-permute-done.20.refs_8_), channel_id=1, source_target_pairs={{0,1},{1,0},{2,3},{3,2},{4,5},{5,4},{6,7},{7,6},{8,9},{9,8},{10,11... | collective-permute-start | bytes 786440 | tf_op jit(solution)/shard_map/ppermute | solution.py:31
  96.1 1.5 collective-permute-start.19
  96.1 1.9 %collective-permute-start.27 = (bf16[32,1,8,512]{3,2,1,0:T(8,128)(2,1)S(1)}, bf16[32,1,8,512]{3,2,1,0:T(8,128)(2,1)S(1)}, u32[]{:S(2)}, u32[]{:S(2)}) collective-permute-start(bf16[32,1,8,512]{3,2,1,0:T(8,128)(2,1)S(1)} %collective-permute-done.26.refs_14_), channel_id=1, source_target_pairs={{0,1},{1,0},{2,3},{3,2},{4,5},{5,4},{6,7},{7,6},{8,9},{9,8},{10,11... | collective-permute-start | bytes 786440 | tf_op jit(solution)/shard_map/ppermute | solution.py:31
  96.7 1.8 %collective-permute-start.23 = (bf16[32,1,8,512]{3,2,1,0:T(8,128)(2,1)S(1)}, bf16[32,1,8,512]{3,2,1,0:T(8,128)(2,1)S(1)}, u32[]{:S(2)}, u32[]{:S(2)}) collective-permute-start(bf16[32,1,8,512]{3,2,1,0:T(8,128)(2,1)S(1)} %collective-permute-done.22.refs_10_), channel_id=1, source_target_pairs={{0,1},{1,0},{2,3},{3,2},{4,5},{5,4},{6,7},{7,6},{8,9},{9,8},{10,11... | collective-permute-start | bytes 786440 | tf_op jit(solution)/shard_map/ppermute | solution.py:31
  96.8 10.0 %collective-permute-start.31 = (s32[4,8,128]{2,1,0:T(8,128)S(1)}, s32[4,8,128]{2,1,0:T(8,128)S(1)}, u32[]{:S(2)}, u32[]{:S(2)}) collective-permute-start(s32[4,8,128]{2,1,0:T(8,128)S(1)} %get-tuple-element.49), channel_id=1, source_target_pairs={{0,2},{1,3},{2,0},{3,1},{4,6},{5,7},{6,4},{7,5},{8,10},{9,11},{10,... | collective-permute-start | bytes 49160 | tf_op jit(solution)/shard_map/ppermute | solution.py:31
  103.0 13.6 %all-to-all-start = ((bf16[16,2,8,512]{3,2,1,0:T(8,128)(2,1)}), bf16[16,2,8,512]{3,2,1,0:T(8,128)(2,1)S(1)}, u32[]{:S(2)}, u32[]{:S(2)}) async-start(bf16[16,2,8,512]{3,2,1,0:T(8,128)(2,1)} %window_columns.1), calls=%async_computation | async-start | bytes 524288 | tf_op jit(solution)/shard_map/all_to_all | solution.py:414
  106.7 1.3 collective-permute-start.32
  121.3 12.2 %collective-permute-start.36 = (bf16[32,1,8,512]{3,2,1,0:T(8,128)(2,1)}, bf16[32,1,8,512]{3,2,1,0:T(8,128)(2,1)S(1)}, u32[]{:S(2)}, u32[]{:S(2)}) collective-permute-start(bf16[32,1,8,512]{3,2,1,0:T(8,128)(2,1)} %convolve.3.refs_0_), channel_id=1, source_target_pairs={{0,4},{1,5},{2,6},{3,7},{4,0},{5,1},{6,2},{7,3},{8,12},{9,13},{10,... | collective-permute-start | bytes 786440 | tf_op jit(solution)/shard_map/ppermute | solution.py:31
  121.3 12.2 %collective-permute-start.34 = (bf16[32,1,8,512]{3,2,1,0:T(8,128)(2,1)}, bf16[32,1,8,512]{3,2,1,0:T(8,128)(2,1)S(1)}, u32[]{:S(2)}, u32[]{:S(2)}) collective-permute-start(bf16[32,1,8,512]{3,2,1,0:T(8,128)(2,1)} %convolve.3.refs_0_), channel_id=1, source_target_pairs={{0,2},{1,3},{2,0},{3,1},{4,6},{5,7},{6,4},{7,5},{8,10},{9,11},{10,... | collective-permute-start | bytes 786440 | tf_op jit(solution)/shard_map/ppermute | solution.py:31
  122.4 14.7 %collective-permute-start.40 = (bf16[32,1,8,512]{3,2,1,0:T(8,128)(2,1)}, bf16[32,1,8,512]{3,2,1,0:T(8,128)(2,1)S(1)}, u32[]{:S(2)}, u32[]{:S(2)}) collective-permute-start(bf16[32,1,8,512]{3,2,1,0:T(8,128)(2,1)} %convolve.3.refs_0_), channel_id=1, source_target_pairs={{0,8},{1,9},{2,10},{3,11},{4,12},{5,13},{6,14},{7,15},{8,0},{9,1},... | collective-permute-start | bytes 786440 | tf_op jit(solution)/shard_map/ppermute | solution.py:31
  133.5 7.3 %collective-permute-start.38 = (bf16[32,1,8,512]{3,2,1,0:T(8,128)(2,1)S(1)}, bf16[32,1,8,512]{3,2,1,0:T(8,128)(2,1)S(1)}, u32[]{:S(2)}, u32[]{:S(2)}) collective-permute-start(bf16[32,1,8,512]{3,2,1,0:T(8,128)(2,1)S(1)} %collective-permute-done.36.refs_4_), channel_id=1, source_target_pairs={{0,2},{1,3},{2,0},{3,1},{4,6},{5,7},{6,4},{7,5},{8,10},{9,11},{10,... | collective-permute-start | bytes 786440 | tf_op jit(solution)/shard_map/ppermute | solution.py:31
  137.2 7.1 %collective-permute-start.44 = (bf16[32,1,8,512]{3,2,1,0:T(8,128)(2,1)S(1)}, bf16[32,1,8,512]{3,2,1,0:T(8,128)(2,1)S(1)}, u32[]{:S(2)}, u32[]{:S(2)}) collective-permute-start(bf16[32,1,8,512]{3,2,1,0:T(8,128)(2,1)S(1)} %collective-permute-done.40.refs_8_), channel_id=1, source_target_pairs={{0,4},{1,5},{2,6},{3,7},{4,0},{5,1},{6,2},{7,3},{8,12},{9,13},{10,... | collective-permute-start | bytes 786440 | tf_op jit(solution)/shard_map/ppermute | solution.py:31
  140.8 7.3 %collective-permute-start.42 = (bf16[32,1,8,512]{3,2,1,0:T(8,128)(2,1)S(1)}, bf16[32,1,8,512]{3,2,1,0:T(8,128)(2,1)S(1)}, u32[]{:S(2)}, u32[]{:S(2)}) collective-permute-start(bf16[32,1,8,512]{3,2,1,0:T(8,128)(2,1)S(1)} %collective-permute-done.40.refs_8_), channel_id=1, source_target_pairs={{0,2},{1,3},{2,0},{3,1},{4,6},{5,7},{6,4},{7,5},{8,10},{9,11},{10,... | collective-permute-start | bytes 786440 | tf_op jit(solution)/shard_map/ppermute | solution.py:31
  142.2 7.7 %collective-permute-start.33 = (bf16[32,1,8,512]{3,2,1,0:T(8,128)(2,1)}, bf16[32,1,8,512]{3,2,1,0:T(8,128)(2,1)S(1)}, u32[]{:S(2)}, u32[]{:S(2)}) collective-permute-start(bf16[32,1,8,512]{3,2,1,0:T(8,128)(2,1)} %convolve.3.refs_0_), channel_id=1, source_target_pairs={{0,1},{1,0},{2,3},{3,2},{4,5},{5,4},{6,7},{7,6},{8,9},{9,8},{10,11... | collective-permute-start | bytes 786440 | tf_op jit(solution)/shard_map/ppermute | solution.py:31
  142.2 8.2 %collective-permute-start.37 = (bf16[32,1,8,512]{3,2,1,0:T(8,128)(2,1)S(1)}, bf16[32,1,8,512]{3,2,1,0:T(8,128)(2,1)S(1)}, u32[]{:S(2)}, u32[]{:S(2)}) collective-permute-start(bf16[32,1,8,512]{3,2,1,0:T(8,128)(2,1)S(1)} %collective-permute-done.36.refs_4_), channel_id=1, source_target_pairs={{0,1},{1,0},{2,3},{3,2},{4,5},{5,4},{6,7},{7,6},{8,9},{9,8},{10,11... | collective-permute-start | bytes 786440 | tf_op jit(solution)/shard_map/ppermute | solution.py:31
  142.7 7.8 %collective-permute-start.35 = (bf16[32,1,8,512]{3,2,1,0:T(8,128)(2,1)S(1)}, bf16[32,1,8,512]{3,2,1,0:T(8,128)(2,1)S(1)}, u32[]{:S(2)}, u32[]{:S(2)}) collective-permute-start(bf16[32,1,8,512]{3,2,1,0:T(8,128)(2,1)S(1)} %collective-permute-done.34.refs_2_), channel_id=1, source_target_pairs={{0,1},{1,0},{2,3},{3,2},{4,5},{5,4},{6,7},{7,6},{8,9},{9,8},{10,11... | collective-permute-start | bytes 786440 | tf_op jit(solution)/shard_map/ppermute | solution.py:31
  148.1 6.7 %collective-permute-start.46 = (bf16[32,1,8,512]{3,2,1,0:T(8,128)(2,1)S(1)}, bf16[32,1,8,512]{3,2,1,0:T(8,128)(2,1)S(1)}, u32[]{:S(2)}, u32[]{:S(2)}) collective-permute-start(bf16[32,1,8,512]{3,2,1,0:T(8,128)(2,1)S(1)} %collective-permute-done.44.refs_12_), channel_id=1, source_target_pairs={{0,2},{1,3},{2,0},{3,1},{4,6},{5,7},{6,4},{7,5},{8,10},{9,11},{10,... | collective-permute-start | bytes 786440 | tf_op jit(solution)/shard_map/ppermute | solution.py:31
  149.8 5.0 %collective-permute-start.41 = (bf16[32,1,8,512]{3,2,1,0:T(8,128)(2,1)S(1)}, bf16[32,1,8,512]{3,2,1,0:T(8,128)(2,1)S(1)}, u32[]{:S(2)}, u32[]{:S(2)}) collective-permute-start(bf16[32,1,8,512]{3,2,1,0:T(8,128)(2,1)S(1)} %collective-permute-done.40.refs_8_), channel_id=1, source_target_pairs={{0,1},{1,0},{2,3},{3,2},{4,5},{5,4},{6,7},{7,6},{8,9},{9,8},{10,11... | collective-permute-start | bytes 786440 | tf_op jit(solution)/shard_map/ppermute | solution.py:31
  149.8 5.0 %collective-permute-start.45 = (bf16[32,1,8,512]{3,2,1,0:T(8,128)(2,1)S(1)}, bf16[32,1,8,512]{3,2,1,0:T(8,128)(2,1)S(1)}, u32[]{:S(2)}, u32[]{:S(2)}) collective-permute-start(bf16[32,1,8,512]{3,2,1,0:T(8,128)(2,1)S(1)} %collective-permute-done.44.refs_12_), channel_id=1, source_target_pairs={{0,1},{1,0},{2,3},{3,2},{4,5},{5,4},{6,7},{7,6},{8,9},{9,8},{10,11... | collective-permute-start | bytes 786440 | tf_op jit(solution)/shard_map/ppermute | solution.py:31
  150.3 4.5 %collective-permute-start.39 = (bf16[32,1,8,512]{3,2,1,0:T(8,128)(2,1)S(1)}, bf16[32,1,8,512]{3,2,1,0:T(8,128)(2,1)S(1)}, u32[]{:S(2)}, u32[]{:S(2)}) collective-permute-start(bf16[32,1,8,512]{3,2,1,0:T(8,128)(2,1)S(1)} %collective-permute-done.38.refs_6_), channel_id=1, source_target_pairs={{0,1},{1,0},{2,3},{3,2},{4,5},{5,4},{6,7},{7,6},{8,9},{9,8},{10,11... | collective-permute-start | bytes 786440 | tf_op jit(solution)/shard_map/ppermute | solution.py:31
  150.4 4.4 %collective-permute-start.43 = (bf16[32,1,8,512]{3,2,1,0:T(8,128)(2,1)S(1)}, bf16[32,1,8,512]{3,2,1,0:T(8,128)(2,1)S(1)}, u32[]{:S(2)}, u32[]{:S(2)}) collective-permute-start(bf16[32,1,8,512]{3,2,1,0:T(8,128)(2,1)S(1)} %collective-permute-done.42.refs_10_), channel_id=1, source_target_pairs={{0,1},{1,0},{2,3},{3,2},{4,5},{5,4},{6,7},{7,6},{8,9},{9,8},{10,11... | collective-permute-start | bytes 786440 | tf_op jit(solution)/shard_map/ppermute | solution.py:31
  154.8 1.5 collective-permute-start.47
  (37 other events, 323.7 us)

commit v5 on v4

--- a/solution.py
+++ b/solution.py
@@ -53,7 +53,7 @@
         in_specs=[pl.BlockSpec((t, v, sb), lambda i: (0, 0, i))],
         out_specs=pl.BlockSpec((v, t, sb), lambda i: (0, 0, i)),
         out_shape=jax.ShapeDtypeStruct((v, t, s), x.dtype),
-        scratch_shapes=[pltpu.VMEM((t * pitch(v), sb), jnp.float32)],
+        scratch_shapes=[pltpu.VMEM(((t + 1) * pitch(v), sb), jnp.float32)],
         compiler_params=params(),
         name="points_major",
     )(x)
@@ -155,8 +155,8 @@
         out_specs=whole,
         out_shape=jax.ShapeDtypeStruct((v, nq, rb, c), jnp.bfloat16),
         scratch_shapes=[
-            pltpu.VMEM((s // 128, rb * pitch(v), 128), jnp.float32),
-            pltpu.VMEM((r // 128, rb * pitch(v), 128), jnp.float32),
+            pltpu.VMEM((s // 128, (rb + 1) * pitch(v), 128), jnp.float32),
+            pltpu.VMEM((r // 128, (rb + 1) * pitch(v), 128), jnp.float32),
         ],
         compiler_params=params(),
         name="convolve",
@@ -287,7 +287,7 @@
         in_specs=specs,
         out_specs=field_spec,
         out_shape=jax.ShapeDtypeStruct((t, onset.shape[0], s), dtype),
-        scratch_shapes=[pltpu.VMEM((sb // 128, t * pitch(v), 128), jnp.float32)],
+        scratch_shapes=[pltpu.VMEM((sb // 128, (t + 1) * pitch(v), 128), jnp.float32)],
         input_output_aliases=aliases,
         compiler_params=params(),
         name="time_block",

time: 165 us -> 165 us (level)
  transfers between devices with their start and end apart: 49 -> 49, of which waited for: 24 -> 24; matrix products, arithmetic and copies ran while one was open for 5% -> 5% of each run, Pallas kernels for 9% -> 8%
where the time goes in v5:
time: 165 us; the launch traced here: 164 us
  waiting for transfers between devices  71.5 us (43%)
  Pallas kernels  39.7 us (24%)
  starting transfers between devices  39.4 us (24%)
  other arithmetic  7.62 us (5%)
  local copies, waits for them, and re-layouts  4.99 us (3%)
    ppermute x48, waiting for transfers between devices, swap(): return lax.ppermute(x, 'freq', [(i, i ^ stride) for i in range(n)])  68.8 us
    ppermute x48, starting transfers between devices, swap(): return lax.ppermute(x, 'freq', [(i, i ^ stride) for i in range(n)])  35.6 us
    pallas_call x2, Pallas kernels, time_block(): pl.pallas_call(kernel, grid=(s // sb,), in_specs=specs, out_specs=field_s...  12.1 us
    pallas_call x2, Pallas kernels, points_major(): pl.pallas_call(kernel, grid=(s // sb,), in_specs=[pl.BlockSpec((t, v, sb)...  10.2 us
    pallas_call x2, Pallas kernels, convolve(): pl.pallas_call(kernel, grid=(nf // fb,), in_specs=specs, out_specs=whole,...  8.18 us
    pallas_call x1, Pallas kernels, partial_spectra(): pl.pallas_call(kernel, grid=(steps,), in_specs=[pl.BlockSpec((rows, 2 * t...  5.35 us
    pallas_call x1, Pallas kernels, window_columns(): pl.pallas_call(kernel, grid_spec=pltpu.PrefetchScalarGridSpec(num_scalar_...  3.87 us
    all_to_all x1, starting transfers between devices, local(): x2 = lax.all_to_all(x2, 'freq', split_axis=0, concat_axis=0, tiled=True)  3.73 us
  transfers between devices with their start and end apart: 49, of which 24 were waited for; matrix products, arithmetic and copies ran while one was open for 5% of the time, Pallas kernels for 8%

profile of v5, /device:TPU:0, one launch (start us, length us, event | category | flops | bytes accessed | tf_op | source)
XLA Modules:
  0.0 164.4 jit_solution(1121211850629220529)
XLA Ops:
  1.1 2.7 %collective-permute-start = (s32[4]{0:T(128)}, s32[4]{0:T(128)S(1)}, u32[]{:S(2)}, u32[]{:S(2)}) collective-permute-start(s32[4]{0:T(128)} %param.7), channel_id=1, source_target_pairs={{0,4},{1,5},{2,6},{3,7},{4,0},{5,1},{6,2},{7,3},{8,12},{9,13},{10,... | collective-permute-start | bytes 56 | tf_op jit(solution)/shard_map/ppermute | solution.py:31
  3.8 2.5 %collective-permute-start.2 = (s32[4]{0:T(128)}, s32[4]{0:T(128)S(1)}, u32[]{:S(2)}, u32[]{:S(2)}) collective-permute-start(s32[4]{0:T(128)} %param.7), channel_id=1, source_target_pairs={{0,12},{1,13},{2,14},{3,15},{4,8},{5,9},{6,10},{7,11},{8,4},{9,5},... | collective-permute-start | bytes 56 | tf_op jit(solution)/shard_map/ppermute | solution.py:31
  6.4 5.1 %points_major.2.own_ref = bf16[32,128,512]{2,1,0:T(8,128)(2,1)} custom-call(bf16[128,32,512]{2,1,0:T(8,128)(2,1)} %refs_19_.1), custom_call_target="tpu_custom_call" | custom-call | tf_op jit(solution)/shard_map/points_major/pallas_call | solution.py:50
  11.6 5.1 %points_major.3.other_ref = bf16[32,128,512]{2,1,0:T(8,128)(2,1)} custom-call(bf16[128,32,512]{2,1,0:T(8,128)(2,1)} %collective-permute-done.3.x_ref), custom_call_target="tpu_custom_call" | custom-call | tf_op jit(solution)/shard_map/points_major/pallas_call | solution.py:50
  16.6 1.5 collective-permute-start.4
  18.2 2.0 %collective-permute-done.4 = s32[4,4]{1,0:T(4,128)S(1)} collective-permute-done((s32[4,4]{1,0:T(4,128)S(1)}, s32[4,4]{1,0:T(4,128)S(1)}, u32[]{:S(2)}, u32[]{:S(2)}) %collective-permute-start.4) | collective-permute-done | bytes 96 | tf_op jit(solution)/shard_map/ppermute | solution.py:31
  21.5 5.4 %partial_spectra.1 = (bf16[32,1,8,512]{3,2,1,0:T(8,128)(2,1)}, bf16[32,1,8,512]{3,2,1,0:T(8,128)(2,1)}, bf16[32,1,8,512]{3,2,1,0:T(8,128)(2,1)}, bf16[32,1,8,512...) custom-call(bf16[64,256]{1,0:T(8,128)(2,1)} %fusion.9.tab_ref, ...), custom_call_target="tpu_custom_call" | custom-call | tf_op jit(solution)/shard_map/partial_spectra/pallas_call | solution.py:81
  26.8 1.5 collective-permute-start.6
  28.9 7.4 %collective-permute-done.6 = bf16[32,1,8,512]{3,2,1,0:T(8,128)(2,1)S(1)} collective-permute-done((bf16[32,1,8,512]{3,2,1,0:T(8,128)(2,1)}, bf16[32,1,8,512]{3,2,1,0:T(8,128)(2,1)S(1)}, u32[]{:S(2)}, u32[]{:S(2)}) %collective-permute-start.6) | collective-permute-done | bytes 262176 | tf_op jit(solution)/shard_map/ppermute | solution.py:31
  36.3 1.5 collective-permute-start.7
  37.8 1.0 add_convert_fusion.1
  38.8 1.9 %collective-permute-start.10 = (bf16[32,1,8,512]{3,2,1,0:T(8,128)(2,1)S(1)}, bf16[32,1,8,512]{3,2,1,0:T(8,128)(2,1)S(1)}, u32[]{:S(2)}, u32[]{:S(2)}) collective-permute-start(bf16[32,1,8,512]{3,2,1,0:T(8,128)(2,1)S(1)} %add_convert_fusion.1), channel_id=1, source_target_pairs={{0,4},{1,5},{2,6},{3,7},{4,0},{5,1},{6,2},{7,3},{8,12},{9,13},{10,... | collective-permute-start | bytes 786440 | tf_op jit(solution)/shard_map/ppermute | solution.py:31
  41.9 1.5 collective-permute-start.9
  43.4 2.1 %collective-permute-done.7 = bf16[32,1,8,512]{3,2,1,0:T(8,128)(2,1)S(1)} collective-permute-done((bf16[32,1,8,512]{3,2,1,0:T(8,128)(2,1)}, bf16[32,1,8,512]{3,2,1,0:T(8,128)(2,1)S(1)}, u32[]{:S(2)}, u32[]{:S(2)}) %collective-permute-start.7) | collective-permute-done | bytes 262176 | tf_op jit(solution)/shard_map/ppermute | solution.py:31
  45.9 1.1 add_convert_fusion
  46.9 3.4 %collective-permute-start.12 = (bf16[32,1,8,512]{3,2,1,0:T(8,128)(2,1)S(1)}, bf16[32,1,8,512]{3,2,1,0:T(8,128)(2,1)S(1)}, u32[]{:S(2)}, u32[]{:S(2)}) collective-permute-start(bf16[32,1,8,512]{3,2,1,0:T(8,128)(2,1)S(1)} %add_convert_fusion), channel_id=1, source_target_pairs={{0,8},{1,9},{2,10},{3,11},{4,12},{5,13},{6,14},{7,15},{8,0},{9,1},... | collective-permute-start | bytes 786440 | tf_op jit(solution)/shard_map/ppermute | solution.py:31
  50.4 1.0 add_convert_fusion.2
  52.4 2.2 %fusion.4.refs_16_ = bf16[128,768]{1,0:T(8,128)(2,1)} fusion(s32[128]{0:T(128)S(1)} %add.84, s32[128]{0:T(128)S(1)} %mul.94), kind=kLoop, calls=%fused_computation.11 | loop fusion | flops 1572864 | bytes 197632 | tf_op jit(solution)/shard_map/convert_element_type | solution.py:407
  54.7 5.9 %collective-permute-done.11.refs_2_ = bf16[32,1,8,512]{3,2,1,0:T(8,128)(2,1)S(1)} collective-permute-done((bf16[32,1,8,512]{3,2,1,0:T(8,128)(2,1)S(1)}, bf16[32,1,8,512]{3,2,1,0:T(8,128)(2,1)S(1)}, u32[]{:S(2)}, u32[]{:S(2)}) %collective-permute-start.11) | collective-permute-done | bytes 262176 | tf_op jit(solution)/shard_map/ppermute | solution.py:31
  62.0 4.2 %convolve.2.refs_0_ = bf16[32,1,8,512]{3,2,1,0:T(8,128)(2,1)} custom-call(bf16[32,1,8,512]{3,2,1,0:T(8,128)(2,1)} %get-tuple-element.31.refs_0_, bf16[32,1,8,512]{3,2,1,0:T(8,128)(2,1)} %copy-done.31, bf16[32,1,8,512]{3,2,1,0:T(8,128)(2,1)} %copy-done.33, bf16[32,1,8,512]{3,2,1,0:T(8,128)(2,1)} %copy-done.32, f32[4,4]{1,0:T(4,128)} %refs_1_.1, ...), custom_call_target="tpu_custom_call" | custom-call | tf_op jit(solution)/shard_map/convolve/pallas_call | solution.py:151
  66.3 2.0 %collective-permute-start.20 = (bf16[32,1,8,512]{3,2,1,0:T(8,128)(2,1)}, bf16[32,1,8,512]{3,2,1,0:T(8,128)(2,1)S(1)}, u32[]{:S(2)}, u32[]{:S(2)}) collective-permute-start(bf16[32,1,8,512]{3,2,1,0:T(8,128)(2,1)} %convolve.2.refs_0_), channel_id=1, source_target_pairs={{0,8},{1,9},{2,10},{3,11},{4,12},{5,13},{6,14},{7,15},{8,0},{9,1},... | collective-permute-start | bytes 786440 | tf_op jit(solution)/shard_map/ppermute | solution.py:31
  68.3 1.8 %collective-permute-start.14 = (bf16[32,1,8,512]{3,2,1,0:T(8,128)(2,1)}, bf16[32,1,8,512]{3,2,1,0:T(8,128)(2,1)S(1)}, u32[]{:S(2)}, u32[]{:S(2)}) collective-permute-start(bf16[32,1,8,512]{3,2,1,0:T(8,128)(2,1)} %convolve.2.refs_0_), channel_id=1, source_target_pairs={{0,2},{1,3},{2,0},{3,1},{4,6},{5,7},{6,4},{7,5},{8,10},{9,11},{10,... | collective-permute-start | bytes 786440 | tf_op jit(solution)/shard_map/ppermute | solution.py:31
  70.1 6.4 %collective-permute-done.16.refs_4_ = bf16[32,1,8,512]{3,2,1,0:T(8,128)(2,1)S(1)} collective-permute-done((bf16[32,1,8,512]{3,2,1,0:T(8,128)(2,1)}, bf16[32,1,8,512]{3,2,1,0:T(8,128)(2,1)S(1)}, u32[]{:S(2)}, u32[]{:S(2)}) %collective-permute-start.16) | collective-permute-done | bytes 262176 | tf_op jit(solution)/shard_map/ppermute | solution.py:31
  77.0 1.6 collective-permute-done.20.refs_8_
  79.2 4.0 %collective-permute-done.18.refs_6_ = bf16[32,1,8,512]{3,2,1,0:T(8,128)(2,1)S(1)} collective-permute-done((bf16[32,1,8,512]{3,2,1,0:T(8,128)(2,1)S(1)}, bf16[32,1,8,512]{3,2,1,0:T(8,128)(2,1)S(1)}, u32[]{:S(2)}, u32[]{:S(2)}) %collective-permute-start.18) | collective-permute-done | bytes 262176 | tf_op jit(solution)/shard_map/ppermute | solution.py:31
  83.2 1.8 %collective-permute-done.24.refs_12_ = bf16[32,1,8,512]{3,2,1,0:T(8,128)(2,1)S(1)} collective-permute-done((bf16[32,1,8,512]{3,2,1,0:T(8,128)(2,1)S(1)}, bf16[32,1,8,512]{3,2,1,0:T(8,128)(2,1)S(1)}, u32[]{:S(2)}, u32[]{:S(2)}) %collective-permute-start.24) | collective-permute-done | bytes 262176 | tf_op jit(solution)/shard_map/ppermute | solution.py:31
  85.0 2.0 %collective-permute-start.22 = (bf16[32,1,8,512]{3,2,1,0:T(8,128)(2,1)S(1)}, bf16[32,1,8,512]{3,2,1,0:T(8,128)(2,1)S(1)}, u32[]{:S(2)}, u32[]{:S(2)}) collective-permute-start(bf16[32,1,8,512]{3,2,1,0:T(8,128)(2,1)S(1)} %collective-permute-done.20.refs_8_), channel_id=1, source_target_pairs={{0,2},{1,3},{2,0},{3,1},{4,6},{5,7},{6,4},{7,5},{8,10},{9,11},{10,... | collective-permute-start | bytes 786440 | tf_op jit(solution)/shard_map/ppermute | solution.py:31
  87.1 2.1 %collective-permute-start.30 = (s32[8,128]{1,0:T(8,128)S(1)}, s32[8,128]{1,0:T(8,128)S(1)}, u32[]{:S(2)}, u32[]{:S(2)}) collective-permute-start(s32[8,128]{1,0:T(8,128)S(1)} %bitcast.46), channel_id=1, source_target_pairs={{0,12},{1,13},{2,14},{3,15},{4,8},{5,9},{6,10},{7,11},{8,4},{9,5},... | collective-permute-start | bytes 12296 | tf_op jit(solution)/shard_map/ppermute | solution.py:31
  89.2 3.4 %collective-permute-done.30 = s32[8,128]{1,0:T(8,128)S(1)} collective-permute-done((s32[8,128]{1,0:T(8,128)S(1)}, s32[8,128]{1,0:T(8,128)S(1)}, u32[]{:S(2)}, u32[]{:S(2)}) %collective-permute-start.30) | collective-permute-done | bytes 4128 | tf_op jit(solution)/shard_map/ppermute | solution.py:31
  92.5 1.1 collective-permute-done.29
  93.7 2.5 %collective-permute-done.28 = s32[8,128]{1,0:T(8,128)S(1)} collective-permute-done((s32[8,128]{1,0:T(8,128)S(1)}, s32[8,128]{1,0:T(8,128)S(1)}, u32[]{:S(2)}, u32[]{:S(2)}) %collective-permute-start.28) | collective-permute-done | bytes 4128 | tf_op jit(solution)/shard_map/ppermute | solution.py:31
  99.1 3.9 %window_columns.1 = bf16[16,2,8,512]{3,2,1,0:T(8,128)(2,1)} custom-call(s32[1]{0:T(128)} %bitcast.21.me_ref, bf16[32,1,8,512]{3,2,1,0:T(8,128)(2,1)} %convolve.2.refs_0_, bf16[32,1,8,512]{3,2,1,0:T(8,128)(2,1)} %copy-done.5, bf16[32,1,8,512]{3,2,1,0:T(8,128)(2,1)} %copy-done.2, bf16[32,1,8,512]{3,2,1,0:T(8,128)(2,1)} %copy-done.7, ...), custom_call_target="tpu_custom_call" | custom-call | tf_op jit(solution)/shard_map/window_columns/pallas_call | solution.py:208
  103.0 3.7 %all-to-all-start = ((bf16[16,2,8,512]{3,2,1,0:T(8,128)(2,1)}), bf16[16,2,8,512]{3,2,1,0:T(8,128)(2,1)S(1)}, u32[]{:S(2)}, u32[]{:S(2)}) async-start(bf16[16,2,8,512]{3,2,1,0:T(8,128)(2,1)} %window_columns.1), calls=%async_computation | async-start | bytes 524288 | tf_op jit(solution)/shard_map/all_to_all | solution.py:414
  108.9 5.0 %time_block.2 = bf16[128,32,512]{2,1,0:T(8,128)(2,1)} custom-call(bf16[32,1,8,512]{3,2,1,0:T(8,128)(2,1)} %convolve.2.refs_0_, bf16[32,1,8,512]{3,2,1,0:T(8,128)(2,1)} %copy-done.5, bf16[32,1,8,512]{3,2,1,0:T(8,128)(2,1)} %copy-done.2, bf16[32,1,8,512]{3,2,1,0:T(8,128)(2,1)} %copy-done.7, bf16[32,1,8,512]{3,2,1,0:T(8,128)(2,1)} %copy-done, ...), custom_call_target="tpu_custom_call" | custom-call | tf_op jit(solution)/shard_map/time_block/pallas_call | solution.py:284
  114.0 2.7 %all-to-all-done = bf16[16,2,8,512]{3,2,1,0:T(8,128)(2,1)S(1)} async-done(((bf16[16,2,8,512]{3,2,1,0:T(8,128)(2,1)}), bf16[16,2,8,512]{3,2,1,0:T(8,128)(2,1)S(1)}, u32[]{:S(2)}, u32[]{:S(2)}) %all-to-all-start) | async-done | bytes 262176 | tf_op jit(solution)/shard_map/all_to_all | solution.py:414
  117.3 4.0 %convolve.3.refs_0_ = bf16[32,1,8,512]{3,2,1,0:T(8,128)(2,1)} custom-call(bf16[32,1,8,512]{3,2,1,0:T(8,128)(2,1)} %bitcast.37, f32[4,4]{1,0:T(4,128)} %refs_1_.1, bf16[4,2,512,512]{3,2,1,0:T(8,128)(2,1)} %refs_2_.1), custom_call_target="tpu_custom_call" | custom-call | tf_op jit(solution)/shard_map/convolve/pallas_call | solution.py:151
  121.3 1.1 collective-permute-start.34
  122.4 1.8 %collective-permute-start.40 = (bf16[32,1,8,512]{3,2,1,0:T(8,128)(2,1)}, bf16[32,1,8,512]{3,2,1,0:T(8,128)(2,1)S(1)}, u32[]{:S(2)}, u32[]{:S(2)}) collective-permute-start(bf16[32,1,8,512]{3,2,1,0:T(8,128)(2,1)} %convolve.3.refs_0_), channel_id=1, source_target_pairs={{0,8},{1,9},{2,10},{3,11},{4,12},{5,13},{6,14},{7,15},{8,0},{9,1},... | collective-permute-start | bytes 786440 | tf_op jit(solution)/shard_map/ppermute | solution.py:31
  124.2 9.3 %collective-permute-done.36.refs_4_ = bf16[32,1,8,512]{3,2,1,0:T(8,128)(2,1)S(1)} collective-permute-done((bf16[32,1,8,512]{3,2,1,0:T(8,128)(2,1)}, bf16[32,1,8,512]{3,2,1,0:T(8,128)(2,1)S(1)}, u32[]{:S(2)}, u32[]{:S(2)}) %collective-permute-start.36) | collective-permute-done | bytes 262176 | tf_op jit(solution)/shard_map/ppermute | solution.py:31
  133.7 3.5 %collective-permute-done.40.refs_8_ = bf16[32,1,8,512]{3,2,1,0:T(8,128)(2,1)S(1)} collective-permute-done((bf16[32,1,8,512]{3,2,1,0:T(8,128)(2,1)}, bf16[32,1,8,512]{3,2,1,0:T(8,128)(2,1)S(1)}, u32[]{:S(2)}, u32[]{:S(2)}) %collective-permute-start.40) | collective-permute-done | bytes 262176 | tf_op jit(solution)/shard_map/ppermute | solution.py:31
  137.2 3.6 %collective-permute-done.38.refs_6_ = bf16[32,1,8,512]{3,2,1,0:T(8,128)(2,1)S(1)} collective-permute-done((bf16[32,1,8,512]{3,2,1,0:T(8,128)(2,1)S(1)}, bf16[32,1,8,512]{3,2,1,0:T(8,128)(2,1)S(1)}, u32[]{:S(2)}, u32[]{:S(2)}) %collective-permute-start.38) | collective-permute-done | bytes 262176 | tf_op jit(solution)/shard_map/ppermute | solution.py:31
  140.8 1.4 collective-permute-start.42
  142.7 1.6 collective-permute-done.44.refs_12_
  144.3 3.8 %collective-permute-done.42.refs_10_ = bf16[32,1,8,512]{3,2,1,0:T(8,128)(2,1)S(1)} collective-permute-done((bf16[32,1,8,512]{3,2,1,0:T(8,128)(2,1)S(1)}, bf16[32,1,8,512]{3,2,1,0:T(8,128)(2,1)S(1)}, u32[]{:S(2)}, u32[]{:S(2)}) %collective-permute-start.42) | collective-permute-done | bytes 262176 | tf_op jit(solution)/shard_map/ppermute | solution.py:31
  148.1 1.7 %collective-permute-start.46 = (bf16[32,1,8,512]{3,2,1,0:T(8,128)(2,1)S(1)}, bf16[32,1,8,512]{3,2,1,0:T(8,128)(2,1)S(1)}, u32[]{:S(2)}, u32[]{:S(2)}) collective-permute-start(bf16[32,1,8,512]{3,2,1,0:T(8,128)(2,1)S(1)} %collective-permute-done.44.refs_12_), channel_id=1, source_target_pairs={{0,2},{1,3},{2,0},{3,1},{4,6},{5,7},{6,4},{7,5},{8,10},{9,11},{10,... | collective-permute-start | bytes 786440 | tf_op jit(solution)/shard_map/ppermute | solution.py:31
  150.9 4.0 %collective-permute-done.46.refs_14_ = bf16[32,1,8,512]{3,2,1,0:T(8,128)(2,1)S(1)} collective-permute-done((bf16[32,1,8,512]{3,2,1,0:T(8,128)(2,1)S(1)}, bf16[32,1,8,512]{3,2,1,0:T(8,128)(2,1)S(1)}, u32[]{:S(2)}, u32[]{:S(2)}) %collective-permute-start.46) | collective-permute-done | bytes 262176 | tf_op jit(solution)/shard_map/ppermute | solution.py:31
  154.9 1.5 collective-permute-done.47.refs_15_
  157.2 7.1 %time_block.3 = f32[128,32,512]{2,1,0:T(8,128)} custom-call(bf16[32,1,8,512]{3,2,1,0:T(8,128)(2,1)} %convolve.3.refs_0_, bf16[32,1,8,512]{3,2,1,0:T(8,128)(2,1)} %copy-done.22, bf16[32,1,8,512]{3,2,1,0:T(8,128)(2,1)} %copy-done.17, bf16[32,1,8,512]{3,2,1,0:T(8,128)(2,1)} %copy-done.24, bf16[32,1,8,512]{3,2,1,0:T(8,128)(2,1)} %copy-done.16, ...), custom_call_target="tpu_custom_call" | custom-call | tf_op jit(solution)/shard_map/time_block/pallas_call | solution.py:284
  (165 shorter events, 16.0 us)
Async XLA Ops:
  0.6 10.9 %collective-permute-start.3 = (bf16[128,32,512]{2,1,0:T(8,128)(2,1)}, bf16[128,32,512]{2,1,0:T(8,128)(2,1)}, u32[]{:S(2)}, u32[]{:S(2)}) collective-permute-start(bf16[128,32,512]{2,1,0:T(8,128)(2,1)} %refs_19_.1), channel_id=1, source_target_pairs={{0,1},{1,0},{2,3},{3,2},{4,5},{5,4},{6,7},{7,6},{8,9},{9,8},{10,11... | collective-permute-start | bytes 12582920 | tf_op jit(solution)/shard_map/ppermute | solution.py:31
  1.1 10.4 %collective-permute-start = (s32[4]{0:T(128)}, s32[4]{0:T(128)S(1)}, u32[]{:S(2)}, u32[]{:S(2)}) collective-permute-start(s32[4]{0:T(128)} %param.7), channel_id=1, source_target_pairs={{0,4},{1,5},{2,6},{3,7},{4,0},{5,1},{6,2},{7,3},{8,12},{9,13},{10,... | collective-permute-start | bytes 56 | tf_op jit(solution)/shard_map/ppermute | solution.py:31
  3.8 7.7 %collective-permute-start.2 = (s32[4]{0:T(128)}, s32[4]{0:T(128)S(1)}, u32[]{:S(2)}, u32[]{:S(2)}) collective-permute-start(s32[4]{0:T(128)} %param.7), channel_id=1, source_target_pairs={{0,12},{1,13},{2,14},{3,15},{4,8},{5,9},{6,10},{7,11},{8,4},{9,5},... | collective-permute-start | bytes 56 | tf_op jit(solution)/shard_map/ppermute | solution.py:31
  6.3 5.2 %collective-permute-start.1 = (s32[4]{0:T(128)}, s32[4]{0:T(128)S(1)}, u32[]{:S(2)}, u32[]{:S(2)}) collective-permute-start(s32[4]{0:T(128)} %param.7), channel_id=1, source_target_pairs={{0,8},{1,9},{2,10},{3,11},{4,12},{5,13},{6,14},{7,15},{8,0},{9,1},... | collective-permute-start | bytes 56 | tf_op jit(solution)/shard_map/ppermute | solution.py:31
  16.6 3.6 %collective-permute-start.4 = (s32[4,4]{1,0:T(4,128)S(1)}, s32[4,4]{1,0:T(4,128)S(1)}, u32[]{:S(2)}, u32[]{:S(2)}) collective-permute-start(s32[4,4]{1,0:T(4,128)S(1)} %pad_add_fusion.5), channel_id=1, source_target_pairs={{0,2},{1,3},{2,0},{3,1},{4,6},{5,7},{6,4},{7,5},{8,10},{9,11},{10,... | collective-permute-start | bytes 200 | tf_op jit(solution)/shard_map/ppermute | solution.py:31
  26.8 9.5 %collective-permute-start.6 = (bf16[32,1,8,512]{3,2,1,0:T(8,128)(2,1)}, bf16[32,1,8,512]{3,2,1,0:T(8,128)(2,1)S(1)}, u32[]{:S(2)}, u32[]{:S(2)}) collective-permute-start(bf16[32,1,8,512]{3,2,1,0:T(8,128)(2,1)} %get-tuple-element.28), channel_id=1, source_target_pairs={{0,2},{1,3},{2,0},{3,1},{4,6},{5,7},{6,4},{7,5},{8,10},{9,11},{10,... | collective-permute-start | bytes 786440 | tf_op jit(solution)/shard_map/ppermute | solution.py:31
  28.4 13.6 %collective-permute-start.8 = (bf16[32,1,8,512]{3,2,1,0:T(8,128)(2,1)}, bf16[32,1,8,512]{3,2,1,0:T(8,128)(2,1)S(1)}, u32[]{:S(2)}, u32[]{:S(2)}) collective-permute-start(bf16[32,1,8,512]{3,2,1,0:T(8,128)(2,1)} %get-tuple-element.33), channel_id=1, source_target_pairs={{0,2},{1,3},{2,0},{3,1},{4,6},{5,7},{6,4},{7,5},{8,10},{9,11},{10,... | collective-permute-start | bytes 786440 | tf_op jit(solution)/shard_map/ppermute | solution.py:31
  36.3 9.2 %collective-permute-start.7 = (bf16[32,1,8,512]{3,2,1,0:T(8,128)(2,1)}, bf16[32,1,8,512]{3,2,1,0:T(8,128)(2,1)S(1)}, u32[]{:S(2)}, u32[]{:S(2)}) collective-permute-start(bf16[32,1,8,512]{3,2,1,0:T(8,128)(2,1)} %get-tuple-element.29), channel_id=1, source_target_pairs={{0,2},{1,3},{2,0},{3,1},{4,6},{5,7},{6,4},{7,5},{8,10},{9,11},{10,... | collective-permute-start | bytes 786440 | tf_op jit(solution)/shard_map/ppermute | solution.py:31
  38.8 7.0 %collective-permute-start.10 = (bf16[32,1,8,512]{3,2,1,0:T(8,128)(2,1)S(1)}, bf16[32,1,8,512]{3,2,1,0:T(8,128)(2,1)S(1)}, u32[]{:S(2)}, u32[]{:S(2)}) collective-permute-start(bf16[32,1,8,512]{3,2,1,0:T(8,128)(2,1)S(1)} %add_convert_fusion.1), channel_id=1, source_target_pairs={{0,4},{1,5},{2,6},{3,7},{4,0},{5,1},{6,2},{7,3},{8,12},{9,13},{10,... | collective-permute-start | bytes 786440 | tf_op jit(solution)/shard_map/ppermute | solution.py:31
  41.9 12.7 %collective-permute-start.9 = (bf16[32,1,8,512]{3,2,1,0:T(8,128)(2,1)}, bf16[32,1,8,512]{3,2,1,0:T(8,128)(2,1)S(1)}, u32[]{:S(2)}, u32[]{:S(2)}) collective-permute-start(bf16[32,1,8,512]{3,2,1,0:T(8,128)(2,1)} %get-tuple-element.34), channel_id=1, source_target_pairs={{0,2},{1,3},{2,0},{3,1},{4,6},{5,7},{6,4},{7,5},{8,10},{9,11},{10,... | collective-permute-start | bytes 786440 | tf_op jit(solution)/shard_map/ppermute | solution.py:31
  46.9 13.7 %collective-permute-start.12 = (bf16[32,1,8,512]{3,2,1,0:T(8,128)(2,1)S(1)}, bf16[32,1,8,512]{3,2,1,0:T(8,128)(2,1)S(1)}, u32[]{:S(2)}, u32[]{:S(2)}) collective-permute-start(bf16[32,1,8,512]{3,2,1,0:T(8,128)(2,1)S(1)} %add_convert_fusion), channel_id=1, source_target_pairs={{0,8},{1,9},{2,10},{3,11},{4,12},{5,13},{6,14},{7,15},{8,0},{9,1},... | collective-permute-start | bytes 786440 | tf_op jit(solution)/shard_map/ppermute | solution.py:31
  51.4 9.2 %collective-permute-start.11 = (bf16[32,1,8,512]{3,2,1,0:T(8,128)(2,1)S(1)}, bf16[32,1,8,512]{3,2,1,0:T(8,128)(2,1)S(1)}, u32[]{:S(2)}, u32[]{:S(2)}) collective-permute-start(bf16[32,1,8,512]{3,2,1,0:T(8,128)(2,1)S(1)} %add_convert_fusion.2), channel_id=1, source_target_pairs={{0,4},{1,5},{2,6},{3,7},{4,0},{5,1},{6,2},{7,3},{8,12},{9,13},{10,... | collective-permute-start | bytes 786440 | tf_op jit(solution)/shard_map/ppermute | solution.py:31
  66.2 10.3 %collective-permute-start.16 = (bf16[32,1,8,512]{3,2,1,0:T(8,128)(2,1)}, bf16[32,1,8,512]{3,2,1,0:T(8,128)(2,1)S(1)}, u32[]{:S(2)}, u32[]{:S(2)}) collective-permute-start(bf16[32,1,8,512]{3,2,1,0:T(8,128)(2,1)} %convolve.2.refs_0_), channel_id=1, source_target_pairs={{0,4},{1,5},{2,6},{3,7},{4,0},{5,1},{6,2},{7,3},{8,12},{9,13},{10,... | collective-permute-start | bytes 786440 | tf_op jit(solution)/shard_map/ppermute | solution.py:31
  66.3 12.3 %collective-permute-start.20 = (bf16[32,1,8,512]{3,2,1,0:T(8,128)(2,1)}, bf16[32,1,8,512]{3,2,1,0:T(8,128)(2,1)S(1)}, u32[]{:S(2)}, u32[]{:S(2)}) collective-permute-start(bf16[32,1,8,512]{3,2,1,0:T(8,128)(2,1)} %convolve.2.refs_0_), channel_id=1, source_target_pairs={{0,8},{1,9},{2,10},{3,11},{4,12},{5,13},{6,14},{7,15},{8,0},{9,1},... | collective-permute-start | bytes 786440 | tf_op jit(solution)/shard_map/ppermute | solution.py:31
  68.3 10.8 %collective-permute-start.14 = (bf16[32,1,8,512]{3,2,1,0:T(8,128)(2,1)}, bf16[32,1,8,512]{3,2,1,0:T(8,128)(2,1)S(1)}, u32[]{:S(2)}, u32[]{:S(2)}) collective-permute-start(bf16[32,1,8,512]{3,2,1,0:T(8,128)(2,1)} %convolve.2.refs_0_), channel_id=1, source_target_pairs={{0,2},{1,3},{2,0},{3,1},{4,6},{5,7},{6,4},{7,5},{8,10},{9,11},{10,... | collective-permute-start | bytes 786440 | tf_op jit(solution)/shard_map/ppermute | solution.py:31
  76.5 6.6 %collective-permute-start.18 = (bf16[32,1,8,512]{3,2,1,0:T(8,128)(2,1)S(1)}, bf16[32,1,8,512]{3,2,1,0:T(8,128)(2,1)S(1)}, u32[]{:S(2)}, u32[]{:S(2)}) collective-permute-start(bf16[32,1,8,512]{3,2,1,0:T(8,128)(2,1)S(1)} %collective-permute-done.16.refs_4_), channel_id=1, source_target_pairs={{0,2},{1,3},{2,0},{3,1},{4,6},{5,7},{6,4},{7,5},{8,10},{9,11},{10,... | collective-permute-start | bytes 786440 | tf_op jit(solution)/shard_map/ppermute | solution.py:31
  78.6 6.4 %collective-permute-start.24 = (bf16[32,1,8,512]{3,2,1,0:T(8,128)(2,1)S(1)}, bf16[32,1,8,512]{3,2,1,0:T(8,128)(2,1)S(1)}, u32[]{:S(2)}, u32[]{:S(2)}) collective-permute-start(bf16[32,1,8,512]{3,2,1,0:T(8,128)(2,1)S(1)} %collective-permute-done.20.refs_8_), channel_id=1, source_target_pairs={{0,4},{1,5},{2,6},{3,7},{4,0},{5,1},{6,2},{7,3},{8,12},{9,13},{10,... | collective-permute-start | bytes 786440 | tf_op jit(solution)/shard_map/ppermute | solution.py:31
  78.6 8.4 %collective-permute-start.13 = (bf16[32,1,8,512]{3,2,1,0:T(8,128)(2,1)}, bf16[32,1,8,512]{3,2,1,0:T(8,128)(2,1)S(1)}, u32[]{:S(2)}, u32[]{:S(2)}) collective-permute-start(bf16[32,1,8,512]{3,2,1,0:T(8,128)(2,1)} %convolve.2.refs_0_), channel_id=1, source_target_pairs={{0,1},{1,0},{2,3},{3,2},{4,5},{5,4},{6,7},{7,6},{8,9},{9,8},{10,11... | collective-permute-start | bytes 786440 | tf_op jit(solution)/shard_map/ppermute | solution.py:31
  78.6 8.4 %collective-permute-start.17 = (bf16[32,1,8,512]{3,2,1,0:T(8,128)(2,1)S(1)}, bf16[32,1,8,512]{3,2,1,0:T(8,128)(2,1)S(1)}, u32[]{:S(2)}, u32[]{:S(2)}) collective-permute-start(bf16[32,1,8,512]{3,2,1,0:T(8,128)(2,1)S(1)} %collective-permute-done.16.refs_4_), channel_id=1, source_target_pairs={{0,1},{1,0},{2,3},{3,2},{4,5},{5,4},{6,7},{7,6},{8,9},{9,8},{10,11... | collective-permute-start | bytes 786440 | tf_op jit(solution)/shard_map/ppermute | solution.py:31
  79.1 10.0 %collective-permute-start.15 = (bf16[32,1,8,512]{3,2,1,0:T(8,128)(2,1)S(1)}, bf16[32,1,8,512]{3,2,1,0:T(8,128)(2,1)S(1)}, u32[]{:S(2)}, u32[]{:S(2)}) collective-permute-start(bf16[32,1,8,512]{3,2,1,0:T(8,128)(2,1)S(1)} %collective-permute-done.14.refs_2_), channel_id=1, source_target_pairs={{0,1},{1,0},{2,3},{3,2},{4,5},{5,4},{6,7},{7,6},{8,9},{9,8},{10,11... | collective-permute-start | bytes 786440 | tf_op jit(solution)/shard_map/ppermute | solution.py:31
  85.0 11.2 %collective-permute-start.26 = (bf16[32,1,8,512]{3,2,1,0:T(8,128)(2,1)S(1)}, bf16[32,1,8,512]{3,2,1,0:T(8,128)(2,1)S(1)}, u32[]{:S(2)}, u32[]{:S(2)}) collective-permute-start(bf16[32,1,8,512]{3,2,1,0:T(8,128)(2,1)S(1)} %collective-permute-done.24.refs_12_), channel_id=1, source_target_pairs={{0,2},{1,3},{2,0},{3,1},{4,6},{5,7},{6,4},{7,5},{8,10},{9,11},{10,... | collective-permute-start | bytes 786440 | tf_op jit(solution)/shard_map/ppermute | solution.py:31
  85.0 11.7 %collective-permute-start.22 = (bf16[32,1,8,512]{3,2,1,0:T(8,128)(2,1)S(1)}, bf16[32,1,8,512]{3,2,1,0:T(8,128)(2,1)S(1)}, u32[]{:S(2)}, u32[]{:S(2)}) collective-permute-start(bf16[32,1,8,512]{3,2,1,0:T(8,128)(2,1)S(1)} %collective-permute-done.20.refs_8_), channel_id=1, source_target_pairs={{0,2},{1,3},{2,0},{3,1},{4,6},{5,7},{6,4},{7,5},{8,10},{9,11},{10,... | collective-permute-start | bytes 786440 | tf_op jit(solution)/shard_map/ppermute | solution.py:31
  87.0 9.7 %collective-permute-start.25 = (bf16[32,1,8,512]{3,2,1,0:T(8,128)(2,1)S(1)}, bf16[32,1,8,512]{3,2,1,0:T(8,128)(2,1)S(1)}, u32[]{:S(2)}, u32[]{:S(2)}) collective-permute-start(bf16[32,1,8,512]{3,2,1,0:T(8,128)(2,1)S(1)} %collective-permute-done.24.refs_12_), channel_id=1, source_target_pairs={{0,1},{1,0},{2,3},{3,2},{4,5},{5,4},{6,7},{7,6},{8,9},{9,8},{10,11... | collective-permute-start | bytes 786440 | tf_op jit(solution)/shard_map/ppermute | solution.py:31
  87.1 5.5 %collective-permute-start.30 = (s32[8,128]{1,0:T(8,128)S(1)}, s32[8,128]{1,0:T(8,128)S(1)}, u32[]{:S(2)}, u32[]{:S(2)}) collective-permute-start(s32[8,128]{1,0:T(8,128)S(1)} %bitcast.46), channel_id=1, source_target_pairs={{0,12},{1,13},{2,14},{3,15},{4,8},{5,9},{6,10},{7,11},{8,4},{9,5},... | collective-permute-start | bytes 12296 | tf_op jit(solution)/shard_map/ppermute | solution.py:31
  89.2 4.5 %collective-permute-start.29 = (s32[8,128]{1,0:T(8,128)S(1)}, s32[8,128]{1,0:T(8,128)S(1)}, u32[]{:S(2)}, u32[]{:S(2)}) collective-permute-start(s32[8,128]{1,0:T(8,128)S(1)} %bitcast.47), channel_id=1, source_target_pairs={{0,8},{1,9},{2,10},{3,11},{4,12},{5,13},{6,14},{7,15},{8,0},{9,1},... | collective-permute-start | bytes 12296 | tf_op jit(solution)/shard_map/ppermute | solution.py:31
  92.5 3.6 %collective-permute-start.28 = (s32[8,128]{1,0:T(8,128)S(1)}, s32[8,128]{1,0:T(8,128)S(1)}, u32[]{:S(2)}, u32[]{:S(2)}) collective-permute-start(s32[8,128]{1,0:T(8,128)S(1)} %bitcast.48), channel_id=1, source_target_pairs={{0,4},{1,5},{2,6},{3,7},{4,0},{5,1},{6,2},{7,3},{8,12},{9,13},{10,... | collective-permute-start | bytes 12296 | tf_op jit(solution)/shard_map/ppermute | solution.py:31
  93.7 3.2 %collective-permute-start.21 = (bf16[32,1,8,512]{3,2,1,0:T(8,128)(2,1)S(1)}, bf16[32,1,8,512]{3,2,1,0:T(8,128)(2,1)S(1)}, u32[]{:S(2)}, u32[]{:S(2)}) collective-permute-start(bf16[32,1,8,512]{3,2,1,0:T(8,128)(2,1)S(1)} %collective-permute-done.20.refs_8_), channel_id=1, source_target_pairs={{0,1},{1,0},{2,3},{3,2},{4,5},{5,4},{6,7},{7,6},{8,9},{9,8},{10,11... | collective-permute-start | bytes 786440 | tf_op jit(solution)/shard_map/ppermute | solution.py:31
  96.1 1.5 collective-permute-start.19
  96.1 1.9 %collective-permute-start.27 = (bf16[32,1,8,512]{3,2,1,0:T(8,128)(2,1)S(1)}, bf16[32,1,8,512]{3,2,1,0:T(8,128)(2,1)S(1)}, u32[]{:S(2)}, u32[]{:S(2)}) collective-permute-start(bf16[32,1,8,512]{3,2,1,0:T(8,128)(2,1)S(1)} %collective-permute-done.26.refs_14_), channel_id=1, source_target_pairs={{0,1},{1,0},{2,3},{3,2},{4,5},{5,4},{6,7},{7,6},{8,9},{9,8},{10,11... | collective-permute-start | bytes 786440 | tf_op jit(solution)/shard_map/ppermute | solution.py:31
  96.7 1.8 %collective-permute-start.23 = (bf16[32,1,8,512]{3,2,1,0:T(8,128)(2,1)S(1)}, bf16[32,1,8,512]{3,2,1,0:T(8,128)(2,1)S(1)}, u32[]{:S(2)}, u32[]{:S(2)}) collective-permute-start(bf16[32,1,8,512]{3,2,1,0:T(8,128)(2,1)S(1)} %collective-permute-done.22.refs_10_), channel_id=1, source_target_pairs={{0,1},{1,0},{2,3},{3,2},{4,5},{5,4},{6,7},{7,6},{8,9},{9,8},{10,11... | collective-permute-start | bytes 786440 | tf_op jit(solution)/shard_map/ppermute | solution.py:31
  96.8 10.0 %collective-permute-start.31 = (s32[4,8,128]{2,1,0:T(8,128)S(1)}, s32[4,8,128]{2,1,0:T(8,128)S(1)}, u32[]{:S(2)}, u32[]{:S(2)}) collective-permute-start(s32[4,8,128]{2,1,0:T(8,128)S(1)} %get-tuple-element.49), channel_id=1, source_target_pairs={{0,2},{1,3},{2,0},{3,1},{4,6},{5,7},{6,4},{7,5},{8,10},{9,11},{10,... | collective-permute-start | bytes 49160 | tf_op jit(solution)/shard_map/ppermute | solution.py:31
  103.0 13.6 %all-to-all-start = ((bf16[16,2,8,512]{3,2,1,0:T(8,128)(2,1)}), bf16[16,2,8,512]{3,2,1,0:T(8,128)(2,1)S(1)}, u32[]{:S(2)}, u32[]{:S(2)}) async-start(bf16[16,2,8,512]{3,2,1,0:T(8,128)(2,1)} %window_columns.1), calls=%async_computation | async-start | bytes 524288 | tf_op jit(solution)/shard_map/all_to_all | solution.py:414
  106.7 1.3 collective-permute-start.32
  121.3 12.2 %collective-permute-start.36 = (bf16[32,1,8,512]{3,2,1,0:T(8,128)(2,1)}, bf16[32,1,8,512]{3,2,1,0:T(8,128)(2,1)S(1)}, u32[]{:S(2)}, u32[]{:S(2)}) collective-permute-start(bf16[32,1,8,512]{3,2,1,0:T(8,128)(2,1)} %convolve.3.refs_0_), channel_id=1, source_target_pairs={{0,4},{1,5},{2,6},{3,7},{4,0},{5,1},{6,2},{7,3},{8,12},{9,13},{10,... | collective-permute-start | bytes 786440 | tf_op jit(solution)/shard_map/ppermute | solution.py:31
  121.3 12.2 %collective-permute-start.34 = (bf16[32,1,8,512]{3,2,1,0:T(8,128)(2,1)}, bf16[32,1,8,512]{3,2,1,0:T(8,128)(2,1)S(1)}, u32[]{:S(2)}, u32[]{:S(2)}) collective-permute-start(bf16[32,1,8,512]{3,2,1,0:T(8,128)(2,1)} %convolve.3.refs_0_), channel_id=1, source_target_pairs={{0,2},{1,3},{2,0},{3,1},{4,6},{5,7},{6,4},{7,5},{8,10},{9,11},{10,... | collective-permute-start | bytes 786440 | tf_op jit(solution)/shard_map/ppermute | solution.py:31
  122.4 14.7 %collective-permute-start.40 = (bf16[32,1,8,512]{3,2,1,0:T(8,128)(2,1)}, bf16[32,1,8,512]{3,2,1,0:T(8,128)(2,1)S(1)}, u32[]{:S(2)}, u32[]{:S(2)}) collective-permute-start(bf16[32,1,8,512]{3,2,1,0:T(8,128)(2,1)} %convolve.3.refs_0_), channel_id=1, source_target_pairs={{0,8},{1,9},{2,10},{3,11},{4,12},{5,13},{6,14},{7,15},{8,0},{9,1},... | collective-permute-start | bytes 786440 | tf_op jit(solution)/shard_map/ppermute | solution.py:31
  133.5 7.3 %collective-permute-start.38 = (bf16[32,1,8,512]{3,2,1,0:T(8,128)(2,1)S(1)}, bf16[32,1,8,512]{3,2,1,0:T(8,128)(2,1)S(1)}, u32[]{:S(2)}, u32[]{:S(2)}) collective-permute-start(bf16[32,1,8,512]{3,2,1,0:T(8,128)(2,1)S(1)} %collective-permute-done.36.refs_4_), channel_id=1, source_target_pairs={{0,2},{1,3},{2,0},{3,1},{4,6},{5,7},{6,4},{7,5},{8,10},{9,11},{10,... | collective-permute-start | bytes 786440 | tf_op jit(solution)/shard_map/ppermute | solution.py:31
  137.2 7.1 %collective-permute-start.44 = (bf16[32,1,8,512]{3,2,1,0:T(8,128)(2,1)S(1)}, bf16[32,1,8,512]{3,2,1,0:T(8,128)(2,1)S(1)}, u32[]{:S(2)}, u32[]{:S(2)}) collective-permute-start(bf16[32,1,8,512]{3,2,1,0:T(8,128)(2,1)S(1)} %collective-permute-done.40.refs_8_), channel_id=1, source_target_pairs={{0,4},{1,5},{2,6},{3,7},{4,0},{5,1},{6,2},{7,3},{8,12},{9,13},{10,... | collective-permute-start | bytes 786440 | tf_op jit(solution)/shard_map/ppermute | solution.py:31
  140.8 7.3 %collective-permute-start.42 = (bf16[32,1,8,512]{3,2,1,0:T(8,128)(2,1)S(1)}, bf16[32,1,8,512]{3,2,1,0:T(8,128)(2,1)S(1)}, u32[]{:S(2)}, u32[]{:S(2)}) collective-permute-start(bf16[32,1,8,512]{3,2,1,0:T(8,128)(2,1)S(1)} %collective-permute-done.40.refs_8_), channel_id=1, source_target_pairs={{0,2},{1,3},{2,0},{3,1},{4,6},{5,7},{6,4},{7,5},{8,10},{9,11},{10,... | collective-permute-start | bytes 786440 | tf_op jit(solution)/shard_map/ppermute | solution.py:31
  142.2 7.7 %collective-permute-start.33 = (bf16[32,1,8,512]{3,2,1,0:T(8,128)(2,1)}, bf16[32,1,8,512]{3,2,1,0:T(8,128)(2,1)S(1)}, u32[]{:S(2)}, u32[]{:S(2)}) collective-permute-start(bf16[32,1,8,512]{3,2,1,0:T(8,128)(2,1)} %convolve.3.refs_0_), channel_id=1, source_target_pairs={{0,1},{1,0},{2,3},{3,2},{4,5},{5,4},{6,7},{7,6},{8,9},{9,8},{10,11... | collective-permute-start | bytes 786440 | tf_op jit(solution)/shard_map/ppermute | solution.py:31
  142.2 8.2 %collective-permute-start.37 = (bf16[32,1,8,512]{3,2,1,0:T(8,128)(2,1)S(1)}, bf16[32,1,8,512]{3,2,1,0:T(8,128)(2,1)S(1)}, u32[]{:S(2)}, u32[]{:S(2)}) collective-permute-start(bf16[32,1,8,512]{3,2,1,0:T(8,128)(2,1)S(1)} %collective-permute-done.36.refs_4_), channel_id=1, source_target_pairs={{0,1},{1,0},{2,3},{3,2},{4,5},{5,4},{6,7},{7,6},{8,9},{9,8},{10,11... | collective-permute-start | bytes 786440 | tf_op jit(solution)/shard_map/ppermute | solution.py:31
  142.7 7.8 %collective-permute-start.35 = (bf16[32,1,8,512]{3,2,1,0:T(8,128)(2,1)S(1)}, bf16[32,1,8,512]{3,2,1,0:T(8,128)(2,1)S(1)}, u32[]{:S(2)}, u32[]{:S(2)}) collective-permute-start(bf16[32,1,8,512]{3,2,1,0:T(8,128)(2,1)S(1)} %collective-permute-done.34.refs_2_), channel_id=1, source_target_pairs={{0,1},{1,0},{2,3},{3,2},{4,5},{5,4},{6,7},{7,6},{8,9},{9,8},{10,11... | collective-permute-start | bytes 786440 | tf_op jit(solution)/shard_map/ppermute | solution.py:31
  148.1 6.7 %collective-permute-start.46 = (bf16[32,1,8,512]{3,2,1,0:T(8,128)(2,1)S(1)}, bf16[32,1,8,512]{3,2,1,0:T(8,128)(2,1)S(1)}, u32[]{:S(2)}, u32[]{:S(2)}) collective-permute-start(bf16[32,1,8,512]{3,2,1,0:T(8,128)(2,1)S(1)} %collective-permute-done.44.refs_12_), channel_id=1, source_target_pairs={{0,2},{1,3},{2,0},{3,1},{4,6},{5,7},{6,4},{7,5},{8,10},{9,11},{10,... | collective-permute-start | bytes 786440 | tf_op jit(solution)/shard_map/ppermute | solution.py:31
  149.8 5.0 %collective-permute-start.41 = (bf16[32,1,8,512]{3,2,1,0:T(8,128)(2,1)S(1)}, bf16[32,1,8,512]{3,2,1,0:T(8,128)(2,1)S(1)}, u32[]{:S(2)}, u32[]{:S(2)}) collective-permute-start(bf16[32,1,8,512]{3,2,1,0:T(8,128)(2,1)S(1)} %collective-permute-done.40.refs_8_), channel_id=1, source_target_pairs={{0,1},{1,0},{2,3},{3,2},{4,5},{5,4},{6,7},{7,6},{8,9},{9,8},{10,11... | collective-permute-start | bytes 786440 | tf_op jit(solution)/shard_map/ppermute | solution.py:31
  149.8 5.0 %collective-permute-start.45 = (bf16[32,1,8,512]{3,2,1,0:T(8,128)(2,1)S(1)}, bf16[32,1,8,512]{3,2,1,0:T(8,128)(2,1)S(1)}, u32[]{:S(2)}, u32[]{:S(2)}) collective-permute-start(bf16[32,1,8,512]{3,2,1,0:T(8,128)(2,1)S(1)} %collective-permute-done.44.refs_12_), channel_id=1, source_target_pairs={{0,1},{1,0},{2,3},{3,2},{4,5},{5,4},{6,7},{7,6},{8,9},{9,8},{10,11... | collective-permute-start | bytes 786440 | tf_op jit(solution)/shard_map/ppermute | solution.py:31
  150.3 4.5 %collective-permute-start.39 = (bf16[32,1,8,512]{3,2,1,0:T(8,128)(2,1)S(1)}, bf16[32,1,8,512]{3,2,1,0:T(8,128)(2,1)S(1)}, u32[]{:S(2)}, u32[]{:S(2)}) collective-permute-start(bf16[32,1,8,512]{3,2,1,0:T(8,128)(2,1)S(1)} %collective-permute-done.38.refs_6_), channel_id=1, source_target_pairs={{0,1},{1,0},{2,3},{3,2},{4,5},{5,4},{6,7},{7,6},{8,9},{9,8},{10,11... | collective-permute-start | bytes 786440 | tf_op jit(solution)/shard_map/ppermute | solution.py:31
  150.4 4.4 %collective-permute-start.43 = (bf16[32,1,8,512]{3,2,1,0:T(8,128)(2,1)S(1)}, bf16[32,1,8,512]{3,2,1,0:T(8,128)(2,1)S(1)}, u32[]{:S(2)}, u32[]{:S(2)}) collective-permute-start(bf16[32,1,8,512]{3,2,1,0:T(8,128)(2,1)S(1)} %collective-permute-done.42.refs_10_), channel_id=1, source_target_pairs={{0,1},{1,0},{2,3},{3,2},{4,5},{5,4},{6,7},{7,6},{8,9},{9,8},{10,11... | collective-permute-start | bytes 786440 | tf_op jit(solution)/shard_map/ppermute | solution.py:31
  154.8 1.5 collective-permute-start.47
  (37 other events, 323.6 us)
